TPU v7x, 128 devices: a whole 4x4x4 slice. The times are simulated.
128 devices in a mesh: rows: 32 (over y, z, core), slab: 4 (over x).
Axes of the slice: x: 4, y: 4, z: 4, core: 2. Of those that a mesh axis runs over, the one named last changes fastest.
Arguments:
- snapshots: bfloat16 [262144, 2048], P(('rows', 'slab')), may hold values from -60 to 60
- start_block: float32 [2048, 64], replicated, may hold values from -6 to 6
- linear_op: float32 [64, 64], replicated, may hold values from -0.75 to 0.75
- quad_op: float32 [4096, 64], replicated, may hold values from -0.009765625 to 0.009765625
- offset: float32 [64], replicated, may hold values from -3 to 3
Outputs:
- projection: bfloat16 [262144, 64], P(('rows', 'slab'))
- reduced: float32 [2048, 64], P(('rows', 'slab'))
- mismatch: float32 [2048, 64], P(('rows', 'slab'))
All inputs are finite; a program needn't handle non-finite values.
Results may differ from a plain program's by a relative error of at most 0.0029.
Values sent between devices are 32-bit elements; how exact they have to be, the bound alone decides.
No kernel may reach another device: no remote copies, remote signals or barrier semaphores. Data moves between devices by JAX's collectives and lax.ppermute only.
A program may use at most 128 MiB of HBM per device.

v0:
```python
import math

import jax
import jax.numpy as jnp
from jax import lax
from jax.sharding import Mesh
from jax.sharding import PartitionSpec as P

ROWS_SLAB = ("rows_0", "rows_1", "rows_2", "slab")


def own_block(parts, axes, turns):
    shape = [lax.axis_size(a) for a in axes]
    parts = parts.reshape(*shape, *parts.shape[1:])
    parts = parts.transpose(*turns, *range(len(axes), parts.ndim))
    parts = parts.reshape(-1, *parts.shape[len(axes) :])
    for k in turns:
        parts = lax.psum_scatter(parts, axes[k], scatter_dimension=0, tiled=True)
    return parts[0]


def split_up(shard, dim, peers):
    shape = shard.shape
    parts = shard.reshape(*shape[:dim], peers, shape[dim] // peers, *shape[dim + 1 :])
    return jnp.moveaxis(parts, dim, 0)


def summed_rows_2(shard, axes, turns, dim):
    peers = lax.axis_size(axes)
    return own_block(split_up(shard, dim, peers), axes, turns)


def joined_along(parts, dim):
    shape = list(parts.shape[1:])
    shape[dim] *= parts.shape[0]
    return jnp.moveaxis(parts, 0, dim).reshape(shape)


def gather_in_order(shard, axes, turns):
    parts = shard
    for k in turns:
        parts = lax.all_gather(parts, axes[k])
    done = turns[::-1]
    back = [done.index(k) for k in range(len(axes))]
    parts = parts.transpose(*back, *range(len(axes), parts.ndim))
    return parts.reshape(-1, *shard.shape)


def whole_of(shard, axes, turns, dim):
    return joined_along(gather_in_order(shard, axes, turns), dim)


def shifted(block, axis, distance):
    devices = range(lax.axis_size(axis))
    route = [(i - distance, i) for i in devices if i - distance in devices]
    return lax.ppermute(block, axis, route)


def advance(state, linear_op, quad_op, offset):
    pairs = (state[:, :, None] * state[:, None, :]).reshape(state.shape[0], -1)
    highest = lax.Precision.HIGHEST
    change = (
        jnp.dot(state, linear_op, precision=highest)
        + jnp.dot(pairs, quad_op, precision=highest)
        + offset[None, :]
    )
    return state + 0.25 * change


def normalize(power):
    highest = lax.Precision.HIGHEST
    factor = jnp.linalg.cholesky(jnp.dot(power.T, power, precision=highest))
    return jax.scipy.linalg.solve_triangular(factor, power.T, lower=True).T


def body(snapshots, start_block, linear_op, quad_op, offset):
    highest = lax.Precision.HIGHEST
    devices = lax.axis_size(ROWS_SLAB)
    width = snapshots.shape[1]
    share = width // devices
    total = snapshots.shape[0] * devices
    factor_scale = math.sqrt(width) / total
    contract = (((0,), (0,)), ((), ()))
    gram_block = summed_rows_2(
        lax.dot_general(snapshots, snapshots, contract, preferred_element_type=jnp.float32),
        ROWS_SLAB,
        (2, 0, 1, 3),
        0,
    )
    power_block = jnp.dot(gram_block, start_block, precision=highest)
    power = whole_of(power_block, ROWS_SLAB, (0, 1, 3, 2), 0)
    basis = normalize(power)
    modes = jnp.dot(snapshots, basis, precision=highest, preferred_element_type=jnp.float32)
    projection = modes.astype(jnp.bfloat16)
    reduced = jnp.dot(gram_block, basis, precision=highest) * factor_scale
    state = advance(advance(reduced, linear_op, quad_op, offset), linear_op, quad_op, offset)
    following = shifted(reduced[:2], ROWS_SLAB, -1)
    target = jnp.concatenate([reduced[2:], following], axis=0)
    position = lax.axis_index(ROWS_SLAB) * share + jnp.arange(share, dtype=jnp.int32)
    mismatch = jnp.where((position < width - 2)[:, None], state - target, jnp.float32(0.0))
    return (projection, reduced, mismatch)


def solution(mesh):
    split = Mesh(
        mesh.devices.reshape(4, 4, 2, mesh.shape["slab"]), ("rows_0", "rows_1", "rows_2", "slab")
    )
    placed = (P(ROWS_SLAB, None), P(), P(), P(), P())
    return jax.shard_map(
        body,
        mesh=split,
        in_specs=placed,
        out_specs=(P(ROWS_SLAB, None), P(ROWS_SLAB, None), P(ROWS_SLAB, None)),
        check_vma=False,
    )
```

profile of v0, /device:TPU:0, one launch (start us, length us, event | category | flops | bytes accessed | tf_op | source)
XLA Modules:
  0.0 291.1 jit_solution(15280385676178518146)
XLA Ops:
  7.2 22.5 %fusion.15 = f32[2048,2048]{1,0:T(8,128)S(1)} fusion(bf16[2048,2048]{1,0:T(8,128)(2,1)} %param.5), kind=kOutput, calls=%fused_computation.30 | convolution fusion | flops 17179869184 | bytes 25165824 | tf_op jit(solution)/shard_map/dot_general | solution.py:85
  29.8 6.0 %copy.12 = f32[4,4,2,4,16,2048]{5,4,3,1,0,2:T(8,128)} copy(f32[4,4,2,4,16,2048]{5,4,3,2,1,0:T(8,128)S(1)} %bitcast.50) | data formatting | bytes 33554432 | tf_op jit(solution)/shard_map/reshape;reshape | solution.py:14
  35.8 0.0 reduce-scatter.7.cloned.1.call-start
  35.9 31.5 %reduce-scatter.5.cloned.1.call-done = f32[64,16,2048]{2,1,0:T(8,128)} async-done(((f32[128,16,2048]{2,1,0:T(8,128)}), f32[64,16,2048]{2,1,0:T(8,128)}) %reduce-scatter.5.cloned.1.call-update) | async-done | bytes 8388624 | tf_op jit(solution)/shard_map/reduce_scatter | solution.py:18
  67.5 84.5 %reduce-scatter.7.cloned.1.call-done = f32[16,16,2048]{2,1,0:T(8,128)} async-done(((f32[64,16,2048]{2,1,0:T(8,128)}), f32[16,16,2048]{2,1,0:T(8,128)}) %reduce-scatter.7.cloned.1.call-update) | async-done | bytes 2097168 | tf_op jit(solution)/shard_map/reduce_scatter | solution.py:18
  152.0 32.1 %reduce-scatter.9.cloned.1.call-done = f32[4,16,2048]{2,1,0:T(8,128)} async-done(((f32[16,16,2048]{2,1,0:T(8,128)}), f32[4,16,2048]{2,1,0:T(8,128)}) %reduce-scatter.9.cloned.1.call-update) | async-done | bytes 524304 | tf_op jit(solution)/shard_map/reduce_scatter | solution.py:18
  184.2 23.2 %reduce-scatter.11.cloned.1.call-done = f32[1,16,2048]{2,1,0:T(8,128)} async-done(((f32[4,16,2048]{2,1,0:T(8,128)}), f32[1,16,2048]{2,1,0:T(8,128)}) %reduce-scatter.11.cloned.1.call-update) | async-done | bytes 131088 | tf_op jit(solution)/shard_map/reduce_scatter | solution.py:18
  207.4 1.5 fusion.8
  208.9 12.2 %all-gather = f32[64,64]{1,0:T(8,128)S(1)} all-gather(f32[16,64]{1,0:T(8,128)S(1)} %fusion.8), channel_id=2, replica_groups=mesh['rows_0'=4,'rows_1'=4,'rows_2'=2,'slab'=4] {'rows_0'}, dimensions={0}, use_global_device_ids=true | all-gather | bytes 20480 | tf_op jit(solution)/shard_map/all_gather | solution.py:42
  221.1 12.5 %all-gather.1 = f32[16,16,64]{2,1,0:T(8,128)S(1)} all-gather(f32[4,16,64]{2,1,0:T(8,128)S(1)} %bitcast.55), channel_id=3, replica_groups=mesh['rows_0'=4,'rows_1'=4,'rows_2'=2,'slab'=4] {'rows_1'}, dimensions={0}, use_global_device_ids=true | all-gather | bytes 81920 | tf_op jit(solution)/shard_map/all_gather | solution.py:42
  233.6 12.8 %all-gather.2 = f32[16,4,16,64]{3,2,1,0:T(8,128)S(1)} all-gather(f32[4,4,16,64]{3,2,1,0:T(8,128)S(1)} %bitcast.54), channel_id=4, replica_groups=mesh['rows_0'=4,'rows_1'=4,'rows_2'=2,'slab'=4] {'slab'}, dimensions={0}, use_global_device_ids=true | all-gather | bytes 327680 | tf_op jit(solution)/shard_map/all_gather | solution.py:42
  246.4 2.7 all-gather.3
  249.1 0.1 copy.13
  249.2 1.9 convolution_bitcast_fusion
  251.1 0.1 copy.14
  251.2 5.8 %cholesky.16 = f32[64,64]{1,0:T(8,128)S(1)} custom-call(f32[64,64]{1,0:T(8,128)S(1)} %fusion.13), custom_call_target="Cholesky" | custom-call | tf_op jit(solution)/shard_map/jit(cholesky)/cholesky | solution.py:72
  257.1 0.6 compare_reduce_fusion
  257.7 0.7 fusion.10
  258.4 4.9 %custom-call.7 = f32[1,64,64]{1,2,0:T(8,128)S(1)} custom-call(f32[1,64,64]{2,1,0:T(8,128)S(1)} %fusion.10), custom_call_target="InvertDiagBlocksLowerTriangular" | custom-call | tf_op jit(solution)/shard_map/jit(_solve_triangular)/triangular_solve | solution.py:73
  263.3 1.3 fusion.11
  264.6 0.5 convolution_multiply_fusion
  265.1 0.2 broadcast_multiply_fusion.1
  265.3 10.7 %fusion = bf16[2048,64]{0,1:T(8,128)(2,1)} fusion(f32[64,2048]{1,0:T(8,128)S(1)} %fusion.11, bf16[2048,2048]{1,0:T(8,128)(2,1)} %param.5), kind=kOutput, calls=%fused_computation.1 | convolution fusion | flops 3221356544 | bytes 9175040 | tf_op jit(solution)/shard_map/dot_general | solution.py:93
  276.1 0.2 mul.67
  276.3 0.1 fusion.16
  276.4 0.9 fusion.5
  277.4 0.2 broadcast_multiply_fusion
  277.6 1.3 collective-permute-start
  278.9 0.1 fusion.17
  279.0 0.2 mul.72
  279.2 3.8 %collective-permute-done = f32[2,64]{1,0:T(2,128)S(1)} collective-permute-done((f32[2,64]{1,0:T(2,128)S(1)}, f32[2,64]{1,0:T(2,128)S(1)}, u32[]{:S(2)}, u32[]{:S(2)}) %collective-permute-start) | collective-permute-done | bytes 544 | tf_op jit(solution)/shard_map/ppermute | solution.py:56
  283.0 1.6 fusion.14
  (24 shorter events, 0.3 us)
Async XLA Ops:
  7.2 269.2 %copy-start = (f32[4096,64]{0,1:T(8,128)S(1)}, f32[4096,64]{0,1:T(8,128)}, u32[]{:S(2)}) copy-start(f32[4096,64]{0,1:T(8,128)} %param.8) | copy-start | bytes 3145732
  7.2 60.2 %reduce-scatter.5.cloned.1.call-start = ((), (), s32[]{:S(2)}) async-start(), calls=%async_computation.4 | async-start | bytes 25165824 | tf_op jit(solution)/shard_map/reduce_scatter | solution.py:18
  35.8 171.6 %copy-start.1 = (f32[2048,64]{0,1:T(8,128)S(1)}, f32[2048,64]{0,1:T(8,128)}, u32[]{:S(2)}) copy-start(f32[2048,64]{0,1:T(8,128)} %param.6) | copy-start | bytes 1572868
  35.8 116.1 %reduce-scatter.7.cloned.1.call-start = ((), (), s32[]{:S(2)}) async-start(), calls=%async_computation.5 | async-start | bytes 10485760 | tf_op jit(solution)/shard_map/reduce_scatter | solution.py:18
  67.4 116.7 %reduce-scatter.9.cloned.1.call-start = ((), (), s32[]{:S(2)}) async-start(), calls=%async_computation.6 | async-start | bytes 2621440 | tf_op jit(solution)/shard_map/reduce_scatter | solution.py:18
  152.0 55.4 %reduce-scatter.11.cloned.1.call-start = ((), (), s32[]{:S(2)}) async-start(), calls=%async_computation.7 | async-start | bytes 655360 | tf_op jit(solution)/shard_map/reduce_scatter | solution.py:18
  207.4 57.2 %copy-start.2 = (f32[1,16,2048]{2,1,0:T(8,128)S(1)}, f32[1,16,2048]{2,1,0:T(8,128)}, u32[]{:S(2)}) copy-start(f32[1,16,2048]{2,1,0:T(8,128)} %reduce-scatter.11.cloned.1.call-done) | copy-start | bytes 393220
  249.1 27.2 %copy-start.4 = (f32[64,64]{1,0:T(8,128)S(1)}, f32[64,64]{1,0:T(8,128)}, u32[]{:S(2)}) copy-start(f32[64,64]{1,0:T(8,128)} %param.7) | copy-start | bytes 49156
  249.1 27.3 %copy-start.5 = (f32[64]{0:T(128)S(1)}, f32[64]{0:T(128)}, u32[]{:S(2)}) copy-start(f32[64]{0:T(128)} %param.9) | copy-start | bytes 772
  265.1 19.5 %copy-start.3 = (f32[16,64]{1,0:T(8,128)}, f32[16,64]{1,0:T(8,128)S(1)}, u32[]{:S(2)}) copy-start(f32[16,64]{1,0:T(8,128)S(1)} %convolution_multiply_fusion) | copy-start | bytes 12292
  277.6 5.5 %collective-permute-start = (f32[2,64]{1,0:T(2,128)S(1)}, f32[2,64]{1,0:T(2,128)S(1)}, u32[]{:S(2)}, u32[]{:S(2)}) collective-permute-start(f32[2,64]{1,0:T(2,128)S(1)} %slice.21), channel_id=1, source_target_pairs={{1,0},{2,1},{3,2},{4,3},{5,4},{6,5},{7,6},{8,7},{9,8},{10,9},{11,1... | collective-permute-start | bytes 1544 | tf_op jit(solution)/shard_map/ppermute | solution.py:56
Sparse Core Ops, SparseCore 0:
  35.9 31.4 reduce-scatter.4
  70.0 81.9 reduce-scatter.6
  154.5 29.6 reduce-scatter.8
  186.4 20.9 reduce-scatter.10
where the time goes:
time: 292 us; the launch traced here: 291 us
  waiting for transfers between devices  175 us (60%)
  matrix products  41.2 us (14%)
  blocking collectives  40.2 us (14%)
  between operations  13.9 us (5%)
  other arithmetic  12.5 us (4%)
  local copies, waits for them, and re-layouts  6.61 us (2%)
    reduce_scatter x4, waiting for transfers between devices, own_block(): parts = lax.psum_scatter(parts, axes[k], scatter_dimension=0, tiled=True)  171 us
    all_gather x4, blocking collectives, gather_in_order(): parts = lax.all_gather(parts, axes[k])  40.2 us
    dot_general x1, matrix products, body(): lax.dot_general(snapshots, snapshots, contract, preferred_element_type=jn...  22.5 us
    dot_general x1, matrix products, body(): jnp.dot(snapshots, basis, precision=highest, preferred_element_type=jnp.f...  10.7 us
    another operation x3, other arithmetic, normalize(): factor = jnp.linalg.cholesky(jnp.dot(power.T, power, precision=highest))  6.52 us
    another operation x1, local copies, waits for them, and re-layouts, own_block(): parts = parts.reshape(*shape, *parts.shape[1:])  6.02 us
  transfers between devices with their start and end apart: 5, of which 5 were waited for; matrix products, arithmetic and copies ran while one was open for 0% of the time, Pallas kernels for 0%

commit v1 on v0

v1 whole, which is shorter than its diff:
```python
import math

import jax
import jax.numpy as jnp
from jax import lax
from jax.experimental import pallas as pl
from jax.experimental.pallas import tpu as pltpu
from jax.sharding import PartitionSpec as P

EVERY = ("rows", "slab")
RANK = 64
CHUNKS = 4
NT = (((1,), (1,)), ((), ()))
LIMIT = pltpu.CompilerParams(vmem_limit_bytes=48 * 1024 * 1024)
VMEM = pl.BlockSpec(memory_space=pltpu.VMEM)
ANY = pl.BlockSpec(memory_space=pl.ANY)


def three(value, axis):
    high = value.astype(jnp.bfloat16)
    rest = value - high.astype(jnp.float32)
    middle = rest.astype(jnp.bfloat16)
    low = (rest - middle.astype(jnp.float32)).astype(jnp.bfloat16)
    return jnp.concatenate([high, middle, low], axis=axis)


def fold(value, axis):
    if axis == 0:
        return value[:RANK] + value[RANK : 2 * RANK] + value[2 * RANK :]
    return value[:, :RANK] + value[:, RANK : 2 * RANK] + value[:, 2 * RANK :]


def fetches(source, buffer, sems):
    rows = source.shape[0] // CHUNKS
    return [
        pltpu.make_async_copy(
            source.at[pl.ds(i * rows, rows)], buffer.at[pl.ds(i * rows, rows)], sems.at[i]
        )
        for i in range(CHUNKS)
    ]


def power_kernel(x_hbm, start_ref, out_ref, x_ref, acc_ref, sems):
    copies = fetches(x_hbm, x_ref, sems)
    for copy in copies:
        copy.start()
    weights = three(start_ref[...], 0)
    rows = x_ref.shape[0] // CHUNKS
    for i, copy in enumerate(copies):
        copy.wait()
        x = x_ref[pl.ds(i * rows, rows), :]
        inner = fold(lax.dot_general(x, weights, NT, preferred_element_type=jnp.float32), 1)
        part = jnp.dot(three(inner.T, 0), x, preferred_element_type=jnp.float32)
        acc_ref[...] = part if i == 0 else acc_ref[...] + part
    power = fold(acc_ref[...], 0)
    wide = power.shape[1] // 128
    for i in range(out_ref.shape[0]):
        a, b = divmod(i, wide)
        out_ref[i] = power[8 * a : 8 * a + 8, 128 * b : 128 * b + 128]


def coords_kernel(x_hbm, power_ref, out_ref, modes_ref, corr_ref, x_ref, acc_ref, sems):
    copies = fetches(x_hbm, x_ref, sems)
    for copy in copies:
        copy.start()
    tall = RANK // 8
    wide = power_ref.shape[0] // tall
    power = jnp.concatenate(
        [
            jnp.concatenate([power_ref[a * wide + b] for b in range(wide)], axis=1)
            for a in range(tall)
        ],
        axis=0,
    )
    weights = three(power, 0)
    gram = lax.dot_general(weights, weights, NT, preferred_element_type=jnp.float32)
    corr_ref[...] = fold(fold(gram, 1), 0)
    rows = x_ref.shape[0] // CHUNKS
    for i, copy in enumerate(copies):
        copy.wait()
        x = x_ref[pl.ds(i * rows, rows), :]
        modes = fold(lax.dot_general(x, weights, NT, preferred_element_type=jnp.float32), 1)
        modes = modes.T
        modes_ref[:, pl.ds(i * rows, rows)] = modes
        part = jnp.dot(three(modes, 0), x, preferred_element_type=jnp.float32)
        acc_ref[...] = part if i == 0 else acc_ref[...] + part
    coords = fold(acc_ref[...], 0).T
    coords = coords.reshape(out_ref.shape[0], 2, 8, RANK)
    out_ref[...] = jnp.concatenate([coords[:, 0], coords[:, 1]], axis=-1)


def factor_kernel(corr_ref, modes_ref, projection_ref, inverse_ref):
    row = lax.broadcasted_iota(jnp.int32, (RANK, RANK), 0)
    column = lax.broadcasted_iota(jnp.int32, (RANK, RANK), 1)
    unit = jnp.where(row == column, jnp.float32(1.0), jnp.float32(0.0))
    work = jnp.concatenate([corr_ref[...], unit], axis=1)
    index = lax.broadcasted_iota(jnp.int32, (RANK, 1), 0)
    for k in range(RANK):
        pivot = work[k : k + 1, k : k + 1]
        scale = 1.0 / jnp.sqrt(pivot)
        line = work[k : k + 1, :] * scale
        multiplier = jnp.where(index > k, work[:, k : k + 1] * scale, 0.0)
        inverse_ref[k : k + 1, :] = line[:, RANK:]
        work = work - multiplier * line
    inverse = inverse_ref[...]
    modes = jnp.dot(
        inverse,
        modes_ref[...],
        precision=lax.Precision.HIGHEST,
        preferred_element_type=jnp.float32,
    )
    projection_ref[...] = modes.astype(jnp.bfloat16)


def advance(state, linear_op, quad_op, offset):
    pairs = (state[:, :, None] * state[:, None, :]).reshape(state.shape[0], -1)
    highest = lax.Precision.HIGHEST
    change = (
        jnp.dot(state, linear_op, precision=highest)
        + jnp.dot(pairs, quad_op, precision=highest)
        + offset[None, :]
    )
    return state + 0.25 * change


def exchanged_sum(parts):
    return jnp.sum(lax.all_to_all(parts, EVERY, 0, 0, tiled=True), axis=0)


def body(snapshots, start_block, linear_op, quad_op, offset):
    devices = lax.axis_size(EVERY)
    rows, width = snapshots.shape
    share = width // devices
    tile = (RANK * share // 128, 128)
    scratch = [
        pltpu.VMEM((rows, width), jnp.bfloat16),
        pltpu.VMEM((3 * RANK, width), jnp.float32),
        pltpu.SemaphoreType.DMA((CHUNKS,)),
    ]
    tiles = jax.ShapeDtypeStruct((devices, *tile), jnp.float32)
    parts = pl.pallas_call(
        power_kernel,
        out_shape=tiles,
        in_specs=[ANY, VMEM],
        out_specs=VMEM,
        scratch_shapes=scratch,
        compiler_params=LIMIT,
        name="power",
    )(snapshots, start_block.T)
    mine = exchanged_sum(parts)
    spread = jnp.broadcast_to(mine[None], (devices, *tile))
    power = lax.all_to_all(spread, EVERY, 0, 0, tiled=True)
    small = jax.ShapeDtypeStruct((RANK, RANK), jnp.float32)
    parts, modes, correlation = pl.pallas_call(
        coords_kernel,
        out_shape=(tiles, jax.ShapeDtypeStruct((RANK, rows), jnp.float32), small),
        in_specs=[ANY, VMEM],
        out_specs=(VMEM, VMEM, VMEM),
        scratch_shapes=scratch,
        compiler_params=LIMIT,
        name="coords",
    )(snapshots, power)
    packed = exchanged_sum(parts)
    projection, inverse = pl.pallas_call(
        factor_kernel,
        out_shape=(jax.ShapeDtypeStruct((RANK, rows), jnp.bfloat16), small),
        in_specs=[VMEM, VMEM],
        out_specs=(VMEM, VMEM),
        compiler_params=LIMIT,
        name="factor",
    )(correlation, modes)
    factor_scale = math.sqrt(width) / (rows * devices)
    highest = lax.Precision.HIGHEST
    coords = jnp.concatenate([packed[:, :RANK], packed[:, RANK:]], axis=0)
    reduced = lax.dot_general(coords, inverse, NT, precision=highest) * factor_scale
    state = advance(advance(reduced, linear_op, quad_op, offset), linear_op, quad_op, offset)
    route = [(i + 1, i) for i in range(devices - 1)]
    following = lax.ppermute(reduced[:2], EVERY, route)
    target = jnp.concatenate([reduced[2:], following], axis=0)
    position = lax.axis_index(EVERY) * share + jnp.arange(share, dtype=jnp.int32)
    mismatch = jnp.where((position < width - 2)[:, None], state - target, jnp.float32(0.0))
    return (projection.T, reduced, mismatch)


def solution(mesh):
    whole = P(EVERY, None)
    return jax.shard_map(
        body,
        mesh=mesh,
        in_specs=(whole, P(), P(), P(), P()),
        out_specs=(whole, whole, whole),
        check_vma=False,
    )
```

time: 292 us -> 92.2 us (0.32)
  waiting for transfers between devices: 175 us -> 9.54 us
  matrix products: 41.2 us -> 2.91 us
  Pallas kernels: 0 us -> 28.5 us
  between operations: 13.9 us -> 0.77 us
  other arithmetic: 12.5 us -> 0.69 us
  local copies, waits for them, and re-layouts: 6.61 us -> 1.66 us
  starting transfers between devices: 1.45 us -> 5.92 us
    reduce_scatter x4 -> x0, waiting for transfers between devices: 171 us -> none  [own_block(): parts = lax.psum_scatter(parts, axes[k], scatter_dimension=0, tiled=True)]
    all_to_all x0 -> x2, blocking collectives: none -> 41.7 us  [the longest x1 24.2 us: exchanged_sum(): return jnp.sum(lax.all_to_all(parts, EVERY, 0, 0, tiled=True), axis=0)]
    all_gather x4 -> x0, blocking collectives: 40.2 us -> none  [gather_in_order(): parts = lax.all_gather(parts, axes[k])]
    dot_general x5 -> x1, matrix products: 37.2 us -> 0.14 us  [body(): lax.dot_general(coords, inverse, NT, precision=highest) * factor_scale]
    pallas_call x0 -> x3, Pallas kernels: none -> 28.5 us  [the longest x1 11 us: body(): pl.pallas_call(coords_kernel, out_shape=(tiles, jax.ShapeDtypeStruct((RAN...]
    another operation x5 -> x0, other arithmetic: 12.1 us -> none  [the longest x3 6.52 us: normalize(): factor = jnp.linalg.cholesky(jnp.dot(power.T, power, precision=highest))]
    another operation x1 -> x0, local copies, waits for them, and re-layouts: 6.02 us -> none  [own_block(): parts = parts.reshape(*shape, *parts.shape[1:])]
    all_to_all x0 -> x1, waiting for transfers between devices: none -> 5.71 us  [exchanged_sum(): return jnp.sum(lax.all_to_all(parts, EVERY, 0, 0, tiled=True), axis=0)]
  transfers between devices with their start and end apart: 5 -> 2, of which waited for: 5 -> 2; matrix products, arithmetic and copies ran while one was open for 0% -> 0% of each run, Pallas kernels for 0% -> 8%
where the time goes in v1:
time: 92.2 us; the launch traced here: 91.7 us
  blocking collectives  41.7 us (45%)
  Pallas kernels  28.5 us (31%)
  waiting for transfers between devices  9.54 us (10%)
  starting transfers between devices  5.92 us (6%)
  matrix products  2.91 us (3%)
  local copies, waits for them, and re-layouts  1.66 us (2%)
    all_to_all x1, blocking collectives, exchanged_sum(): return jnp.sum(lax.all_to_all(parts, EVERY, 0, 0, tiled=True), axis=0)  24.2 us
    all_to_all x1, blocking collectives, body(): power = lax.all_to_all(spread, EVERY, 0, 0, tiled=True)  17.5 us
    pallas_call x1, Pallas kernels, body(): pl.pallas_call(coords_kernel, out_shape=(tiles, jax.ShapeDtypeStruct((RAN...  11 us
    pallas_call x1, Pallas kernels, body(): pl.pallas_call(power_kernel, out_shape=tiles, in_specs=[ANY, VMEM], out_s...  9.96 us
    pallas_call x1, Pallas kernels, body(): pl.pallas_call(factor_kernel, out_shape=(jax.ShapeDtypeStruct((RANK, rows...  7.58 us
    all_to_all x1, waiting for transfers between devices, exchanged_sum(): return jnp.sum(lax.all_to_all(parts, EVERY, 0, 0, tiled=True), axis=0)  5.71 us
    all_to_all x1, starting transfers between devices, exchanged_sum(): return jnp.sum(lax.all_to_all(parts, EVERY, 0, 0, tiled=True), axis=0)  4.63 us
    ppermute x1, waiting for transfers between devices, body(): following = lax.ppermute(reduced[:2], EVERY, route)  3.83 us
  transfers between devices with their start and end apart: 2, of which 2 were waited for; matrix products, arithmetic and copies ran while one was open for 0% of the time, Pallas kernels for 8%

profile of v1, /device:TPU:0, one launch (start us, length us, event | category | flops | bytes accessed | tf_op | source)
XLA Modules:
  0.0 91.7 jit_solution(7058382802600491948)
XLA Ops:
  0.6 0.0 copy-start
  0.6 0.0 copy-start.1
  0.7 1.1 %copy-done.1 = f32[2048,64]{0,1:T(8,128)S(1)} copy-done((f32[2048,64]{0,1:T(8,128)S(1)}, f32[2048,64]{0,1:T(8,128)}, u32[]{:S(2)}) %copy-start.1) | copy-done | bytes 524312
  1.8 10.0 %power.1 = f32[128,8,128]{2,1,0:T(8,128)S(1)} custom-call(bf16[2048,2048]{1,0:T(8,128)(2,1)} %x_hbm.3, f32[64,2048]{1,0:T(8,128)S(1)} %bitcast.11), custom_call_target="tpu_custom_call" | custom-call | tf_op jit(solution)/shard_map/power/pallas_call | solution.py:141
  11.7 0.0 copy-start.3
  11.8 0.0 copy-start.4
  11.8 24.2 %all_to_all.15 = f32[128,8,128]{2,1,0:T(8,128)S(1)} all-to-all(f32[128,8,128]{2,1,0:T(8,128)S(1)} %power.1), channel_id=1, replica_groups=mesh['rows'=32,'slab'=4] {'rows','slab'}, dimensions={0} | all-to-all | bytes 1048576 | tf_op jit(solution)/shard_map/all_to_all | solution.py:127
  36.0 0.1 reduce_sum.18
  36.2 17.5 %all_to_all.16.power_ref = f32[128,8,128]{2,1,0:T(8,128)S(1)} all-to-all(f32[128,8,128]{2,1,0:T(8,128)S(1)} %broadcast_in_dim.10), channel_id=1, replica_groups=mesh['rows'=32,'slab'=4] {'rows','slab'}, dimensions={0} | all-to-all | bytes 1048576 | tf_op jit(solution)/shard_map/all_to_all | solution.py:152
  53.7 11.0 %coords.1 = (f32[128,8,128]{2,1,0:T(8,128)}, f32[64,2048]{1,0:T(8,128)S(1)}, f32[64,64]{1,0:T(8,128)S(1)}) custom-call(bf16[2048,2048]{1,0:T(8,128)(2,1)} %x_hbm.3, f32[128,8,128]{2,1,0:T(8,128)S(1)} %all_to_all.16.power_ref), custom_call_target="tpu_custom_call" | custom-call | tf_op jit(solution)/shard_map/coords/pallas_call | solution.py:154
  64.7 4.6 %all-to-all-start.2 = ((f32[128,8,128]{2,1,0:T(8,128)}), f32[128,8,128]{2,1,0:T(8,128)S(1)}, u32[]{:S(2)}, u32[]{:S(2)}) async-start(f32[128,8,128]{2,1,0:T(8,128)} %get-tuple-element.11), calls=%async_computation.2 | async-start | bytes 1048576 | tf_op jit(solution)/shard_map/all_to_all | solution.py:127
  69.3 7.6 %factor.1 = (bf16[64,2048]{1,0:T(8,128)(2,1)}, f32[64,64]{1,0:T(8,128)S(1)}) custom-call(f32[64,64]{1,0:T(8,128)S(1)} %get-tuple-element.8.corr_ref, f32[64,2048]{1,0:T(8,128)S(1)} %get-tuple-element.9.modes_ref), custom_call_target="tpu_custom_call" | custom-call | tf_op jit(solution)/shard_map/factor/pallas_call | solution.py:164
  76.9 5.7 %all-to-all-done.2 = f32[128,8,128]{2,1,0:T(8,128)S(1)} async-done(((f32[128,8,128]{2,1,0:T(8,128)}), f32[128,8,128]{2,1,0:T(8,128)S(1)}, u32[]{:S(2)}, u32[]{:S(2)}) %all-to-all-start.2) | async-done | bytes 524320 | tf_op jit(solution)/shard_map/all_to_all | solution.py:127
  82.6 0.1 reduce_sum.19
  82.7 0.1 fusion.11
  82.8 0.1 convolution_multiply_fusion
  83.0 0.0 copy-start.2
  83.0 0.2 broadcast_multiply_fusion.1
  83.2 0.2 mul.59
  83.4 0.0 copy-done.3
  83.4 0.1 fusion.12
  83.5 0.0 copy-done
  83.5 0.0 copy-done.4
  83.6 0.9 %fusion.4 = f32[16,64]{1,0:T(8,128)S(1)} fusion(f32[16,64]{1,0:T(8,128)S(1)} %convolution_multiply_fusion, f32[16,64]{1,0:T(8,128)S(1)} %fusion.12, f32[16,4096]{1,0:T(8,128)S(1)} %mul.59, f32[4096,64]{0,1:T(8,128)S(1)} %copy-done, f32[64]{0:T(128)S(1)} %copy-done.4), kind=kOutput, calls=%fused_computation.7 | convolution fusion | flops 50335744 | bytes 1323264 | tf_op jit(solution)/shard_map/dot_general | solution.py:120
  84.5 0.2 broadcast_multiply_fusion
  84.7 1.3 %collective-permute-start = (f32[2,64]{1,0:T(2,128)S(1)}, f32[2,64]{1,0:T(2,128)S(1)}, u32[]{:S(2)}, u32[]{:S(2)}) collective-permute-start(f32[2,64]{1,0:T(2,128)S(1)} %slice.17), channel_id=1, source_target_pairs={{1,0},{2,1},{3,2},{4,3},{5,4},{6,5},{7,6},{8,7},{9,8},{10,9},{11,1... | collective-permute-start | bytes 1544 | tf_op jit(solution)/shard_map/ppermute | solution.py:178
  86.0 0.1 fusion.13
  86.2 0.2 mul.64
  86.3 3.8 %collective-permute-done = f32[2,64]{1,0:T(2,128)S(1)} collective-permute-done((f32[2,64]{1,0:T(2,128)S(1)}, f32[2,64]{1,0:T(2,128)S(1)}, u32[]{:S(2)}, u32[]{:S(2)}) %collective-permute-start) | collective-permute-done | bytes 544 | tf_op jit(solution)/shard_map/ppermute | solution.py:178
  90.2 1.6 %fusion.9 = f32[16,64]{1,0:T(8,128)} fusion(f32[2,64]{1,0:T(2,128)S(1)} %collective-permute-done, f32[14,64]{1,0:T(8,128)S(1)} %slice.16, f32[16,64]{1,0:T(8,128)S(1)} %fusion.4, f32[16,64]{1,0:T(8,128)S(1)} %fusion.13, f32[16,4096]{1,0:T(8,128)S(1)} %mul.64, f32[4096,64]{0,1:T(8,128)S(1)} %copy-done, f32[64]{0:T(128)S(1)} %copy-done.4, ...), kind=kOutput, calls=%fused_computation.15 | convolution fusion | flops 50338816 | bytes 1327376 | tf_op jit(solution)/shard_map/dot_general | solution.py:120
  91.7 0.0 copy-done.2
  (4 shorter events, 0.1 us)
Async XLA Ops:
  0.6 82.9 %copy-start = (f32[4096,64]{0,1:T(8,128)S(1)}, f32[4096,64]{0,1:T(8,128)}, u32[]{:S(2)}) copy-start(f32[4096,64]{0,1:T(8,128)} %param.8) | copy-start | bytes 3145732
  0.6 1.1 %copy-start.1 = (f32[2048,64]{0,1:T(8,128)S(1)}, f32[2048,64]{0,1:T(8,128)}, u32[]{:S(2)}) copy-start(f32[2048,64]{0,1:T(8,128)} %param.6) | copy-start | bytes 1572868
  11.7 71.7 %copy-start.3 = (f32[64,64]{1,0:T(8,128)S(1)}, f32[64,64]{1,0:T(8,128)}, u32[]{:S(2)}) copy-start(f32[64,64]{1,0:T(8,128)} %param.7) | copy-start | bytes 49156
  11.8 71.8 %copy-start.4 = (f32[64]{0:T(128)S(1)}, f32[64]{0:T(128)}, u32[]{:S(2)}) copy-start(f32[64]{0:T(128)} %param.9) | copy-start | bytes 772
  64.7 17.9 %all-to-all-start.2 = ((f32[128,8,128]{2,1,0:T(8,128)}), f32[128,8,128]{2,1,0:T(8,128)S(1)}, u32[]{:S(2)}, u32[]{:S(2)}) async-start(f32[128,8,128]{2,1,0:T(8,128)} %get-tuple-element.11), calls=%async_computation.2 | async-start | bytes 1048576 | tf_op jit(solution)/shard_map/all_to_all | solution.py:127
  83.0 8.8 %copy-start.2 = (f32[16,64]{1,0:T(8,128)}, f32[16,64]{1,0:T(8,128)S(1)}, u32[]{:S(2)}) copy-start(f32[16,64]{1,0:T(8,128)S(1)} %convolution_multiply_fusion) | copy-start | bytes 12292
  84.7 5.5 %collective-permute-start = (f32[2,64]{1,0:T(2,128)S(1)}, f32[2,64]{1,0:T(2,128)S(1)}, u32[]{:S(2)}, u32[]{:S(2)}) collective-permute-start(f32[2,64]{1,0:T(2,128)S(1)} %slice.17), channel_id=1, source_target_pairs={{1,0},{2,1},{3,2},{4,3},{5,4},{6,5},{7,6},{8,7},{9,8},{10,9},{11,1... | collective-permute-start | bytes 1544 | tf_op jit(solution)/shard_map/ppermute | solution.py:178

commit v2 on v1

v2 whole, which is shorter than its diff:
```python
import math

import jax
import jax.numpy as jnp
from jax import lax
from jax.experimental import pallas as pl
from jax.experimental.pallas import tpu as pltpu
from jax.sharding import PartitionSpec as P

EVERY = ("rows", "slab")
RANK = 64
CHUNKS = 4
NT = (((1,), (1,)), ((), ()))
LIMIT = pltpu.CompilerParams(vmem_limit_bytes=20 * 1024 * 1024)
VMEM = pl.BlockSpec(memory_space=pltpu.VMEM)
HBM = pl.BlockSpec(memory_space=pltpu.HBM)


def three(value):
    high = value.astype(jnp.bfloat16)
    rest = value - high.astype(jnp.float32)
    middle = rest.astype(jnp.bfloat16)
    low = (rest - middle.astype(jnp.float32)).astype(jnp.bfloat16)
    return jnp.concatenate([high, middle, low], axis=0)


def fold_rows(value):
    third = value.shape[0] // 3
    return value[:third] + value[third : 2 * third] + value[2 * third :]


def fold_lanes(value):
    third = value.shape[1] // 3
    return value[:, :third] + value[:, third : 2 * third] + value[:, 2 * third :]


def dot_nt(left, right):
    return lax.dot_general(left, right, NT, preferred_element_type=jnp.float32)


def passes(weights, block, ready, acc_ref, keep):
    held = None
    for i in range(CHUNKS):
        ready(i)
        inner = fold_rows(dot_nt(weights, block(i)))
        if held is not None:
            part = jnp.dot(held, block(i - 1), preferred_element_type=jnp.float32)
            acc_ref[...] = part if i == 1 else acc_ref[...] + part
        keep(i, inner)
        held = three(inner)
    part = jnp.dot(held, block(CHUNKS - 1), preferred_element_type=jnp.float32)
    return fold_rows(acc_ref[...] + part)


def power_kernel(x_hbm, start_hbm, out_ref, x_ref, start_ref, acc_ref, sems):
    rows = x_ref.shape[0] // CHUNKS
    first = pltpu.make_async_copy(start_hbm, start_ref, sems.at[CHUNKS])
    first.start()
    copies = [
        pltpu.make_async_copy(
            x_hbm.at[pl.ds(i * rows, rows)], x_ref.at[pl.ds(i * rows, rows)], sems.at[i]
        )
        for i in range(CHUNKS)
    ]
    for copy in copies:
        copy.start()
    first.wait()
    weights = three(start_ref[...])
    power = passes(
        weights,
        lambda i: x_ref[pl.ds(i * rows, rows), :],
        lambda i: copies[i].wait(),
        acc_ref,
        lambda i, inner: None,
    )
    wide = power.shape[1] // 128
    for i in range(out_ref.shape[0]):
        a, b = divmod(i, wide)
        out_ref[i] = power[8 * a : 8 * a + 8, 128 * b : 128 * b + 128]


def spread_kernel(parts_ref, out_ref):
    out_ref[...] = jnp.broadcast_to(jnp.sum(parts_ref[...], axis=0)[None], out_ref.shape)


def coords_kernel(x_ref, power_ref, out_ref, modes_ref, corr_ref, acc_ref):
    rows = x_ref.shape[0] // CHUNKS
    tall = RANK // 8
    wide = power_ref.shape[0] // tall
    power = jnp.concatenate(
        [
            jnp.concatenate([power_ref[a * wide + b] for b in range(wide)], axis=1)
            for a in range(tall)
        ],
        axis=0,
    )
    weights = three(power)

    def keep(i, inner):
        modes_ref[:, pl.ds(i * rows, rows)] = inner

    coords = passes(
        weights, lambda i: x_ref[pl.ds(i * rows, rows), :], lambda i: None, acc_ref, keep
    ).T
    coords = coords.reshape(out_ref.shape[0], 2, 8, RANK)
    out_ref[...] = jnp.concatenate([coords[:, 0], coords[:, 1]], axis=-1)
    corr_ref[...] = fold_rows(fold_lanes(dot_nt(weights, weights)))


def factor_kernel(corr_ref, modes_ref, quad_ref, projection_ref, inverse_ref, pieces_ref):
    pieces_ref[...] = three(quad_ref[...])
    row = lax.broadcasted_iota(jnp.int32, (RANK, RANK), 0)
    column = lax.broadcasted_iota(jnp.int32, (RANK, RANK), 1)
    unit = jnp.where(row == column, jnp.float32(1.0), jnp.float32(0.0))
    work = jnp.concatenate([corr_ref[...], unit], axis=1)
    index = lax.broadcasted_iota(jnp.int32, (RANK, 1), 0)
    for k in range(RANK):
        line = work[k : k + 1, :]
        pivot = line[:, k : k + 1]
        inverse_ref[k : k + 1, :] = line[:, RANK:] * (1.0 / jnp.sqrt(pivot))
        multiplier = jnp.where(index > k, work[:, k : k + 1], 0.0)
        work = work - multiplier * (line * (1.0 / pivot))
    inverse = inverse_ref[...]
    modes = jnp.dot(
        inverse,
        modes_ref[...],
        precision=lax.Precision.HIGHEST,
        preferred_element_type=jnp.float32,
    )
    projection_ref[...] = modes.astype(jnp.bfloat16)


def reduced_kernel(scale, parts_ref, inverse_ref, out_ref, keep_ref, head_ref):
    packed = jnp.sum(parts_ref[...], axis=0)
    coords = jnp.concatenate([packed[:, :RANK], packed[:, RANK:]], axis=0)
    reduced = scale * lax.dot_general(
        coords,
        inverse_ref[...],
        NT,
        precision=lax.Precision.HIGHEST,
        preferred_element_type=jnp.float32,
    )
    out_ref[...] = reduced
    keep_ref[...] = reduced
    head_ref[...] = reduced[:2]


def rollout_kernel(reduced_ref, linear_ref, pieces_ref, offset_ref, out_ref):
    state = reduced_ref[...]
    pieces = pieces_ref[...]
    upper = lax.broadcasted_iota(jnp.int32, (state.shape[0], 2 * RANK), 1) >= RANK
    for _ in range(2):
        twice = jnp.concatenate([state, state], axis=1)
        pairs = jnp.concatenate(
            [
                jnp.where(upper, state[:, 2 * i + 1 : 2 * i + 2], state[:, 2 * i : 2 * i + 1])
                * twice
                for i in range(RANK // 2)
            ],
            axis=1,
        )
        quadratic = fold_rows(fold_lanes(dot_nt(three(pairs), pieces)))
        linear = jnp.dot(
            state,
            linear_ref[...],
            precision=lax.Precision.HIGHEST,
            preferred_element_type=jnp.float32,
        )
        state = state + 0.25 * (linear + quadratic + offset_ref[...])
    out_ref[...] = state


def in_hbm(value):
    return pltpu.with_memory_space_constraint(value, pltpu.HBM)


def call(kernel, name, outs, ins, scratch=()):
    return pl.pallas_call(
        kernel,
        out_shape=outs,
        in_specs=ins,
        out_specs=jax.tree.map(lambda _: VMEM, outs),
        scratch_shapes=list(scratch),
        compiler_params=LIMIT,
        name=name,
    )


def body(snapshots, start_block, linear_op, quad_op, offset):
    devices = lax.axis_size(EVERY)
    rows, width = snapshots.shape
    share = width // devices
    f32 = jnp.float32
    shape = jax.ShapeDtypeStruct
    tiles = shape((devices, RANK * share // 128, 128), f32)
    small = shape((RANK, RANK), f32)
    own = shape((share, RANK), f32)
    acc = pltpu.VMEM((3 * RANK, width), f32)
    parts, held = call(
        power_kernel,
        "power",
        (tiles, shape((rows, width), jnp.bfloat16)),
        [HBM, HBM],
        [
            pltpu.VMEM((RANK, width), f32),
            acc,
            pltpu.SemaphoreType.DMA((CHUNKS + 1,)),
        ],
    )(in_hbm(snapshots), in_hbm(start_block.T))
    parts = lax.all_to_all(parts, EVERY, 0, 0, tiled=True)
    spread = call(spread_kernel, "spread", tiles, [VMEM])(parts)
    power = lax.all_to_all(spread, EVERY, 0, 0, tiled=True)
    parts, modes, correlation = call(
        coords_kernel,
        "coords",
        (tiles, shape((RANK, rows), f32), small),
        [VMEM, VMEM],
        [acc],
    )(held, power)
    parts = lax.all_to_all(parts, EVERY, 0, 0, tiled=True)
    projection, inverse, pieces = call(
        factor_kernel,
        "factor",
        (shape((RANK, rows), jnp.bfloat16), small, shape((3 * RANK, RANK * RANK), jnp.bfloat16)),
        [VMEM, VMEM, VMEM],
    )(correlation, modes, quad_op.T)
    factor_scale = math.sqrt(width) / (rows * devices)
    reduced, kept, head = call(
        lambda *refs: reduced_kernel(factor_scale, *refs),
        "reduced",
        (own, own, shape((2, RANK), f32)),
        [VMEM, VMEM],
    )(parts, inverse)
    route = [(i + 1, i) for i in range(devices - 1)]
    following = lax.ppermute(head, EVERY, route)
    state = call(rollout_kernel, "rollout", own, [VMEM] * 4)(
        kept, linear_op, pieces, offset[None, :]
    )
    target = jnp.concatenate([kept[2:], following], axis=0)
    position = lax.axis_index(EVERY) * share + jnp.arange(share, dtype=jnp.int32)
    mismatch = jnp.where((position < width - 2)[:, None], state - target, jnp.float32(0.0))
    return (projection.T, reduced, mismatch)


def solution(mesh):
    whole = P(EVERY, None)
    return jax.shard_map(
        body,
        mesh=mesh,
        in_specs=(whole, P(), P(), P(), P()),
        out_specs=(whole, whole, whole),
        check_vma=False,
    )
```

time: 92.2 us -> 82.1 us (0.89); the launches traced: 91.7 us -> 80.6 us
  Pallas kernels: 28.5 us -> 22.5 us
  matrix products: 2.91 us -> 0 us
  waiting for transfers between devices: 9.54 us -> 7.21 us
    pallas_call x3 -> x6, Pallas kernels: 28.5 us -> 22.5 us  [the longest x1 7.07 us: body(): call(factor_kernel, 'factor', (shape((RANK, rows), jnp.bfloat16), small,...]
    dot_general x5 -> x0, matrix products: 2.91 us -> none  [the longest x2 2.5 us: advance(): jnp.dot(pairs, quad_op, precision=highest)]
    ppermute x1, waiting for transfers between devices: 3.83 us -> 2.04 us  [body(): following = lax.ppermute(head, EVERY, route)]
  transfers between devices with their start and end apart: 2 -> 2, of which waited for: 2 -> 2; matrix products, arithmetic and copies ran while one was open for 0% -> 0% of each run, Pallas kernels for 8% -> 11%
where the time goes in v2:
time: 82.1 us; the launch traced here: 80.6 us
  blocking collectives  41.7 us (51%)
  Pallas kernels  22.5 us (27%)
  waiting for transfers between devices  7.21 us (9%)
  starting transfers between devices  5.88 us (7%)
  local copies, waits for them, and re-layouts  1.84 us (2%)
    all_to_all x1, blocking collectives, body(): parts = lax.all_to_all(parts, EVERY, 0, 0, tiled=True)  24.3 us
    all_to_all x1, blocking collectives, body(): power = lax.all_to_all(spread, EVERY, 0, 0, tiled=True)  17.5 us
    pallas_call x1, Pallas kernels, body(): call(factor_kernel, 'factor', (shape((RANK, rows), jnp.bfloat16), small,...  7.07 us
    pallas_call x1, Pallas kernels, body(): call(power_kernel, 'power', (tiles, shape((rows, width), jnp.bfloat16)),...  6.59 us
    pallas_call x1, Pallas kernels, body(): call(coords_kernel, 'coords', (tiles, shape((RANK, rows), f32), small), [...  5.64 us
    all_to_all x1, waiting for transfers between devices, body(): parts = lax.all_to_all(parts, EVERY, 0, 0, tiled=True)  5.17 us
    all_to_all x1, starting transfers between devices, body(): parts = lax.all_to_all(parts, EVERY, 0, 0, tiled=True)  4.6 us
    pallas_call x1, Pallas kernels, body(): call(rollout_kernel, 'rollout', own, [VMEM] * 4)  2.07 us
  transfers between devices with their start and end apart: 2, of which 2 were waited for; matrix products, arithmetic and copies ran while one was open for 0% of the time, Pallas kernels for 11%

profile of v2, /device:TPU:0, one launch (start us, length us, event | category | flops | bytes accessed | tf_op | source)
XLA Modules:
  0.0 80.6 jit_solution(18443444276421475001)
XLA Ops:
  0.6 6.6 %power.1 = (f32[128,8,128]{2,1,0:T(8,128)S(1)}, bf16[2048,2048]{1,0:T(8,128)(2,1)S(1)}) custom-call(bf16[2048,2048]{1,0:T(8,128)(2,1)} %x_hbm.1, f32[64,2048]{1,0:T(8,128)} %bitcast.6), custom_call_target="tpu_custom_call" | custom-call | tf_op jit(solution)/shard_map/power/pallas_call | solution.py:199
  7.2 0.0 copy-start
  7.2 0.0 copy-start.3
  7.3 0.0 copy-start.4
  7.3 24.3 %all_to_all.15.parts_ref = f32[128,8,128]{2,1,0:T(8,128)S(1)} all-to-all(f32[128,8,128]{2,1,0:T(8,128)S(1)} %get-tuple-element.15), channel_id=1, replica_groups=mesh['rows'=32,'slab'=4] {'rows','slab'}, dimensions={0} | all-to-all | bytes 1048576 | tf_op jit(solution)/shard_map/all_to_all | solution.py:210
  31.5 0.2 spread.1
  31.7 17.5 %all_to_all.16.power_ref = f32[128,8,128]{2,1,0:T(8,128)S(1)} all-to-all(f32[128,8,128]{2,1,0:T(8,128)S(1)} %spread.1), channel_id=1, replica_groups=mesh['rows'=32,'slab'=4] {'rows','slab'}, dimensions={0} | all-to-all | bytes 1048576 | tf_op jit(solution)/shard_map/all_to_all | solution.py:212
  49.2 5.6 %coords.1 = (f32[128,8,128]{2,1,0:T(8,128)}, f32[64,2048]{1,0:T(8,128)S(1)}, f32[64,64]{1,0:T(8,128)S(1)}) custom-call(bf16[2048,2048]{1,0:T(8,128)(2,1)S(1)} %get-tuple-element.14.x_ref, f32[128,8,128]{2,1,0:T(8,128)S(1)} %all_to_all.16.power_ref), custom_call_target="tpu_custom_call" | custom-call | tf_op jit(solution)/shard_map/coords/pallas_call | solution.py:213
  54.8 0.0 copy-start.1
  54.8 0.8 copy-done.1
  55.6 4.6 %all-to-all-start.2 = ((f32[128,8,128]{2,1,0:T(8,128)}), f32[128,8,128]{2,1,0:T(8,128)S(1)}, u32[]{:S(2)}, u32[]{:S(2)}) async-start(f32[128,8,128]{2,1,0:T(8,128)} %get-tuple-element.19), calls=%async_computation.2 | async-start | bytes 1048576 | tf_op jit(solution)/shard_map/all_to_all | solution.py:220
  60.2 0.0 copy-done
  60.2 0.0 copy-start.2
  60.2 1.0 %copy-done.2 = f32[64,2048]{1,0:T(8,128)S(1)} copy-done((f32[64,2048]{1,0:T(8,128)S(1)}, f32[64,2048]{1,0:T(8,128)}, u32[]{:S(2)}) %copy-start.2) | copy-done | bytes 524312
  61.3 7.1 %factor.1 = (bf16[64,2048]{1,0:T(8,128)(2,1)}, f32[64,64]{1,0:T(8,128)S(1)}, bf16[192,4096]{1,0:T(8,128)(2,1)S(1)}) custom-call(f32[64,64]{1,0:T(8,128)S(1)} %get-tuple-element.16.corr_ref, f32[64,2048]{1,0:T(8,128)S(1)} %copy-done.2, f32[64,4096]{1,0:T(8,128)S(1)} %bitcast.4), custom_call_target="tpu_custom_call" | custom-call | tf_op jit(solution)/shard_map/factor/pallas_call | solution.py:221
  68.3 5.2 %all-to-all-done.2.refs_0_ = f32[128,8,128]{2,1,0:T(8,128)S(1)} async-done(((f32[128,8,128]{2,1,0:T(8,128)}), f32[128,8,128]{2,1,0:T(8,128)S(1)}, u32[]{:S(2)}, u32[]{:S(2)}) %all-to-all-start.2) | async-done | bytes 524320 | tf_op jit(solution)/shard_map/all_to_all | solution.py:220
  73.5 1.0 %reduced.1 = (f32[16,64]{1,0:T(8,128)}, f32[16,64]{1,0:T(8,128)S(1)}, f32[2,64]{1,0:T(2,128)S(1)}) custom-call(f32[128,8,128]{2,1,0:T(8,128)S(1)} %all-to-all-done.2.refs_0_, f32[64,64]{1,0:T(8,128)S(1)} %get-tuple-element.20.refs_1_), custom_call_target="tpu_custom_call" | custom-call | tf_op jit(solution)/shard_map/reduced/pallas_call | solution.py:228
  74.5 1.3 %collective-permute-start = (f32[2,64]{1,0:T(2,128)S(1)}, f32[2,64]{1,0:T(2,128)S(1)}, u32[]{:S(2)}, u32[]{:S(2)}) collective-permute-start(f32[2,64]{1,0:T(2,128)S(1)} %get-tuple-element.24), channel_id=1, source_target_pairs={{1,0},{2,1},{3,2},{4,3},{5,4},{6,5},{7,6},{8,7},{9,8},{10,9},{11,1... | collective-permute-start | bytes 1544 | tf_op jit(solution)/shard_map/ppermute | solution.py:235
  75.8 0.0 copy-done.3
  75.8 0.0 copy-done.4
  75.8 2.1 %rollout.1 = f32[16,64]{1,0:T(8,128)S(1)} custom-call(f32[16,64]{1,0:T(8,128)S(1)} %get-tuple-element.22.reduced_ref, f32[64,64]{1,0:T(8,128)S(1)} %copy-done.3, bf16[192,4096]{1,0:T(8,128)(2,1)S(1)} %get-tuple-element.23.pieces_ref, f32[1,64]{1,0:T(1,128)S(1)} %bitcast.5), custom_call_target="tpu_custom_call" | custom-call | tf_op jit(solution)/shard_map/rollout/pallas_call | solution.py:236
  77.9 2.0 %collective-permute-done = f32[2,64]{1,0:T(2,128)S(1)} collective-permute-done((f32[2,64]{1,0:T(2,128)S(1)}, f32[2,64]{1,0:T(2,128)S(1)}, u32[]{:S(2)}, u32[]{:S(2)}) %collective-permute-start) | collective-permute-done | bytes 544 | tf_op jit(solution)/shard_map/ppermute | solution.py:235
  79.9 0.7 fusion
  (2 shorter events, 0.0 us)
Async XLA Ops:
  7.2 53.0 %copy-start = (f32[4096,64]{0,1:T(8,128)S(1)}, f32[4096,64]{0,1:T(8,128)}, u32[]{:S(2)}) copy-start(f32[4096,64]{0,1:T(8,128)} %param.8) | copy-start | bytes 3145732
  7.2 68.5 %copy-start.3 = (f32[64,64]{1,0:T(8,128)S(1)}, f32[64,64]{1,0:T(8,128)}, u32[]{:S(2)}) copy-start(f32[64,64]{1,0:T(8,128)} %linear_ref.1) | copy-start | bytes 49156
  7.3 68.5 %copy-start.4 = (f32[64]{0:T(128)S(1)}, f32[64]{0:T(128)}, u32[]{:S(2)}) copy-start(f32[64]{0:T(128)} %param.9) | copy-start | bytes 772
  54.8 0.8 copy-start.1
  55.6 17.9 %all-to-all-start.2 = ((f32[128,8,128]{2,1,0:T(8,128)}), f32[128,8,128]{2,1,0:T(8,128)S(1)}, u32[]{:S(2)}, u32[]{:S(2)}) async-start(f32[128,8,128]{2,1,0:T(8,128)} %get-tuple-element.19), calls=%async_computation.2 | async-start | bytes 1048576 | tf_op jit(solution)/shard_map/all_to_all | solution.py:220
  60.2 1.0 %copy-start.2 = (f32[64,2048]{1,0:T(8,128)S(1)}, f32[64,2048]{1,0:T(8,128)}, u32[]{:S(2)}) copy-start(f32[64,2048]{1,0:T(8,128)} %copy-done.1) | copy-start | bytes 1572868
  74.5 5.5 %collective-permute-start = (f32[2,64]{1,0:T(2,128)S(1)}, f32[2,64]{1,0:T(2,128)S(1)}, u32[]{:S(2)}, u32[]{:S(2)}) collective-permute-start(f32[2,64]{1,0:T(2,128)S(1)} %get-tuple-element.24), channel_id=1, source_target_pairs={{1,0},{2,1},{3,2},{4,3},{5,4},{6,5},{7,6},{8,7},{9,8},{10,9},{11,1... | collective-permute-start | bytes 1544 | tf_op jit(solution)/shard_map/ppermute | solution.py:235

commit v3 on v2

--- a/solution.py
+++ b/solution.py
@@ -5,13 +5,17 @@
 from jax import lax
 from jax.experimental import pallas as pl
 from jax.experimental.pallas import tpu as pltpu
+from jax.sharding import Mesh
 from jax.sharding import PartitionSpec as P
 
-EVERY = ("rows", "slab")
+EVERY = ("yz", "core", "slab")
+CHIPS = ("yz", "slab")
+CORES = 2
 RANK = 64
 CHUNKS = 4
 NT = (((1,), (1,)), ((), ()))
 LIMIT = pltpu.CompilerParams(vmem_limit_bytes=20 * 1024 * 1024)
+SMEM = pl.BlockSpec(memory_space=pltpu.SMEM)
 VMEM = pl.BlockSpec(memory_space=pltpu.VMEM)
 HBM = pl.BlockSpec(memory_space=pltpu.HBM)
 
@@ -83,32 +87,65 @@
     out_ref[...] = jnp.broadcast_to(jnp.sum(parts_ref[...], axis=0)[None], out_ref.shape)
 
 
-def coords_kernel(x_ref, power_ref, out_ref, modes_ref, corr_ref, acc_ref):
-    rows = x_ref.shape[0] // CHUNKS
+def whole_power(power_ref):
     tall = RANK // 8
     wide = power_ref.shape[0] // tall
-    power = jnp.concatenate(
-        [
-            jnp.concatenate([power_ref[a * wide + b] for b in range(wide)], axis=1)
-            for a in range(tall)
-        ],
-        axis=0,
-    )
-    weights = three(power)
-
-    def keep(i, inner):
+    rows = [
+        jnp.concatenate([power_ref[a * wide + b] for b in range(wide)], axis=1)
+        for a in range(tall)
+    ]
+    return jnp.concatenate(rows, axis=0)
+
+
+def coords_kernel(core_ref, x_ref, power_ref, keep_ref, send_ref, modes_ref, acc_ref):
+    rows = x_ref.shape[0] // CHUNKS
+    weights = three(whole_power(power_ref))
+
+    def store(i, inner):
         modes_ref[:, pl.ds(i * rows, rows)] = inner
 
     coords = passes(
-        weights, lambda i: x_ref[pl.ds(i * rows, rows), :], lambda i: None, acc_ref, keep
+        weights, lambda i: x_ref[pl.ds(i * rows, rows), :], lambda i: None, acc_ref, store
     ).T
-    coords = coords.reshape(out_ref.shape[0], 2, 8, RANK)
-    out_ref[...] = jnp.concatenate([coords[:, 0], coords[:, 1]], axis=-1)
+    groups, deep, _ = keep_ref.shape
+    coords = coords.reshape(groups, coords.shape[0] // groups, RANK)
+    after = jnp.concatenate([coords[1:, :8], coords[:1, :8]], axis=0)
+    coords = jnp.concatenate([coords, after], axis=1)
+    half = deep - 8
+    packed = [
+        jnp.concatenate(
+            [coords[:, 2 * half * c : 2 * half * c + deep], coords[:, 2 * half * c + half :][:, :deep]],
+            axis=-1,
+        )
+        for c in range(CORES)
+    ]
+    first = core_ref[0] == 0
+    keep_ref[...] = jnp.where(first, packed[0], packed[1])
+    send_ref[...] = jnp.where(first, packed[1], packed[0])
+
+
+def prepare_kernel(power_ref, quad_ref, corr_ref, pieces_ref):
+    pieces_ref[...] = three(quad_ref[...])
+    weights = three(whole_power(power_ref))
     corr_ref[...] = fold_rows(fold_lanes(dot_nt(weights, weights)))
 
 
-def factor_kernel(corr_ref, modes_ref, quad_ref, projection_ref, inverse_ref, pieces_ref):
-    pieces_ref[...] = three(quad_ref[...])
+def pair_kernel(keep_ref, came_ref, out_ref):
+    total = keep_ref[...] + came_ref[...]
+    groups = total.shape[0]
+    chips, share, _ = out_ref.shape
+    slabs = chips // groups
+    chunks = []
+    for x in range(slabs):
+        side, place = divmod(x * share, total.shape[1] - 8)
+        rows = total[:, place : place + share + 8, side * RANK : (side + 1) * RANK]
+        chunks.append(jnp.concatenate([rows[:, :share], rows[:, 2 : share + 2]], axis=-1))
+    out_ref[...] = jnp.stack(chunks, axis=1).reshape(out_ref.shape)
+
+
+def factor_kernel(corr_ref, modes_hbm, projection_ref, inverse_ref, modes_ref, sem):
+    fetch = pltpu.make_async_copy(modes_hbm, modes_ref, sem)
+    fetch.start()
     row = lax.broadcasted_iota(jnp.int32, (RANK, RANK), 0)
     column = lax.broadcasted_iota(jnp.int32, (RANK, RANK), 1)
     unit = jnp.where(row == column, jnp.float32(1.0), jnp.float32(0.0))
@@ -120,9 +157,9 @@
         inverse_ref[k : k + 1, :] = line[:, RANK:] * (1.0 / jnp.sqrt(pivot))
         multiplier = jnp.where(index > k, work[:, k : k + 1], 0.0)
         work = work - multiplier * (line * (1.0 / pivot))
-    inverse = inverse_ref[...]
+    fetch.wait()
     modes = jnp.dot(
-        inverse,
+        inverse_ref[...],
         modes_ref[...],
         precision=lax.Precision.HIGHEST,
         preferred_element_type=jnp.float32,
@@ -130,25 +167,24 @@
     projection_ref[...] = modes.astype(jnp.bfloat16)
 
 
-def reduced_kernel(scale, parts_ref, inverse_ref, out_ref, keep_ref, head_ref):
+def rollout_kernel(
+    scale, width, place_ref, parts_ref, inverse_ref, linear_ref, pieces_ref, offset_ref,
+    reduced_ref, mismatch_ref,
+):
     packed = jnp.sum(parts_ref[...], axis=0)
+    share = packed.shape[0]
     coords = jnp.concatenate([packed[:, :RANK], packed[:, RANK:]], axis=0)
-    reduced = scale * lax.dot_general(
+    coords = scale * lax.dot_general(
         coords,
         inverse_ref[...],
         NT,
         precision=lax.Precision.HIGHEST,
         preferred_element_type=jnp.float32,
     )
-    out_ref[...] = reduced
-    keep_ref[...] = reduced
-    head_ref[...] = reduced[:2]
-
-
-def rollout_kernel(reduced_ref, linear_ref, pieces_ref, offset_ref, out_ref):
-    state = reduced_ref[...]
+    state, target = coords[:share], coords[share:]
+    reduced_ref[...] = state
     pieces = pieces_ref[...]
-    upper = lax.broadcasted_iota(jnp.int32, (state.shape[0], 2 * RANK), 1) >= RANK
+    upper = lax.broadcasted_iota(jnp.int32, (share, 2 * RANK), 1) >= RANK
     for _ in range(2):
         twice = jnp.concatenate([state, state], axis=1)
         pairs = jnp.concatenate(
@@ -167,7 +203,8 @@
             preferred_element_type=jnp.float32,
         )
         state = state + 0.25 * (linear + quadratic + offset_ref[...])
-    out_ref[...] = state
+    position = place_ref[0] * share + lax.broadcasted_iota(jnp.int32, (share, 1), 0)
+    mismatch_ref[...] = jnp.where(position < width - 2, state - target, jnp.float32(0.0))
 
 
 def in_hbm(value):
@@ -196,6 +233,8 @@
     small = shape((RANK, RANK), f32)
     own = shape((share, RANK), f32)
     acc = pltpu.VMEM((3 * RANK, width), f32)
+    core, place = lax.axis_index("core")[None], lax.axis_index(EVERY)[None]
+    start_block, core, place = lax.optimization_barrier((start_block, core, place))
     parts, held = call(
         power_kernel,
         "power",
@@ -210,43 +249,51 @@
     parts = lax.all_to_all(parts, EVERY, 0, 0, tiled=True)
     spread = call(spread_kernel, "spread", tiles, [VMEM])(parts)
     power = lax.all_to_all(spread, EVERY, 0, 0, tiled=True)
-    parts, modes, correlation = call(
+    groups = lax.axis_size("yz")
+    deep = width // groups // CORES // 2 + 8
+    packed = shape((groups, deep, 2 * RANK), f32)
+    keep, send, modes = call(
         coords_kernel,
         "coords",
-        (tiles, shape((RANK, rows), f32), small),
+        (packed, packed, shape((RANK, rows), f32)),
+        [SMEM, VMEM, VMEM],
+        [acc],
+    )(core, held, power)
+    came = lax.ppermute(send, "core", [(0, 1), (1, 0)])
+    correlation, pieces = call(
+        prepare_kernel,
+        "prepare",
+        (small, shape((3 * RANK, RANK * RANK), jnp.bfloat16)),
         [VMEM, VMEM],
-        [acc],
-    )(held, power)
-    parts = lax.all_to_all(parts, EVERY, 0, 0, tiled=True)
-    projection, inverse, pieces = call(
+    )(power, quad_op.T)
+    came, correlation, pieces = lax.optimization_barrier((came, correlation, pieces))
+    chunks = shape((devices // CORES, share, 2 * RANK), f32)
+    parts = call(pair_kernel, "pair", chunks, [VMEM, VMEM])(keep, came)
+    parts = lax.all_to_all(parts, CHIPS, 0, 0, tiled=True)
+    projection, inverse = call(
         factor_kernel,
         "factor",
-        (shape((RANK, rows), jnp.bfloat16), small, shape((3 * RANK, RANK * RANK), jnp.bfloat16)),
-        [VMEM, VMEM, VMEM],
-    )(correlation, modes, quad_op.T)
+        (shape((RANK, rows), jnp.bfloat16), small),
+        [VMEM, HBM],
+        [pltpu.VMEM((RANK, rows), f32), pltpu.SemaphoreType.DMA(())],
+    )(correlation, in_hbm(modes))
     factor_scale = math.sqrt(width) / (rows * devices)
-    reduced, kept, head = call(
-        lambda *refs: reduced_kernel(factor_scale, *refs),
-        "reduced",
-        (own, own, shape((2, RANK), f32)),
-        [VMEM, VMEM],
-    )(parts, inverse)
-    route = [(i + 1, i) for i in range(devices - 1)]
-    following = lax.ppermute(head, EVERY, route)
-    state = call(rollout_kernel, "rollout", own, [VMEM] * 4)(
-        kept, linear_op, pieces, offset[None, :]
-    )
-    target = jnp.concatenate([kept[2:], following], axis=0)
-    position = lax.axis_index(EVERY) * share + jnp.arange(share, dtype=jnp.int32)
-    mismatch = jnp.where((position < width - 2)[:, None], state - target, jnp.float32(0.0))
+    reduced, mismatch = call(
+        lambda *refs: rollout_kernel(factor_scale, width, *refs),
+        "rollout",
+        (own, own),
+        [SMEM] + [VMEM] * 5,
+    )(place, parts, inverse, linear_op, pieces, offset[None, :])
     return (projection.T, reduced, mismatch)
 
 
 def solution(mesh):
+    slabs = mesh.shape["slab"]
+    split = Mesh(mesh.devices.reshape(-1, CORES, slabs), EVERY)
     whole = P(EVERY, None)
     return jax.shard_map(
         body,
-        mesh=mesh,
+        mesh=split,
         in_specs=(whole, P(), P(), P(), P()),
         out_specs=(whole, whole, whole),
         check_vma=False,

time: 82.1 us -> 79 us (0.962); the launches traced: 80.6 us -> 78.7 us
  local copies, waits for them, and re-layouts: 1.84 us -> 0.02 us
  Pallas kernels: 22.5 us -> 23.8 us
    unnamed x10 -> x8, local copies, waits for them, and re-layouts: 1.83 us -> 0.02 us
    all_to_all x1, waiting for transfers between devices: 5.17 us -> 6.81 us  [body(): parts = lax.all_to_all(parts, CHIPS, 0, 0, tiled=True)]
    ppermute x1, waiting for transfers between devices: 2.04 us -> 0.4 us  [body(): came = lax.ppermute(send, 'core', [(0, 1), (1, 0)])]
    pallas_call x4 -> x5, Pallas kernels: 15.7 us -> 16.9 us  [the longest x1 7.06 us: body(): call(factor_kernel, 'factor', (shape((RANK, rows), jnp.bfloat16), small),...]
    ppermute x1, starting transfers between devices: 1.28 us -> 0.35 us  [body(): came = lax.ppermute(send, 'core', [(0, 1), (1, 0)])]
  transfers between devices with their start and end apart: 2 -> 2, of which waited for: 2 -> 2; matrix products, arithmetic and copies ran while one was open for 0% -> 0% of each run, Pallas kernels for 11% -> 10%
where the time goes in v3:
time: 79 us; the launch traced here: 78.7 us
  blocking collectives  41.7 us (53%)
  Pallas kernels  23.8 us (30%)
  waiting for transfers between devices  7.21 us (9%)
  starting transfers between devices  5.27 us (7%)
    all_to_all x1, blocking collectives, body(): parts = lax.all_to_all(parts, EVERY, 0, 0, tiled=True)  24.3 us
    all_to_all x1, blocking collectives, body(): power = lax.all_to_all(spread, EVERY, 0, 0, tiled=True)  17.5 us
    pallas_call x1, Pallas kernels, body(): call(factor_kernel, 'factor', (shape((RANK, rows), jnp.bfloat16), small),...  7.06 us
    all_to_all x1, waiting for transfers between devices, body(): parts = lax.all_to_all(parts, CHIPS, 0, 0, tiled=True)  6.81 us
    pallas_call x1, Pallas kernels, body(): call(power_kernel, 'power', (tiles, shape((rows, width), jnp.bfloat16)),...  6.71 us
    pallas_call x1, Pallas kernels, body(): call(coords_kernel, 'coords', (packed, packed, shape((RANK, rows), f32)),...  4.94 us
    all_to_all x1, starting transfers between devices, body(): parts = lax.all_to_all(parts, CHIPS, 0, 0, tiled=True)  4.92 us
    pallas_call x1, Pallas kernels, body(): call(lambda *refs: rollout_kernel(factor_scale, width, *refs), 'rollout',...  2.98 us
  transfers between devices with their start and end apart: 2, of which 2 were waited for; matrix products, arithmetic and copies ran while one was open for 0% of the time, Pallas kernels for 10%

profile of v3, /device:TPU:0, one launch (start us, length us, event | category | flops | bytes accessed | tf_op | source)
XLA Modules:
  0.0 78.7 jit_solution(8816611624253392788)
XLA Ops:
  0.6 0.0 copy-start
  0.6 6.7 %power.1 = (f32[128,8,128]{2,1,0:T(8,128)S(1)}, bf16[2048,2048]{1,0:T(8,128)(2,1)S(1)}) custom-call(bf16[2048,2048]{1,0:T(8,128)(2,1)} %x_hbm.1, f32[64,2048]{1,0:T(8,128)} %bitcast.8), custom_call_target="tpu_custom_call" | custom-call | tf_op jit(solution)/shard_map/power/pallas_call | solution.py:238
  7.4 0.0 copy-start.2
  7.4 0.0 copy-start.3
  7.4 24.3 %all_to_all.15.parts_ref = f32[128,8,128]{2,1,0:T(8,128)S(1)} all-to-all(f32[128,8,128]{2,1,0:T(8,128)S(1)} %get-tuple-element.23), channel_id=1, replica_groups=mesh['yz'=16,'core'=2,'slab'=4] {'yz','core','slab'}, dimensions={0} | all-to-all | bytes 1048576 | tf_op jit(solution)/shard_map/all_to_all | solution.py:249
  31.6 0.2 spread.1
  31.8 17.5 %all_to_all.16.power_ref = f32[128,8,128]{2,1,0:T(8,128)S(1)} all-to-all(f32[128,8,128]{2,1,0:T(8,128)S(1)} %spread.1), channel_id=1, replica_groups=mesh['yz'=16,'core'=2,'slab'=4] {'yz','core','slab'}, dimensions={0} | all-to-all | bytes 1048576 | tf_op jit(solution)/shard_map/all_to_all | solution.py:251
  49.3 4.9 %coords.1 = (f32[16,40,128]{2,1,0:T(8,128)S(1)}, f32[16,40,128]{2,1,0:T(8,128)S(1)}, f32[64,2048]{1,0:T(8,128)S(1)}) custom-call(s32[1]{0:T(128)} %bitcast.core_ref, bf16[2048,2048]{1,0:T(8,128)(2,1)S(1)} %get-tuple-element.22.x_ref, f32[128,8,128]{2,1,0:T(8,128)S(1)} %all_to_all.16.power_ref), custom_call_target="tpu_custom_call" | custom-call | tf_op jit(solution)/shard_map/coords/pallas_call | solution.py:255
  54.2 0.0 copy-start.1
  54.3 0.4 collective-permute-start
  54.6 0.0 copy-done
  54.6 0.9 %prepare.1 = (f32[64,64]{1,0:T(8,128)S(1)}, bf16[192,4096]{1,0:T(8,128)(2,1)S(1)}) custom-call(f32[128,8,128]{2,1,0:T(8,128)S(1)} %all_to_all.16.power_ref, f32[64,4096]{1,0:T(8,128)S(1)} %bitcast.6), custom_call_target="tpu_custom_call" | custom-call | tf_op jit(solution)/shard_map/prepare/pallas_call | solution.py:263
  55.6 0.0 copy-done.1
  55.6 0.4 collective-permute-done.came_ref
  56.0 1.0 %pair.1 = f32[64,16,128]{2,1,0:T(8,128)} custom-call(f32[16,40,128]{2,1,0:T(8,128)S(1)} %get-tuple-element.31.keep_ref, f32[16,40,128]{2,1,0:T(8,128)S(1)} %collective-permute-done.came_ref), custom_call_target="tpu_custom_call" | custom-call | tf_op jit(solution)/shard_map/pair/pallas_call | solution.py:271
  57.0 4.9 %all-to-all-start.2 = ((f32[64,16,128]{2,1,0:T(8,128)}), f32[64,16,128]{2,1,0:T(8,128)S(1)}, u32[]{:S(2)}, u32[]{:S(2)}) async-start(f32[64,16,128]{2,1,0:T(8,128)} %pair.1), calls=%async_computation.2 | async-start | bytes 1048576 | tf_op jit(solution)/shard_map/all_to_all | solution.py:272
  61.9 7.1 %factor.1 = (bf16[64,2048]{1,0:T(8,128)(2,1)}, f32[64,64]{1,0:T(8,128)S(1)}) custom-call(f32[64,64]{1,0:T(8,128)S(1)} %get-tuple-element.27.corr_ref, f32[64,2048]{1,0:T(8,128)} %copy-done.1), custom_call_target="tpu_custom_call" | custom-call | tf_op jit(solution)/shard_map/factor/pallas_call | solution.py:273
  68.9 6.8 %all-to-all-done.2.refs_1_ = f32[64,16,128]{2,1,0:T(8,128)S(1)} async-done(((f32[64,16,128]{2,1,0:T(8,128)}), f32[64,16,128]{2,1,0:T(8,128)S(1)}, u32[]{:S(2)}, u32[]{:S(2)}) %all-to-all-start.2) | async-done | bytes 524320 | tf_op jit(solution)/shard_map/all_to_all | solution.py:272
  75.8 0.0 copy-done.2
  75.8 0.0 copy-done.3
  75.8 3.0 %rollout.1 = (f32[16,64]{1,0:T(8,128)}, f32[16,64]{1,0:T(8,128)}) custom-call(s32[1]{0:T(128)} %bitcast.1.refs_0_, f32[64,16,128]{2,1,0:T(8,128)S(1)} %all-to-all-done.2.refs_1_, f32[64,64]{1,0:T(8,128)S(1)} %get-tuple-element.33.refs_2_, f32[64,64]{1,0:T(8,128)S(1)} %copy-done.2, bf16[192,4096]{1,0:T(8,128)(2,1)S(1)} %get-tuple-element.34.refs_4_, ...), custom_call_target="tpu_custom_call" | custom-call | tf_op jit(solution)/shard_map/rollout/pallas_call | solution.py:281
Async XLA Ops:
  0.6 54.0 %copy-start = (f32[4096,64]{0,1:T(8,128)S(1)}, f32[4096,64]{0,1:T(8,128)}, u32[]{:S(2)}) copy-start(f32[4096,64]{0,1:T(8,128)} %param.8) | copy-start | bytes 3145732
  7.4 68.4 %copy-start.2 = (f32[64,64]{1,0:T(8,128)S(1)}, f32[64,64]{1,0:T(8,128)}, u32[]{:S(2)}) copy-start(f32[64,64]{1,0:T(8,128)} %refs_3_.1) | copy-start | bytes 49156
  7.4 68.4 %copy-start.3 = (f32[64]{0:T(128)S(1)}, f32[64]{0:T(128)}, u32[]{:S(2)}) copy-start(f32[64]{0:T(128)} %param.9) | copy-start | bytes 772
  54.2 1.3 %copy-start.1 = (f32[64,2048]{1,0:T(8,128)}, f32[64,2048]{1,0:T(8,128)S(1)}, u32[]{:S(2)}) copy-start(f32[64,2048]{1,0:T(8,128)S(1)} %get-tuple-element.28.modes_hbm) | copy-start | bytes 1572868
  54.3 1.7 %collective-permute-start = (f32[16,40,128]{2,1,0:T(8,128)S(1)}, f32[16,40,128]{2,1,0:T(8,128)S(1)}, u32[]{:S(2)}, u32[]{:S(2)}) collective-permute-start(f32[16,40,128]{2,1,0:T(8,128)S(1)} %get-tuple-element.24), channel_id=1, source_target_pairs={{0,4},{4,0},{1,5},{5,1},{2,6},{6,2},{3,7},{7,3},{8,12},{12,8},{9,1... | collective-permute-start | bytes 983048 | tf_op jit(solution)/shard_map/ppermute | solution.py:262
  57.0 18.8 %all-to-all-start.2 = ((f32[64,16,128]{2,1,0:T(8,128)}), f32[64,16,128]{2,1,0:T(8,128)S(1)}, u32[]{:S(2)}, u32[]{:S(2)}) async-start(f32[64,16,128]{2,1,0:T(8,128)} %pair.1), calls=%async_computation.2 | async-start | bytes 1048576 | tf_op jit(solution)/shard_map/all_to_all | solution.py:272

commit v4 on v3

--- a/solution.py
+++ b/solution.py
@@ -42,91 +42,128 @@
     return lax.dot_general(left, right, NT, preferred_element_type=jnp.float32)
 
 
-def passes(weights, block, ready, acc_ref, keep):
+def passes(inner, block, count, acc_ref):
     held = None
-    for i in range(CHUNKS):
-        ready(i)
-        inner = fold_rows(dot_nt(weights, block(i)))
+    for i in range(count):
+        value = inner(i)
         if held is not None:
             part = jnp.dot(held, block(i - 1), preferred_element_type=jnp.float32)
             acc_ref[...] = part if i == 1 else acc_ref[...] + part
-        keep(i, inner)
-        held = three(inner)
-    part = jnp.dot(held, block(CHUNKS - 1), preferred_element_type=jnp.float32)
+        held = three(value)
+    part = jnp.dot(held, block(count - 1), preferred_element_type=jnp.float32)
     return fold_rows(acc_ref[...] + part)
 
 
-def power_kernel(x_hbm, start_hbm, out_ref, x_ref, start_ref, acc_ref, sems):
-    rows = x_ref.shape[0] // CHUNKS
-    first = pltpu.make_async_copy(start_hbm, start_ref, sems.at[CHUNKS])
-    first.start()
-    copies = [
-        pltpu.make_async_copy(
-            x_hbm.at[pl.ds(i * rows, rows)], x_ref.at[pl.ds(i * rows, rows)], sems.at[i]
-        )
-        for i in range(CHUNKS)
-    ]
-    for copy in copies:
-        copy.start()
-    first.wait()
-    weights = three(start_ref[...])
-    power = passes(
-        weights,
-        lambda i: x_ref[pl.ds(i * rows, rows), :],
-        lambda i: copies[i].wait(),
-        acc_ref,
-        lambda i, inner: None,
-    )
-    wide = power.shape[1] // 128
+def put_tiles(out_ref, value):
+    wide = value.shape[1] // 128
     for i in range(out_ref.shape[0]):
         a, b = divmod(i, wide)
-        out_ref[i] = power[8 * a : 8 * a + 8, 128 * b : 128 * b + 128]
+        out_ref[i] = value[8 * a : 8 * a + 8, 128 * b : 128 * b + 128]
+
+
+def get_tiles(ref):
+    tall = RANK // 8
+    wide = ref.shape[0] // tall
+    rows = [
+        jnp.concatenate([ref[a * wide + b] for b in range(wide)], axis=1) for a in range(tall)
+    ]
+    return jnp.concatenate(rows, axis=0)
+
+
+def power_kernel(core_ref, x_hbm, start_hbm, send_ref, x_ref, inner_ref, start_ref, acc_ref, sems):
+    half = x_ref.shape[1] // CORES
+    rows = x_ref.shape[0] // CHUNKS
+    copies = []
+    for k in range(CORES):
+        source = pl.multiple_of(half * jnp.bitwise_xor(core_ref[0], k), half)
+        there, here = pl.ds(source, half), pl.ds(k * half, half)
+        copies.append(
+            [pltpu.make_async_copy(start_hbm.at[:, there], start_ref.at[:, here], sems.at[k, CHUNKS])]
+            + [
+                pltpu.make_async_copy(
+                    x_hbm.at[pl.ds(i * rows, rows), there],
+                    x_ref.at[pl.ds(i * rows, rows), here],
+                    sems.at[k, i],
+                )
+                for i in range(CHUNKS)
+            ]
+        )
+    for pair in zip(*copies):
+        for copy in pair:
+            copy.start()
+    for k in range(CORES):
+        copies[k][0].wait()
+    weights = three(start_ref[...])
+
+    def inner(i):
+        for k in range(CORES):
+            copies[k][i + 1].wait()
+        value = fold_rows(dot_nt(weights, x_ref[pl.ds(i * rows, rows), :]))
+        inner_ref[:, pl.ds(i * rows, rows)] = three(value)
+        return value
+
+    put_tiles(
+        send_ref,
+        passes(inner, lambda i: x_ref[pl.ds(i * rows, rows), half:], CHUNKS, acc_ref),
+    )
+
+
+def own_power_kernel(inner_ref, x_ref, keep_ref):
+    half = x_ref.shape[1] // CORES
+    put_tiles(
+        keep_ref,
+        fold_rows(jnp.dot(inner_ref[...], x_ref[:, :half], preferred_element_type=jnp.float32)),
+    )
+
+
+def add_kernel(keep_ref, came_ref, out_ref):
+    out_ref[...] = keep_ref[...] + came_ref[...]
 
 
 def spread_kernel(parts_ref, out_ref):
     out_ref[...] = jnp.broadcast_to(jnp.sum(parts_ref[...], axis=0)[None], out_ref.shape)
 
 
-def whole_power(power_ref):
-    tall = RANK // 8
-    wide = power_ref.shape[0] // tall
-    rows = [
-        jnp.concatenate([power_ref[a * wide + b] for b in range(wide)], axis=1)
-        for a in range(tall)
-    ]
-    return jnp.concatenate(rows, axis=0)
-
-
-def coords_kernel(core_ref, x_ref, power_ref, keep_ref, send_ref, modes_ref, acc_ref):
+def own_modes_kernel(x_ref, own_ref, modes_ref):
+    half = x_ref.shape[1] // CORES
+    modes_ref[...] = fold_rows(dot_nt(three(get_tiles(own_ref)), x_ref[:, :half]))
+
+
+def coords_kernel(core_ref, x_ref, own_modes_ref, other_ref, keep_ref, send_ref, modes_ref, acc_ref):
+    half = x_ref.shape[1] // CORES
     rows = x_ref.shape[0] // CHUNKS
-    weights = three(whole_power(power_ref))
-
-    def store(i, inner):
-        modes_ref[:, pl.ds(i * rows, rows)] = inner
-
-    coords = passes(
-        weights, lambda i: x_ref[pl.ds(i * rows, rows), :], lambda i: None, acc_ref, store
-    ).T
+    weights = three(get_tiles(other_ref))
+
+    def inner(i):
+        here = pl.ds(i * rows, rows)
+        value = own_modes_ref[:, here] + fold_rows(dot_nt(weights, x_ref[here, half:]))
+        modes_ref[:, here] = value
+        return value
+
+    coords = passes(inner, lambda i: x_ref[pl.ds(i * rows, rows), :], CHUNKS, acc_ref).T
+    first = core_ref[0] == 0
+    own, other = coords[:half], coords[half:]
+    coords = jnp.concatenate([jnp.where(first, own, other), jnp.where(first, other, own)], axis=0)
     groups, deep, _ = keep_ref.shape
     coords = coords.reshape(groups, coords.shape[0] // groups, RANK)
     after = jnp.concatenate([coords[1:, :8], coords[:1, :8]], axis=0)
     coords = jnp.concatenate([coords, after], axis=1)
-    half = deep - 8
+    span = deep - 8
     packed = [
         jnp.concatenate(
-            [coords[:, 2 * half * c : 2 * half * c + deep], coords[:, 2 * half * c + half :][:, :deep]],
+            [coords[:, 2 * span * c : 2 * span * c + deep], coords[:, 2 * span * c + span :][:, :deep]],
             axis=-1,
         )
         for c in range(CORES)
     ]
-    first = core_ref[0] == 0
     keep_ref[...] = jnp.where(first, packed[0], packed[1])
     send_ref[...] = jnp.where(first, packed[1], packed[0])
 
 
-def prepare_kernel(power_ref, quad_ref, corr_ref, pieces_ref):
+def prepare_kernel(own_ref, other_ref, quad_ref, corr_ref, pieces_ref):
     pieces_ref[...] = three(quad_ref[...])
-    weights = three(whole_power(power_ref))
+    power = jnp.concatenate([get_tiles(own_ref), get_tiles(other_ref)], axis=1)
+    weights = three(power)
     corr_ref[...] = fold_rows(fold_lanes(dot_nt(weights, weights)))
 
 
@@ -229,26 +266,38 @@
     share = width // devices
     f32 = jnp.float32
     shape = jax.ShapeDtypeStruct
-    tiles = shape((devices, RANK * share // 128, 128), f32)
+    chips = devices // CORES
+    tiles = shape((chips, RANK * share // 128, 128), f32)
     small = shape((RANK, RANK), f32)
     own = shape((share, RANK), f32)
-    acc = pltpu.VMEM((3 * RANK, width), f32)
     core, place = lax.axis_index("core")[None], lax.axis_index(EVERY)[None]
     start_block, core, place = lax.optimization_barrier((start_block, core, place))
-    parts, held = call(
+    send, held, inner = call(
         power_kernel,
         "power",
-        (tiles, shape((rows, width), jnp.bfloat16)),
-        [HBM, HBM],
+        (
+            tiles,
+            shape((rows, width), jnp.bfloat16),
+            shape((3 * RANK, rows), jnp.bfloat16),
+        ),
+        [SMEM, HBM, HBM],
         [
             pltpu.VMEM((RANK, width), f32),
-            acc,
-            pltpu.SemaphoreType.DMA((CHUNKS + 1,)),
+            pltpu.VMEM((3 * RANK, width // CORES), f32),
+            pltpu.SemaphoreType.DMA((CORES, CHUNKS + 1)),
         ],
-    )(in_hbm(snapshots), in_hbm(start_block.T))
-    parts = lax.all_to_all(parts, EVERY, 0, 0, tiled=True)
+    )(core, in_hbm(snapshots), in_hbm(start_block.T))
+    swap = [(0, 1), (1, 0)]
+    came = lax.ppermute(send, "core", swap)
+    keep = call(own_power_kernel, "own_power", tiles, [VMEM, VMEM])(inner, held)
+    parts = call(add_kernel, "add", tiles, [VMEM, VMEM])(keep, came)
+    parts = lax.all_to_all(parts, CHIPS, 0, 0, tiled=True)
     spread = call(spread_kernel, "spread", tiles, [VMEM])(parts)
-    power = lax.all_to_all(spread, EVERY, 0, 0, tiled=True)
+    mine = lax.all_to_all(spread, CHIPS, 0, 0, tiled=True)
+    theirs = lax.ppermute(mine, "core", swap)
+    own_modes = call(own_modes_kernel, "own_modes", shape((RANK, rows), f32), [VMEM, VMEM])(
+        held, mine
+    )
     groups = lax.axis_size("yz")
     deep = width // groups // CORES // 2 + 8
     packed = shape((groups, deep, 2 * RANK), f32)
@@ -256,18 +305,18 @@
         coords_kernel,
         "coords",
         (packed, packed, shape((RANK, rows), f32)),
-        [SMEM, VMEM, VMEM],
-        [acc],
-    )(core, held, power)
-    came = lax.ppermute(send, "core", [(0, 1), (1, 0)])
+        [SMEM, VMEM, VMEM, VMEM],
+        [pltpu.VMEM((3 * RANK, width), f32)],
+    )(core, held, own_modes, theirs)
+    came = lax.ppermute(send, "core", swap)
     correlation, pieces = call(
         prepare_kernel,
         "prepare",
         (small, shape((3 * RANK, RANK * RANK), jnp.bfloat16)),
-        [VMEM, VMEM],
-    )(power, quad_op.T)
+        [VMEM, VMEM, VMEM],
+    )(mine, theirs, quad_op.T)
     came, correlation, pieces = lax.optimization_barrier((came, correlation, pieces))
-    chunks = shape((devices // CORES, share, 2 * RANK), f32)
+    chunks = shape((chips, share, 2 * RANK), f32)
     parts = call(pair_kernel, "pair", chunks, [VMEM, VMEM])(keep, came)
     parts = lax.all_to_all(parts, CHIPS, 0, 0, tiled=True)
     projection, inverse = call(

time: 79 us -> 76 us (0.962)
  blocking collectives: 41.7 us -> 37.5 us
    all_to_all x2, blocking collectives: 41.7 us -> 37.5 us  [the longest x1 22.2 us: body(): parts = lax.all_to_all(parts, CHIPS, 0, 0, tiled=True)]
    pallas_call x1 -> x4, Pallas kernels: 6.71 us -> 8.36 us  [the longest x1 5.81 us: body(): call(power_kernel, 'power', (tiles, shape((rows, width), jnp.bfloat16), s...]
    pallas_call x1, Pallas kernels: 4.94 us -> 3.54 us  [body(): call(coords_kernel, 'coords', (packed, packed, shape((RANK, rows), f32)),...]
  transfers between devices with their start and end apart: 2 -> 4, of which waited for: 2 -> 3; matrix products, arithmetic and copies ran while one was open for 0% -> 0% of each run, Pallas kernels for 10% -> 14%
where the time goes in v4:
time: 76 us; the launch traced here: 75.7 us
  blocking collectives  37.5 us (49%)
  Pallas kernels  24 us (32%)
  waiting for transfers between devices  7.97 us (10%)
  starting transfers between devices  5.54 us (7%)
    all_to_all x1, blocking collectives, body(): parts = lax.all_to_all(parts, CHIPS, 0, 0, tiled=True)  22.2 us
    all_to_all x1, blocking collectives, body(): mine = lax.all_to_all(spread, CHIPS, 0, 0, tiled=True)  15.3 us
    all_to_all x1, waiting for transfers between devices, body(): parts = lax.all_to_all(parts, CHIPS, 0, 0, tiled=True)  7.14 us
    pallas_call x1, Pallas kernels, body(): call(factor_kernel, 'factor', (shape((RANK, rows), jnp.bfloat16), small),...  7.06 us
    pallas_call x1, Pallas kernels, body(): call(power_kernel, 'power', (tiles, shape((rows, width), jnp.bfloat16), s...  5.81 us
    all_to_all x1, starting transfers between devices, body(): parts = lax.all_to_all(parts, CHIPS, 0, 0, tiled=True)  4.88 us
    pallas_call x1, Pallas kernels, body(): call(coords_kernel, 'coords', (packed, packed, shape((RANK, rows), f32)),...  3.54 us
    pallas_call x1, Pallas kernels, body(): call(lambda *refs: rollout_kernel(factor_scale, width, *refs), 'rollout',...  2.98 us
  transfers between devices with their start and end apart: 4, of which 3 were waited for; matrix products, arithmetic and copies ran while one was open for 0% of the time, Pallas kernels for 14%

profile of v4, /device:TPU:0, one launch (start us, length us, event | category | flops | bytes accessed | tf_op | source)
XLA Modules:
  0.0 75.7 jit_solution(10966230195995812455)
XLA Ops:
  0.6 5.8 %power.1 = (f32[64,8,128]{2,1,0:T(8,128)S(1)}, bf16[2048,2048]{1,0:T(8,128)(2,1)S(1)}, bf16[192,2048]{1,0:T(8,128)(2,1)S(1)}) custom-call(s32[1]{0:T(128)} %bitcast.core_ref, bf16[2048,2048]{1,0:T(8,128)(2,1)} %x_hbm.1, f32[64,2048]{1,0:T(8,128)} %bitcast.8), custom_call_target="tpu_custom_call" | custom-call | tf_op jit(solution)/shard_map/power/pallas_call | solution.py:275
  6.5 0.1 collective-permute-start
  6.6 1.0 %own_power.1.keep_ref = f32[64,8,128]{2,1,0:T(8,128)S(1)} custom-call(bf16[192,2048]{1,0:T(8,128)(2,1)S(1)} %get-tuple-element.24.inner_ref, bf16[2048,2048]{1,0:T(8,128)(2,1)S(1)} %get-tuple-element.23.x_ref), custom_call_target="tpu_custom_call" | custom-call | tf_op jit(solution)/shard_map/own_power/pallas_call | solution.py:292
  7.6 0.5 collective-permute-done.came_ref
  8.1 22.2 %all_to_all.15.parts_ref = f32[64,8,128]{2,1,0:T(8,128)S(1)} all-to-all(f32[64,8,128]{2,1,0:T(8,128)S(1)} %add.9), channel_id=1, replica_groups=mesh['yz'=16,'core'=2,'slab'=4] {'yz','slab'}, dimensions={0} | all-to-all | bytes 524288 | tf_op jit(solution)/shard_map/all_to_all | solution.py:294
  30.3 0.1 spread.1
  30.4 15.3 %all_to_all.16.own_ref = f32[64,8,128]{2,1,0:T(8,128)S(1)} all-to-all(f32[64,8,128]{2,1,0:T(8,128)S(1)} %spread.1), channel_id=1, replica_groups=mesh['yz'=16,'core'=2,'slab'=4] {'yz','slab'}, dimensions={0} | all-to-all | bytes 524288 | tf_op jit(solution)/shard_map/all_to_all | solution.py:296
  45.7 0.0 copy-start
  45.7 0.0 collective-permute-start.1
  45.7 1.5 %own_modes.1.own_modes_ref = f32[64,2048]{1,0:T(8,128)S(1)} custom-call(bf16[2048,2048]{1,0:T(8,128)(2,1)S(1)} %get-tuple-element.23.x_ref, f32[64,8,128]{2,1,0:T(8,128)S(1)} %all_to_all.16.own_ref), custom_call_target="tpu_custom_call" | custom-call | tf_op jit(solution)/shard_map/own_modes/pallas_call | solution.py:298
  47.2 0.0 copy-start.2
  47.2 0.0 copy-start.3
  47.2 0.0 collective-permute-done.1.other_ref
  47.2 3.5 %coords.1 = (f32[16,40,128]{2,1,0:T(8,128)S(1)}, f32[16,40,128]{2,1,0:T(8,128)S(1)}, f32[64,2048]{1,0:T(8,128)S(1)}) custom-call(s32[1]{0:T(128)} %bitcast.core_ref, bf16[2048,2048]{1,0:T(8,128)(2,1)S(1)} %get-tuple-element.23.x_ref, f32[64,2048]{1,0:T(8,128)S(1)} %own_modes.1.own_modes_ref, f32[64,8,128]{2,1,0:T(8,128)S(1)} %collective-permute-done.1.other_ref), custom_call_target="tpu_custom_call" | custom-call | tf_op jit(solution)/shard_map/coords/pallas_call | solution.py:304
  50.8 0.0 copy-start.1
  50.8 0.6 collective-permute-start.2
  51.4 0.0 copy-done
  51.4 0.9 %prepare.1 = (f32[64,64]{1,0:T(8,128)S(1)}, bf16[192,4096]{1,0:T(8,128)(2,1)S(1)}) custom-call(f32[64,8,128]{2,1,0:T(8,128)S(1)} %all_to_all.16.own_ref, f32[64,8,128]{2,1,0:T(8,128)S(1)} %collective-permute-done.1.other_ref, f32[64,4096]{1,0:T(8,128)S(1)} %bitcast.6), custom_call_target="tpu_custom_call" | custom-call | tf_op jit(solution)/shard_map/prepare/pallas_call | solution.py:312
  52.3 0.0 copy-done.1
  52.3 0.3 collective-permute-done.2.came_ref
  52.6 1.0 %pair.1 = f32[64,16,128]{2,1,0:T(8,128)} custom-call(f32[16,40,128]{2,1,0:T(8,128)S(1)} %get-tuple-element.33.keep_ref, f32[16,40,128]{2,1,0:T(8,128)S(1)} %collective-permute-done.2.came_ref), custom_call_target="tpu_custom_call" | custom-call | tf_op jit(solution)/shard_map/pair/pallas_call | solution.py:320
  53.6 4.9 %all-to-all-start.2 = ((f32[64,16,128]{2,1,0:T(8,128)}), f32[64,16,128]{2,1,0:T(8,128)S(1)}, u32[]{:S(2)}, u32[]{:S(2)}) async-start(f32[64,16,128]{2,1,0:T(8,128)} %pair.1), calls=%async_computation.2 | async-start | bytes 1048576 | tf_op jit(solution)/shard_map/all_to_all | solution.py:321
  58.5 7.1 %factor.1 = (bf16[64,2048]{1,0:T(8,128)(2,1)}, f32[64,64]{1,0:T(8,128)S(1)}) custom-call(f32[64,64]{1,0:T(8,128)S(1)} %get-tuple-element.29.corr_ref, f32[64,2048]{1,0:T(8,128)} %copy-done.1), custom_call_target="tpu_custom_call" | custom-call | tf_op jit(solution)/shard_map/factor/pallas_call | solution.py:322
  65.6 7.1 %all-to-all-done.2.refs_1_ = f32[64,16,128]{2,1,0:T(8,128)S(1)} async-done(((f32[64,16,128]{2,1,0:T(8,128)}), f32[64,16,128]{2,1,0:T(8,128)S(1)}, u32[]{:S(2)}, u32[]{:S(2)}) %all-to-all-start.2) | async-done | bytes 524320 | tf_op jit(solution)/shard_map/all_to_all | solution.py:321
  72.7 0.0 copy-done.2
  72.7 0.0 copy-done.3
  72.7 3.0 %rollout.1 = (f32[16,64]{1,0:T(8,128)}, f32[16,64]{1,0:T(8,128)}) custom-call(s32[1]{0:T(128)} %bitcast.1.refs_0_, f32[64,16,128]{2,1,0:T(8,128)S(1)} %all-to-all-done.2.refs_1_, f32[64,64]{1,0:T(8,128)S(1)} %get-tuple-element.35.refs_2_, f32[64,64]{1,0:T(8,128)S(1)} %copy-done.2, bf16[192,4096]{1,0:T(8,128)(2,1)S(1)} %get-tuple-element.36.refs_4_, ...), custom_call_target="tpu_custom_call" | custom-call | tf_op jit(solution)/shard_map/rollout/pallas_call | solution.py:330
  (1 shorter events, 0.0 us)
Async XLA Ops:
  6.5 1.6 %collective-permute-start = (f32[64,8,128]{2,1,0:T(8,128)S(1)}, f32[64,8,128]{2,1,0:T(8,128)S(1)}, u32[]{:S(2)}, u32[]{:S(2)}) collective-permute-start(f32[64,8,128]{2,1,0:T(8,128)S(1)} %get-tuple-element.25), channel_id=1, source_target_pairs={{0,4},{4,0},{1,5},{5,1},{2,6},{6,2},{3,7},{7,3},{8,12},{12,8},{9,1... | collective-permute-start | bytes 786440 | tf_op jit(solution)/shard_map/ppermute | solution.py:291
  45.7 5.7 %copy-start = (f32[4096,64]{0,1:T(8,128)S(1)}, f32[4096,64]{0,1:T(8,128)}, u32[]{:S(2)}) copy-start(f32[4096,64]{0,1:T(8,128)} %param.8) | copy-start | bytes 3145732
  45.7 1.6 %collective-permute-start.1 = (f32[64,8,128]{2,1,0:T(8,128)S(1)}, f32[64,8,128]{2,1,0:T(8,128)S(1)}, u32[]{:S(2)}, u32[]{:S(2)}) collective-permute-start(f32[64,8,128]{2,1,0:T(8,128)S(1)} %all_to_all.16.own_ref), channel_id=1, source_target_pairs={{0,4},{4,0},{1,5},{5,1},{2,6},{6,2},{3,7},{7,3},{8,12},{12,8},{9,1... | collective-permute-start | bytes 786440 | tf_op jit(solution)/shard_map/ppermute | solution.py:297
  47.2 25.5 %copy-start.2 = (f32[64,64]{1,0:T(8,128)S(1)}, f32[64,64]{1,0:T(8,128)}, u32[]{:S(2)}) copy-start(f32[64,64]{1,0:T(8,128)} %refs_3_.1) | copy-start | bytes 49156
  47.2 25.5 %copy-start.3 = (f32[64]{0:T(128)S(1)}, f32[64]{0:T(128)}, u32[]{:S(2)}) copy-start(f32[64]{0:T(128)} %param.9) | copy-start | bytes 772
  50.8 1.5 %copy-start.1 = (f32[64,2048]{1,0:T(8,128)}, f32[64,2048]{1,0:T(8,128)S(1)}, u32[]{:S(2)}) copy-start(f32[64,2048]{1,0:T(8,128)S(1)} %get-tuple-element.30.modes_hbm) | copy-start | bytes 1572868
  50.8 1.8 %collective-permute-start.2 = (f32[16,40,128]{2,1,0:T(8,128)S(1)}, f32[16,40,128]{2,1,0:T(8,128)S(1)}, u32[]{:S(2)}, u32[]{:S(2)}) collective-permute-start(f32[16,40,128]{2,1,0:T(8,128)S(1)} %get-tuple-element.26), channel_id=1, source_target_pairs={{0,4},{4,0},{1,5},{5,1},{2,6},{6,2},{3,7},{7,3},{8,12},{12,8},{9,1... | collective-permute-start | bytes 983048 | tf_op jit(solution)/shard_map/ppermute | solution.py:311
  53.6 19.1 %all-to-all-start.2 = ((f32[64,16,128]{2,1,0:T(8,128)}), f32[64,16,128]{2,1,0:T(8,128)S(1)}, u32[]{:S(2)}, u32[]{:S(2)}) async-start(f32[64,16,128]{2,1,0:T(8,128)} %pair.1), calls=%async_computation.2 | async-start | bytes 1048576 | tf_op jit(solution)/shard_map/all_to_all | solution.py:321

commit v5 on v4

--- a/solution.py
+++ b/solution.py
@@ -13,6 +13,7 @@
 CORES = 2
 RANK = 64
 CHUNKS = 4
+PIECES = 2
 NT = (((1,), (1,)), ((), ()))
 LIMIT = pltpu.CompilerParams(vmem_limit_bytes=20 * 1024 * 1024)
 SMEM = pl.BlockSpec(memory_space=pltpu.SMEM)
@@ -20,22 +21,23 @@
 HBM = pl.BlockSpec(memory_space=pltpu.HBM)
 
 
-def three(value):
-    high = value.astype(jnp.bfloat16)
-    rest = value - high.astype(jnp.float32)
-    middle = rest.astype(jnp.bfloat16)
-    low = (rest - middle.astype(jnp.float32)).astype(jnp.bfloat16)
-    return jnp.concatenate([high, middle, low], axis=0)
-
-
-def fold_rows(value):
-    third = value.shape[0] // 3
-    return value[:third] + value[third : 2 * third] + value[2 * third :]
-
-
-def fold_lanes(value):
-    third = value.shape[1] // 3
-    return value[:, :third] + value[:, third : 2 * third] + value[:, 2 * third :]
+def pieces_of(value, count, axis=0):
+    pieces = []
+    for _ in range(count):
+        piece = value.astype(jnp.bfloat16)
+        pieces.append(piece)
+        value = value - piece.astype(jnp.float32)
+    return jnp.concatenate(pieces, axis=axis)
+
+
+def fold_rows(value, count):
+    part = value.shape[0] // count
+    return sum(value[i * part : (i + 1) * part] for i in range(count))
+
+
+def fold_lanes(value, count):
+    part = value.shape[1] // count
+    return sum(value[:, i * part : (i + 1) * part] for i in range(count))
 
 
 def dot_nt(left, right):
@@ -49,9 +51,9 @@
         if held is not None:
             part = jnp.dot(held, block(i - 1), preferred_element_type=jnp.float32)
             acc_ref[...] = part if i == 1 else acc_ref[...] + part
-        held = three(value)
+        held = pieces_of(value, PIECES)
     part = jnp.dot(held, block(count - 1), preferred_element_type=jnp.float32)
-    return fold_rows(acc_ref[...] + part)
+    return fold_rows(acc_ref[...] + part, PIECES)
 
 
 def put_tiles(out_ref, value):
@@ -93,13 +95,13 @@
             copy.start()
     for k in range(CORES):
         copies[k][0].wait()
-    weights = three(start_ref[...])
+    weights = pieces_of(start_ref[...], PIECES)
 
     def inner(i):
         for k in range(CORES):
             copies[k][i + 1].wait()
-        value = fold_rows(dot_nt(weights, x_ref[pl.ds(i * rows, rows), :]))
-        inner_ref[:, pl.ds(i * rows, rows)] = three(value)
+        value = fold_rows(dot_nt(weights, x_ref[pl.ds(i * rows, rows), :]), PIECES)
+        inner_ref[:, pl.ds(i * rows, rows)] = pieces_of(value, PIECES)
         return value
 
     put_tiles(
@@ -110,10 +112,8 @@
 
 def own_power_kernel(inner_ref, x_ref, keep_ref):
     half = x_ref.shape[1] // CORES
-    put_tiles(
-        keep_ref,
-        fold_rows(jnp.dot(inner_ref[...], x_ref[:, :half], preferred_element_type=jnp.float32)),
-    )
+    power = jnp.dot(inner_ref[...], x_ref[:, :half], preferred_element_type=jnp.float32)
+    put_tiles(keep_ref, fold_rows(power, PIECES))
 
 
 def add_kernel(keep_ref, came_ref, out_ref):
@@ -126,17 +126,19 @@
 
 def own_modes_kernel(x_ref, own_ref, modes_ref):
     half = x_ref.shape[1] // CORES
-    modes_ref[...] = fold_rows(dot_nt(three(get_tiles(own_ref)), x_ref[:, :half]))
+    weights = pieces_of(get_tiles(own_ref), PIECES)
+    modes_ref[...] = fold_rows(dot_nt(weights, x_ref[:, :half]), PIECES)
 
 
 def coords_kernel(core_ref, x_ref, own_modes_ref, other_ref, keep_ref, send_ref, modes_ref, acc_ref):
     half = x_ref.shape[1] // CORES
     rows = x_ref.shape[0] // CHUNKS
-    weights = three(get_tiles(other_ref))
+    weights = pieces_of(get_tiles(other_ref), PIECES)
 
     def inner(i):
         here = pl.ds(i * rows, rows)
-        value = own_modes_ref[:, here] + fold_rows(dot_nt(weights, x_ref[here, half:]))
+        value = fold_rows(dot_nt(weights, x_ref[here, half:]), PIECES)
+        value = own_modes_ref[:, here] + value
         modes_ref[:, here] = value
         return value
 
@@ -160,11 +162,10 @@
     send_ref[...] = jnp.where(first, packed[1], packed[0])
 
 
-def prepare_kernel(own_ref, other_ref, quad_ref, corr_ref, pieces_ref):
-    pieces_ref[...] = three(quad_ref[...])
+def correlation_kernel(own_ref, other_ref, corr_ref):
     power = jnp.concatenate([get_tiles(own_ref), get_tiles(other_ref)], axis=1)
-    weights = three(power)
-    corr_ref[...] = fold_rows(fold_lanes(dot_nt(weights, weights)))
+    pieces = pieces_of(power, 3)
+    corr_ref[...] = fold_rows(fold_lanes(dot_nt(pieces, pieces), 3), 3)
 
 
 def pair_kernel(keep_ref, came_ref, out_ref):
@@ -180,21 +181,45 @@
     out_ref[...] = jnp.stack(chunks, axis=1).reshape(out_ref.shape)
 
 
-def factor_kernel(corr_ref, modes_hbm, projection_ref, inverse_ref, modes_ref, sem):
-    fetch = pltpu.make_async_copy(modes_hbm, modes_ref, sem)
-    fetch.start()
+def spread_lane(line, k):
+    return jnp.broadcast_to(line[:, k : k + 1], line.shape)
+
+
+def factor_kernel(
+    corr_ref, modes_hbm, quad_hbm, projection_ref, inverse_ref, pieces_ref, modes_ref, quad_ref, sems
+):
+    quad_fetch = pltpu.make_async_copy(quad_hbm, quad_ref, sems.at[0])
+    modes_fetch = pltpu.make_async_copy(modes_hbm, modes_ref, sems.at[1])
+    quad_fetch.start()
+    modes_fetch.start()
     row = lax.broadcasted_iota(jnp.int32, (RANK, RANK), 0)
     column = lax.broadcasted_iota(jnp.int32, (RANK, RANK), 1)
     unit = jnp.where(row == column, jnp.float32(1.0), jnp.float32(0.0))
     work = jnp.concatenate([corr_ref[...], unit], axis=1)
     index = lax.broadcasted_iota(jnp.int32, (RANK, 1), 0)
-    for k in range(RANK):
-        line = work[k : k + 1, :]
-        pivot = line[:, k : k + 1]
-        inverse_ref[k : k + 1, :] = line[:, RANK:] * (1.0 / jnp.sqrt(pivot))
-        multiplier = jnp.where(index > k, work[:, k : k + 1], 0.0)
-        work = work - multiplier * (line * (1.0 / pivot))
-    fetch.wait()
+    top = 0
+    for k in range(0, RANK, 2):
+        first, second = work[k - top : k - top + 1], work[k - top + 1 : k - top + 2]
+        pivot, cross = spread_lane(first, k), spread_lane(first, k + 1)
+        inverse = 1.0 / pivot
+        ratio = cross * inverse
+        other = spread_lane(second, k + 1) - cross * ratio
+        second = second - ratio * first
+        inverse_ref[k : k + 1] = first[:, RANK:] * (1.0 / jnp.sqrt(pivot[:, RANK:]))
+        inverse_ref[k + 1 : k + 2] = second[:, RANK:] * (1.0 / jnp.sqrt(other[:, RANK:]))
+        if k + 2 == RANK:
+            break
+        place = (k + 2) // 8 * 8
+        work = work[place - top :]
+        top = place
+        below = index[top:] > k + 1
+        left = jnp.where(below, work[:, k : k + 1], 0.0)
+        right = jnp.where(below, work[:, k + 1 : k + 2], 0.0)
+        scaled = second * (1.0 / other)
+        work = work - (left * (first * inverse - ratio * scaled) + right * scaled)
+    quad_fetch.wait()
+    pieces_ref[...] = pieces_of(quad_ref[...], 3).T
+    modes_fetch.wait()
     modes = jnp.dot(
         inverse_ref[...],
         modes_ref[...],
@@ -232,7 +257,8 @@
             ],
             axis=1,
         )
-        quadratic = fold_rows(fold_lanes(dot_nt(three(pairs), pieces)))
+        quadratic = jnp.dot(pieces_of(pairs, 3), pieces, preferred_element_type=jnp.float32)
+        quadratic = fold_rows(fold_lanes(quadratic, 3), 3)
         linear = jnp.dot(
             state,
             linear_ref[...],
@@ -278,12 +304,12 @@
         (
             tiles,
             shape((rows, width), jnp.bfloat16),
-            shape((3 * RANK, rows), jnp.bfloat16),
+            shape((PIECES * RANK, rows), jnp.bfloat16),
         ),
         [SMEM, HBM, HBM],
         [
             pltpu.VMEM((RANK, width), f32),
-            pltpu.VMEM((3 * RANK, width // CORES), f32),
+            pltpu.VMEM((PIECES * RANK, width // CORES), f32),
             pltpu.SemaphoreType.DMA((CORES, CHUNKS + 1)),
         ],
     )(core, in_hbm(snapshots), in_hbm(start_block.T))
@@ -306,26 +332,29 @@
         "coords",
         (packed, packed, shape((RANK, rows), f32)),
         [SMEM, VMEM, VMEM, VMEM],
-        [pltpu.VMEM((3 * RANK, width), f32)],
+        [pltpu.VMEM((PIECES * RANK, width), f32)],
     )(core, held, own_modes, theirs)
     came = lax.ppermute(send, "core", swap)
-    correlation, pieces = call(
-        prepare_kernel,
-        "prepare",
-        (small, shape((3 * RANK, RANK * RANK), jnp.bfloat16)),
-        [VMEM, VMEM, VMEM],
-    )(mine, theirs, quad_op.T)
-    came, correlation, pieces = lax.optimization_barrier((came, correlation, pieces))
+    correlation = call(correlation_kernel, "correlation", small, [VMEM, VMEM])(mine, theirs)
+    came, correlation = lax.optimization_barrier((came, correlation))
     chunks = shape((chips, share, 2 * RANK), f32)
     parts = call(pair_kernel, "pair", chunks, [VMEM, VMEM])(keep, came)
     parts = lax.all_to_all(parts, CHIPS, 0, 0, tiled=True)
-    projection, inverse = call(
+    projection, inverse, pieces = call(
         factor_kernel,
         "factor",
-        (shape((RANK, rows), jnp.bfloat16), small),
-        [VMEM, HBM],
-        [pltpu.VMEM((RANK, rows), f32), pltpu.SemaphoreType.DMA(())],
-    )(correlation, in_hbm(modes))
+        (
+            shape((RANK, rows), jnp.bfloat16),
+            small,
+            shape((RANK * RANK, 3 * RANK), jnp.bfloat16),
+        ),
+        [VMEM, HBM, HBM],
+        [
+            pltpu.VMEM((RANK, rows), f32),
+            pltpu.VMEM((RANK, RANK * RANK), f32),
+            pltpu.SemaphoreType.DMA((2,)),
+        ],
+    )(correlation, in_hbm(modes), in_hbm(quad_op.T))
     factor_scale = math.sqrt(width) / (rows * devices)
     reduced, mismatch = call(
         lambda *refs: rollout_kernel(factor_scale, width, *refs),

time: 76 us -> 74.5 us (0.980)
  Pallas kernels: 24 us -> 20.3 us
  waiting for transfers between devices: 7.97 us -> 9.92 us
    pallas_call x2, Pallas kernels: 7.99 us -> 5.94 us  [the longest x1 5.49 us: body(): call(factor_kernel, 'factor', (shape((RANK, rows), jnp.bfloat16), small,...]
    all_to_all x1, waiting for transfers between devices: 7.14 us -> 8.35 us  [body(): parts = lax.all_to_all(parts, CHIPS, 0, 0, tiled=True)]
  transfers between devices with their start and end apart: 4 -> 4, of which waited for: 3 -> 3; matrix products, arithmetic and copies ran while one was open for 0% -> 0% of each run, Pallas kernels for 14% -> 11%
where the time goes in v5:
time: 74.5 us; the launch traced here: 74.2 us
  blocking collectives  37.5 us (50%)
  Pallas kernels  20.3 us (27%)
  waiting for transfers between devices  9.92 us (13%)
  starting transfers between devices  5.72 us (8%)
  between operations  0.75 us (1%)
    all_to_all x1, blocking collectives, body(): parts = lax.all_to_all(parts, CHIPS, 0, 0, tiled=True)  22.2 us
    all_to_all x1, blocking collectives, body(): mine = lax.all_to_all(spread, CHIPS, 0, 0, tiled=True)  15.3 us
    all_to_all x1, waiting for transfers between devices, body(): parts = lax.all_to_all(parts, CHIPS, 0, 0, tiled=True)  8.35 us
    pallas_call x1, Pallas kernels, body(): call(factor_kernel, 'factor', (shape((RANK, rows), jnp.bfloat16), small,...  5.49 us
    pallas_call x1, Pallas kernels, body(): call(power_kernel, 'power', (tiles, shape((rows, width), jnp.bfloat16), s...  5.47 us
    all_to_all x1, starting transfers between devices, body(): parts = lax.all_to_all(parts, CHIPS, 0, 0, tiled=True)  5.06 us
    pallas_call x1, Pallas kernels, body(): call(coords_kernel, 'coords', (packed, packed, shape((RANK, rows), f32)),...  3.07 us
    pallas_call x1, Pallas kernels, body(): call(lambda *refs: rollout_kernel(factor_scale, width, *refs), 'rollout',...  2.47 us
  transfers between devices with their start and end apart: 4, of which 3 were waited for; matrix products, arithmetic and copies ran while one was open for 0% of the time, Pallas kernels for 11%

profile of v5, /device:TPU:0, one launch (start us, length us, event | category | flops | bytes accessed | tf_op | source)
XLA Modules:
  0.0 74.2 jit_solution(7154292153578891960)
XLA Ops:
  0.6 5.5 %power.1 = (f32[64,8,128]{2,1,0:T(8,128)S(1)}, bf16[2048,2048]{1,0:T(8,128)(2,1)S(1)}, bf16[128,2048]{1,0:T(8,128)(2,1)S(1)}) custom-call(s32[1]{0:T(128)} %bitcast.core_ref, bf16[2048,2048]{1,0:T(8,128)(2,1)} %x_hbm.1, f32[64,2048]{1,0:T(8,128)} %bitcast.8), custom_call_target="tpu_custom_call" | custom-call | tf_op jit(solution)/shard_map/power/pallas_call | solution.py:301
  6.1 0.1 collective-permute-start
  6.2 0.7 own_power.1.keep_ref
  6.9 0.8 %collective-permute-done.came_ref = f32[64,8,128]{2,1,0:T(8,128)S(1)} collective-permute-done((f32[64,8,128]{2,1,0:T(8,128)S(1)}, f32[64,8,128]{2,1,0:T(8,128)S(1)}, u32[]{:S(2)}, u32[]{:S(2)}) %collective-permute-start) | collective-permute-done | bytes 262176 | tf_op jit(solution)/shard_map/ppermute | solution.py:317
  7.8 22.2 %all_to_all.15.parts_ref = f32[64,8,128]{2,1,0:T(8,128)S(1)} all-to-all(f32[64,8,128]{2,1,0:T(8,128)S(1)} %add.9), channel_id=1, replica_groups=mesh['yz'=16,'core'=2,'slab'=4] {'yz','slab'}, dimensions={0} | all-to-all | bytes 524288 | tf_op jit(solution)/shard_map/all_to_all | solution.py:320
  30.0 0.1 spread.1
  30.1 15.3 %all_to_all.16.own_ref = f32[64,8,128]{2,1,0:T(8,128)S(1)} all-to-all(f32[64,8,128]{2,1,0:T(8,128)S(1)} %spread.1), channel_id=1, replica_groups=mesh['yz'=16,'core'=2,'slab'=4] {'yz','slab'}, dimensions={0} | all-to-all | bytes 524288 | tf_op jit(solution)/shard_map/all_to_all | solution.py:322
  45.3 0.0 collective-permute-start.1
  45.3 1.5 %own_modes.1.own_modes_ref = f32[64,2048]{1,0:T(8,128)S(1)} custom-call(bf16[2048,2048]{1,0:T(8,128)(2,1)S(1)} %get-tuple-element.21.x_ref, f32[64,8,128]{2,1,0:T(8,128)S(1)} %all_to_all.16.own_ref), custom_call_target="tpu_custom_call" | custom-call | tf_op jit(solution)/shard_map/own_modes/pallas_call | solution.py:324
  46.8 0.0 copy-start.1
  46.9 0.0 copy-start.2
  46.9 0.0 collective-permute-done.1.other_ref
  46.9 3.1 %coords.1 = (f32[16,40,128]{2,1,0:T(8,128)S(1)}, f32[16,40,128]{2,1,0:T(8,128)S(1)}, f32[64,2048]{1,0:T(8,128)S(1)}) custom-call(s32[1]{0:T(128)} %bitcast.core_ref, bf16[2048,2048]{1,0:T(8,128)(2,1)S(1)} %get-tuple-element.21.x_ref, f32[64,2048]{1,0:T(8,128)S(1)} %own_modes.1.own_modes_ref, f32[64,8,128]{2,1,0:T(8,128)S(1)} %collective-permute-done.1.other_ref), custom_call_target="tpu_custom_call" | custom-call | tf_op jit(solution)/shard_map/coords/pallas_call | solution.py:330
  50.0 0.0 copy-start
  50.0 0.6 collective-permute-start.2
  50.5 0.5 correlation.1.corr_ref
  51.0 0.0 copy-done
  51.0 0.8 %collective-permute-done.2.came_ref = f32[16,40,128]{2,1,0:T(8,128)S(1)} collective-permute-done((f32[16,40,128]{2,1,0:T(8,128)S(1)}, f32[16,40,128]{2,1,0:T(8,128)S(1)}, u32[]{:S(2)}, u32[]{:S(2)}) %collective-permute-start.2) | collective-permute-done | bytes 327712 | tf_op jit(solution)/shard_map/ppermute | solution.py:337
  51.8 1.0 %pair.1 = f32[64,16,128]{2,1,0:T(8,128)} custom-call(f32[16,40,128]{2,1,0:T(8,128)S(1)} %get-tuple-element.29.keep_ref, f32[16,40,128]{2,1,0:T(8,128)S(1)} %collective-permute-done.2.came_ref), custom_call_target="tpu_custom_call" | custom-call | tf_op jit(solution)/shard_map/pair/pallas_call | solution.py:341
  52.8 5.1 %all-to-all-start.2 = ((f32[64,16,128]{2,1,0:T(8,128)}), f32[64,16,128]{2,1,0:T(8,128)S(1)}, u32[]{:S(2)}, u32[]{:S(2)}) async-start(f32[64,16,128]{2,1,0:T(8,128)} %pair.1), calls=%async_computation.2 | async-start | bytes 1048576 | tf_op jit(solution)/shard_map/all_to_all | solution.py:342
  57.9 5.5 %factor.1 = (bf16[64,2048]{1,0:T(8,128)(2,1)}, f32[64,64]{1,0:T(8,128)S(1)}, bf16[4096,192]{1,0:T(8,128)(2,1)S(1)}) custom-call(f32[64,64]{1,0:T(8,128)S(1)} %correlation.1.corr_ref, f32[64,2048]{1,0:T(8,128)} %copy-done, f32[64,4096]{1,0:T(8,128)} %bitcast.7), custom_call_target="tpu_custom_call" | custom-call | tf_op jit(solution)/shard_map/factor/pallas_call | solution.py:343
  63.4 8.3 %all-to-all-done.2.refs_1_ = f32[64,16,128]{2,1,0:T(8,128)S(1)} async-done(((f32[64,16,128]{2,1,0:T(8,128)}), f32[64,16,128]{2,1,0:T(8,128)S(1)}, u32[]{:S(2)}, u32[]{:S(2)}) %all-to-all-start.2) | async-done | bytes 524320 | tf_op jit(solution)/shard_map/all_to_all | solution.py:342
  71.7 0.0 copy-done.1
  71.7 0.0 copy-done.2
  71.7 2.5 %rollout.1 = (f32[16,64]{1,0:T(8,128)}, f32[16,64]{1,0:T(8,128)}) custom-call(s32[1]{0:T(128)} %bitcast.1.refs_0_, f32[64,16,128]{2,1,0:T(8,128)S(1)} %all-to-all-done.2.refs_1_, f32[64,64]{1,0:T(8,128)S(1)} %get-tuple-element.31.refs_2_, f32[64,64]{1,0:T(8,128)S(1)} %copy-done.1, bf16[4096,192]{1,0:T(8,128)(2,1)S(1)} %get-tuple-element.32.refs_4_, ...), custom_call_target="tpu_custom_call" | custom-call | tf_op jit(solution)/shard_map/rollout/pallas_call | solution.py:359
  (1 shorter events, 0.0 us)
Async XLA Ops:
  6.1 1.6 %collective-permute-start = (f32[64,8,128]{2,1,0:T(8,128)S(1)}, f32[64,8,128]{2,1,0:T(8,128)S(1)}, u32[]{:S(2)}, u32[]{:S(2)}) collective-permute-start(f32[64,8,128]{2,1,0:T(8,128)S(1)} %get-tuple-element.23), channel_id=1, source_target_pairs={{0,4},{4,0},{1,5},{5,1},{2,6},{6,2},{3,7},{7,3},{8,12},{12,8},{9,1... | collective-permute-start | bytes 786440 | tf_op jit(solution)/shard_map/ppermute | solution.py:317
  45.3 1.5 %collective-permute-start.1 = (f32[64,8,128]{2,1,0:T(8,128)S(1)}, f32[64,8,128]{2,1,0:T(8,128)S(1)}, u32[]{:S(2)}, u32[]{:S(2)}) collective-permute-start(f32[64,8,128]{2,1,0:T(8,128)S(1)} %all_to_all.16.own_ref), channel_id=1, source_target_pairs={{0,4},{4,0},{1,5},{5,1},{2,6},{6,2},{3,7},{7,3},{8,12},{12,8},{9,1... | collective-permute-start | bytes 786440 | tf_op jit(solution)/shard_map/ppermute | solution.py:323
  46.8 24.9 %copy-start.1 = (f32[64,64]{1,0:T(8,128)S(1)}, f32[64,64]{1,0:T(8,128)}, u32[]{:S(2)}) copy-start(f32[64,64]{1,0:T(8,128)} %refs_3_.1) | copy-start | bytes 49156
  46.9 24.9 %copy-start.2 = (f32[64]{0:T(128)S(1)}, f32[64]{0:T(128)}, u32[]{:S(2)}) copy-start(f32[64]{0:T(128)} %param.9) | copy-start | bytes 772
  50.0 1.1 %copy-start = (f32[64,2048]{1,0:T(8,128)}, f32[64,2048]{1,0:T(8,128)S(1)}, u32[]{:S(2)}) copy-start(f32[64,2048]{1,0:T(8,128)S(1)} %get-tuple-element.26.modes_hbm) | copy-start | bytes 1572868
  50.0 1.8 %collective-permute-start.2 = (f32[16,40,128]{2,1,0:T(8,128)S(1)}, f32[16,40,128]{2,1,0:T(8,128)S(1)}, u32[]{:S(2)}, u32[]{:S(2)}) collective-permute-start(f32[16,40,128]{2,1,0:T(8,128)S(1)} %get-tuple-element.24), channel_id=1, source_target_pairs={{0,4},{4,0},{1,5},{5,1},{2,6},{6,2},{3,7},{7,3},{8,12},{12,8},{9,1... | collective-permute-start | bytes 983048 | tf_op jit(solution)/shard_map/ppermute | solution.py:337
  52.8 18.9 %all-to-all-start.2 = ((f32[64,16,128]{2,1,0:T(8,128)}), f32[64,16,128]{2,1,0:T(8,128)S(1)}, u32[]{:S(2)}, u32[]{:S(2)}) async-start(f32[64,16,128]{2,1,0:T(8,128)} %pair.1), calls=%async_computation.2 | async-start | bytes 1048576 | tf_op jit(solution)/shard_map/all_to_all | solution.py:342

commit v6 on v5

--- a/solution.py
+++ b/solution.py
@@ -16,7 +16,6 @@
 PIECES = 2
 NT = (((1,), (1,)), ((), ()))
 LIMIT = pltpu.CompilerParams(vmem_limit_bytes=20 * 1024 * 1024)
-SMEM = pl.BlockSpec(memory_space=pltpu.SMEM)
 VMEM = pl.BlockSpec(memory_space=pltpu.VMEM)
 HBM = pl.BlockSpec(memory_space=pltpu.HBM)
 
@@ -72,12 +71,12 @@
     return jnp.concatenate(rows, axis=0)
 
 
-def power_kernel(core_ref, x_hbm, start_hbm, send_ref, x_ref, inner_ref, start_ref, acc_ref, sems):
+def power_kernel(x_hbm, start_hbm, send_ref, x_ref, inner_ref, start_ref, acc_ref, sems):
     half = x_ref.shape[1] // CORES
     rows = x_ref.shape[0] // CHUNKS
     copies = []
     for k in range(CORES):
-        source = pl.multiple_of(half * jnp.bitwise_xor(core_ref[0], k), half)
+        source = pl.multiple_of(half * jnp.bitwise_xor(lax.axis_index("core"), k), half)
         there, here = pl.ds(source, half), pl.ds(k * half, half)
         copies.append(
             [pltpu.make_async_copy(start_hbm.at[:, there], start_ref.at[:, here], sems.at[k, CHUNKS])]
@@ -127,10 +126,11 @@
 def own_modes_kernel(x_ref, own_ref, modes_ref):
     half = x_ref.shape[1] // CORES
     weights = pieces_of(get_tiles(own_ref), PIECES)
-    modes_ref[...] = fold_rows(dot_nt(weights, x_ref[:, :half]), PIECES)
-
-
-def coords_kernel(core_ref, x_ref, own_modes_ref, other_ref, keep_ref, send_ref, modes_ref, acc_ref):
+    modes = jnp.dot(x_ref[:, :half], weights.T, preferred_element_type=jnp.float32)
+    modes_ref[...] = fold_rows(modes.T, PIECES)
+
+
+def coords_kernel(x_ref, own_modes_ref, other_ref, keep_ref, send_ref, modes_ref, acc_ref):
     half = x_ref.shape[1] // CORES
     rows = x_ref.shape[0] // CHUNKS
     weights = pieces_of(get_tiles(other_ref), PIECES)
@@ -142,22 +142,15 @@
         modes_ref[:, here] = value
         return value
 
-    coords = passes(inner, lambda i: x_ref[pl.ds(i * rows, rows), :], CHUNKS, acc_ref).T
-    first = core_ref[0] == 0
-    own, other = coords[:half], coords[half:]
-    coords = jnp.concatenate([jnp.where(first, own, other), jnp.where(first, other, own)], axis=0)
+    coords = passes(inner, lambda i: x_ref[pl.ds(i * rows, rows), :], CHUNKS, acc_ref)
+    first = lax.axis_index("core") == 0
+    own, other = coords[:, :half], coords[:, half:]
+    coords = jnp.concatenate([jnp.where(first, own, other), jnp.where(first, other, own)], axis=1)
     groups, deep, _ = keep_ref.shape
-    coords = coords.reshape(groups, coords.shape[0] // groups, RANK)
-    after = jnp.concatenate([coords[1:, :8], coords[:1, :8]], axis=0)
-    coords = jnp.concatenate([coords, after], axis=1)
     span = deep - 8
-    packed = [
-        jnp.concatenate(
-            [coords[:, 2 * span * c : 2 * span * c + deep], coords[:, 2 * span * c + span :][:, :deep]],
-            axis=-1,
-        )
-        for c in range(CORES)
-    ]
+    later = jnp.concatenate([coords[:, span:], coords[:, :span]], axis=1)
+    coords = jnp.concatenate([coords, later], axis=0).T.reshape(groups, -1, 2 * RANK)
+    packed = [coords[:, 2 * span * c : 2 * span * c + deep] for c in range(CORES)]
     keep_ref[...] = jnp.where(first, packed[0], packed[1])
     send_ref[...] = jnp.where(first, packed[1], packed[0])
 
@@ -170,15 +163,19 @@
 
 def pair_kernel(keep_ref, came_ref, out_ref):
     total = keep_ref[...] + came_ref[...]
+    turned = pltpu.roll(total, RANK, axis=2)
+    left = lax.broadcasted_iota(jnp.int32, (1, 1, 2 * RANK), 2) < RANK
     groups = total.shape[0]
     chips, share, _ = out_ref.shape
     slabs = chips // groups
-    chunks = []
     for x in range(slabs):
         side, place = divmod(x * share, total.shape[1] - 8)
-        rows = total[:, place : place + share + 8, side * RANK : (side + 1) * RANK]
-        chunks.append(jnp.concatenate([rows[:, :share], rows[:, 2 : share + 2]], axis=-1))
-    out_ref[...] = jnp.stack(chunks, axis=1).reshape(out_ref.shape)
+        near, far = (total, turned) if side == 0 else (turned, total)
+        chunk = jnp.where(
+            left, near[:, place : place + share], far[:, place + 2 : place + share + 2]
+        )
+        for g in range(groups):
+            out_ref[slabs * g + x] = chunk[g]
 
 
 def spread_lane(line, k):
@@ -218,7 +215,7 @@
         scaled = second * (1.0 / other)
         work = work - (left * (first * inverse - ratio * scaled) + right * scaled)
     quad_fetch.wait()
-    pieces_ref[...] = pieces_of(quad_ref[...], 3).T
+    pieces_ref[...] = pieces_of(quad_ref[...], PIECES).T
     modes_fetch.wait()
     modes = jnp.dot(
         inverse_ref[...],
@@ -230,7 +227,7 @@
 
 
 def rollout_kernel(
-    scale, width, place_ref, parts_ref, inverse_ref, linear_ref, pieces_ref, offset_ref,
+    scale, width, parts_ref, inverse_ref, linear_ref, pieces_ref, offset_ref,
     reduced_ref, mismatch_ref,
 ):
     packed = jnp.sum(parts_ref[...], axis=0)
@@ -257,8 +254,10 @@
             ],
             axis=1,
         )
-        quadratic = jnp.dot(pieces_of(pairs, 3), pieces, preferred_element_type=jnp.float32)
-        quadratic = fold_rows(fold_lanes(quadratic, 3), 3)
+        quadratic = jnp.dot(
+            pieces_of(pairs, PIECES), pieces, preferred_element_type=jnp.float32
+        )
+        quadratic = fold_rows(fold_lanes(quadratic, PIECES), PIECES)
         linear = jnp.dot(
             state,
             linear_ref[...],
@@ -266,7 +265,7 @@
             preferred_element_type=jnp.float32,
         )
         state = state + 0.25 * (linear + quadratic + offset_ref[...])
-    position = place_ref[0] * share + lax.broadcasted_iota(jnp.int32, (share, 1), 0)
+    position = lax.axis_index(EVERY) * share + lax.broadcasted_iota(jnp.int32, (share, 1), 0)
     mismatch_ref[...] = jnp.where(position < width - 2, state - target, jnp.float32(0.0))
 
 
@@ -296,8 +295,6 @@
     tiles = shape((chips, RANK * share // 128, 128), f32)
     small = shape((RANK, RANK), f32)
     own = shape((share, RANK), f32)
-    core, place = lax.axis_index("core")[None], lax.axis_index(EVERY)[None]
-    start_block, core, place = lax.optimization_barrier((start_block, core, place))
     send, held, inner = call(
         power_kernel,
         "power",
@@ -306,13 +303,13 @@
             shape((rows, width), jnp.bfloat16),
             shape((PIECES * RANK, rows), jnp.bfloat16),
         ),
-        [SMEM, HBM, HBM],
+        [HBM, HBM],
         [
             pltpu.VMEM((RANK, width), f32),
             pltpu.VMEM((PIECES * RANK, width // CORES), f32),
             pltpu.SemaphoreType.DMA((CORES, CHUNKS + 1)),
         ],
-    )(core, in_hbm(snapshots), in_hbm(start_block.T))
+    )(in_hbm(snapshots), in_hbm(start_block.T))
     swap = [(0, 1), (1, 0)]
     came = lax.ppermute(send, "core", swap)
     keep = call(own_power_kernel, "own_power", tiles, [VMEM, VMEM])(inner, held)
@@ -331,9 +328,9 @@
         coords_kernel,
         "coords",
         (packed, packed, shape((RANK, rows), f32)),
-        [SMEM, VMEM, VMEM, VMEM],
+        [VMEM, VMEM, VMEM],
         [pltpu.VMEM((PIECES * RANK, width), f32)],
-    )(core, held, own_modes, theirs)
+    )(held, own_modes, theirs)
     came = lax.ppermute(send, "core", swap)
     correlation = call(correlation_kernel, "correlation", small, [VMEM, VMEM])(mine, theirs)
     came, correlation = lax.optimization_barrier((came, correlation))
@@ -346,7 +343,7 @@
         (
             shape((RANK, rows), jnp.bfloat16),
             small,
-            shape((RANK * RANK, 3 * RANK), jnp.bfloat16),
+            shape((RANK * RANK, PIECES * RANK), jnp.bfloat16),
         ),
         [VMEM, HBM, HBM],
         [
@@ -360,8 +357,8 @@
         lambda *refs: rollout_kernel(factor_scale, width, *refs),
         "rollout",
         (own, own),
-        [SMEM] + [VMEM] * 5,
-    )(place, parts, inverse, linear_op, pieces, offset[None, :])
+        [VMEM] * 5,
+    )(parts, inverse, linear_op, pieces, offset[None, :])
     return (projection.T, reduced, mismatch)
 
 

time: 74.5 us -> 73.6 us (0.988)
  Pallas kernels: 20.3 us -> 19.2 us
  transfers between devices with their start and end apart: 4 -> 4, of which waited for: 3 -> 4; matrix products, arithmetic and copies ran while one was open for 0% -> 0% of each run, Pallas kernels for 11% -> 10%
where the time goes in v6:
time: 73.6 us; the launch traced here: 73.4 us
  blocking collectives  37.5 us (51%)
  Pallas kernels  19.2 us (26%)
  waiting for transfers between devices  10.4 us (14%)
  starting transfers between devices  5.58 us (8%)
    all_to_all x1, blocking collectives, body(): parts = lax.all_to_all(parts, CHIPS, 0, 0, tiled=True)  22.2 us
    all_to_all x1, blocking collectives, body(): mine = lax.all_to_all(spread, CHIPS, 0, 0, tiled=True)  15.3 us
    all_to_all x1, waiting for transfers between devices, body(): parts = lax.all_to_all(parts, CHIPS, 0, 0, tiled=True)  8.62 us
    pallas_call x1, Pallas kernels, body(): call(power_kernel, 'power', (tiles, shape((rows, width), jnp.bfloat16), s...  5.46 us
    pallas_call x1, Pallas kernels, body(): call(factor_kernel, 'factor', (shape((RANK, rows), jnp.bfloat16), small,...  5.19 us
    all_to_all x1, starting transfers between devices, body(): parts = lax.all_to_all(parts, CHIPS, 0, 0, tiled=True)  5.06 us
    pallas_call x1, Pallas kernels, body(): call(coords_kernel, 'coords', (packed, packed, shape((RANK, rows), f32)),...  3.05 us
    pallas_call x1, Pallas kernels, body(): call(lambda *refs: rollout_kernel(factor_scale, width, *refs), 'rollout',...  1.91 us
  transfers between devices with their start and end apart: 4, of which 4 were waited for; matrix products, arithmetic and copies ran while one was open for 0% of the time, Pallas kernels for 10%

profile of v6, /device:TPU:0, one launch (start us, length us, event | category | flops | bytes accessed | tf_op | source)
XLA Modules:
  0.0 73.4 jit_solution(4660686794792068760)
XLA Ops:
  0.6 5.5 %power.1 = (f32[64,8,128]{2,1,0:T(8,128)S(1)}, bf16[2048,2048]{1,0:T(8,128)(2,1)S(1)}, bf16[128,2048]{1,0:T(8,128)(2,1)S(1)}) custom-call(bf16[2048,2048]{1,0:T(8,128)(2,1)} %x_hbm.1, f32[64,2048]{1,0:T(8,128)} %bitcast.6), custom_call_target="tpu_custom_call" | custom-call | tf_op jit(solution)/shard_map/power/pallas_call | solution.py:298
  6.1 0.1 collective-permute-start
  6.2 0.7 own_power.1.keep_ref
  6.9 0.8 %collective-permute-done.came_ref = f32[64,8,128]{2,1,0:T(8,128)S(1)} collective-permute-done((f32[64,8,128]{2,1,0:T(8,128)S(1)}, f32[64,8,128]{2,1,0:T(8,128)S(1)}, u32[]{:S(2)}, u32[]{:S(2)}) %collective-permute-start) | collective-permute-done | bytes 262176 | tf_op jit(solution)/shard_map/ppermute | solution.py:314
  7.7 22.2 %all_to_all.15.parts_ref = f32[64,8,128]{2,1,0:T(8,128)S(1)} all-to-all(f32[64,8,128]{2,1,0:T(8,128)S(1)} %add.1), channel_id=1, replica_groups=mesh['yz'=16,'core'=2,'slab'=4] {'yz','slab'}, dimensions={0} | all-to-all | bytes 524288 | tf_op jit(solution)/shard_map/all_to_all | solution.py:317
  29.9 0.1 spread.1
  30.0 15.3 %all_to_all.16.own_ref = f32[64,8,128]{2,1,0:T(8,128)S(1)} all-to-all(f32[64,8,128]{2,1,0:T(8,128)S(1)} %spread.1), channel_id=1, replica_groups=mesh['yz'=16,'core'=2,'slab'=4] {'yz','slab'}, dimensions={0} | all-to-all | bytes 524288 | tf_op jit(solution)/shard_map/all_to_all | solution.py:319
  45.3 0.0 collective-permute-start.1
  45.3 1.3 %own_modes.1.own_modes_ref = f32[64,2048]{1,0:T(8,128)S(1)} custom-call(bf16[2048,2048]{1,0:T(8,128)(2,1)S(1)} %get-tuple-element.16.x_ref, f32[64,8,128]{2,1,0:T(8,128)S(1)} %all_to_all.16.own_ref), custom_call_target="tpu_custom_call" | custom-call | tf_op jit(solution)/shard_map/own_modes/pallas_call | solution.py:321
  46.6 0.0 copy-start.1
  46.6 0.0 copy-start.2
  46.7 0.2 collective-permute-done.1.other_ref
  46.8 3.1 %coords.1 = (f32[16,40,128]{2,1,0:T(8,128)S(1)}, f32[16,40,128]{2,1,0:T(8,128)S(1)}, f32[64,2048]{1,0:T(8,128)S(1)}) custom-call(bf16[2048,2048]{1,0:T(8,128)(2,1)S(1)} %get-tuple-element.16.x_ref, f32[64,2048]{1,0:T(8,128)S(1)} %own_modes.1.own_modes_ref, f32[64,8,128]{2,1,0:T(8,128)S(1)} %collective-permute-done.1.other_ref), custom_call_target="tpu_custom_call" | custom-call | tf_op jit(solution)/shard_map/coords/pallas_call | solution.py:327
  49.9 0.0 copy-start
  49.9 0.4 collective-permute-start.2
  50.3 0.5 correlation.1.corr_ref
  50.8 0.0 copy-done
  50.8 0.8 %collective-permute-done.2.came_ref = f32[16,40,128]{2,1,0:T(8,128)S(1)} collective-permute-done((f32[16,40,128]{2,1,0:T(8,128)S(1)}, f32[16,40,128]{2,1,0:T(8,128)S(1)}, u32[]{:S(2)}, u32[]{:S(2)}) %collective-permute-start.2) | collective-permute-done | bytes 327712 | tf_op jit(solution)/shard_map/ppermute | solution.py:334
  51.6 0.9 %pair.1 = f32[64,16,128]{2,1,0:T(8,128)} custom-call(f32[16,40,128]{2,1,0:T(8,128)S(1)} %get-tuple-element.23.keep_ref, f32[16,40,128]{2,1,0:T(8,128)S(1)} %collective-permute-done.2.came_ref), custom_call_target="tpu_custom_call" | custom-call | tf_op jit(solution)/shard_map/pair/pallas_call | solution.py:338
  52.6 5.1 %all-to-all-start.2 = ((f32[64,16,128]{2,1,0:T(8,128)}), f32[64,16,128]{2,1,0:T(8,128)S(1)}, u32[]{:S(2)}, u32[]{:S(2)}) async-start(f32[64,16,128]{2,1,0:T(8,128)} %pair.1), calls=%async_computation.2 | async-start | bytes 1048576 | tf_op jit(solution)/shard_map/all_to_all | solution.py:339
  57.6 5.2 %factor.1 = (bf16[64,2048]{1,0:T(8,128)(2,1)}, f32[64,64]{1,0:T(8,128)S(1)}, bf16[4096,128]{1,0:T(8,128)(2,1)S(1)}) custom-call(f32[64,64]{1,0:T(8,128)S(1)} %correlation.1.corr_ref, f32[64,2048]{1,0:T(8,128)} %copy-done, f32[64,4096]{1,0:T(8,128)} %bitcast.5), custom_call_target="tpu_custom_call" | custom-call | tf_op jit(solution)/shard_map/factor/pallas_call | solution.py:340
  62.8 8.6 %all-to-all-done.2.refs_0_ = f32[64,16,128]{2,1,0:T(8,128)S(1)} async-done(((f32[64,16,128]{2,1,0:T(8,128)}), f32[64,16,128]{2,1,0:T(8,128)S(1)}, u32[]{:S(2)}, u32[]{:S(2)}) %all-to-all-start.2) | async-done | bytes 524320 | tf_op jit(solution)/shard_map/all_to_all | solution.py:339
  71.4 0.0 copy-done.1
  71.4 0.0 copy-done.2
  71.4 1.9 %rollout.1 = (f32[16,64]{1,0:T(8,128)}, f32[16,64]{1,0:T(8,128)}) custom-call(f32[64,16,128]{2,1,0:T(8,128)S(1)} %all-to-all-done.2.refs_0_, f32[64,64]{1,0:T(8,128)S(1)} %get-tuple-element.25.refs_1_, f32[64,64]{1,0:T(8,128)S(1)} %copy-done.1, bf16[4096,128]{1,0:T(8,128)(2,1)S(1)} %get-tuple-element.26.refs_3_, f32[1,64]{1,0:T(1,128)S(1)} %bitcast.4), custom_call_target="tpu_custom_call" | custom-call | tf_op jit(solution)/shard_map/rollout/pallas_call | solution.py:356
  (1 shorter events, 0.0 us)
Async XLA Ops:
  6.1 1.6 %collective-permute-start = (f32[64,8,128]{2,1,0:T(8,128)S(1)}, f32[64,8,128]{2,1,0:T(8,128)S(1)}, u32[]{:S(2)}, u32[]{:S(2)}) collective-permute-start(f32[64,8,128]{2,1,0:T(8,128)S(1)} %get-tuple-element.18), channel_id=1, source_target_pairs={{0,4},{4,0},{1,5},{5,1},{2,6},{6,2},{3,7},{7,3},{8,12},{12,8},{9,1... | collective-permute-start | bytes 786440 | tf_op jit(solution)/shard_map/ppermute | solution.py:314
  45.3 1.5 %collective-permute-start.1 = (f32[64,8,128]{2,1,0:T(8,128)S(1)}, f32[64,8,128]{2,1,0:T(8,128)S(1)}, u32[]{:S(2)}, u32[]{:S(2)}) collective-permute-start(f32[64,8,128]{2,1,0:T(8,128)S(1)} %all_to_all.16.own_ref), channel_id=1, source_target_pairs={{0,4},{4,0},{1,5},{5,1},{2,6},{6,2},{3,7},{7,3},{8,12},{12,8},{9,1... | collective-permute-start | bytes 786440 | tf_op jit(solution)/shard_map/ppermute | solution.py:320
  46.6 24.8 %copy-start.1 = (f32[64,64]{1,0:T(8,128)S(1)}, f32[64,64]{1,0:T(8,128)}, u32[]{:S(2)}) copy-start(f32[64,64]{1,0:T(8,128)} %refs_2_.1) | copy-start | bytes 49156
  46.6 24.8 %copy-start.2 = (f32[64]{0:T(128)S(1)}, f32[64]{0:T(128)}, u32[]{:S(2)}) copy-start(f32[64]{0:T(128)} %param.9) | copy-start | bytes 772
  49.9 0.9 %copy-start = (f32[64,2048]{1,0:T(8,128)}, f32[64,2048]{1,0:T(8,128)S(1)}, u32[]{:S(2)}) copy-start(f32[64,2048]{1,0:T(8,128)S(1)} %get-tuple-element.21.modes_hbm) | copy-start | bytes 1572868
  49.9 1.7 %collective-permute-start.2 = (f32[16,40,128]{2,1,0:T(8,128)S(1)}, f32[16,40,128]{2,1,0:T(8,128)S(1)}, u32[]{:S(2)}, u32[]{:S(2)}) collective-permute-start(f32[16,40,128]{2,1,0:T(8,128)S(1)} %get-tuple-element.19), channel_id=1, source_target_pairs={{0,4},{4,0},{1,5},{5,1},{2,6},{6,2},{3,7},{7,3},{8,12},{12,8},{9,1... | collective-permute-start | bytes 983048 | tf_op jit(solution)/shard_map/ppermute | solution.py:334
  52.6 18.9 %all-to-all-start.2 = ((f32[64,16,128]{2,1,0:T(8,128)}), f32[64,16,128]{2,1,0:T(8,128)S(1)}, u32[]{:S(2)}, u32[]{:S(2)}) async-start(f32[64,16,128]{2,1,0:T(8,128)} %pair.1), calls=%async_computation.2 | async-start | bytes 1048576 | tf_op jit(solution)/shard_map/all_to_all | solution.py:339

commit v7 on v6

--- a/solution.py
+++ b/solution.py
@@ -13,6 +13,7 @@
 CORES = 2
 RANK = 64
 CHUNKS = 4
+BLOCKS = 2
 PIECES = 2
 NT = (((1,), (1,)), ((), ()))
 LIMIT = pltpu.CompilerParams(vmem_limit_bytes=20 * 1024 * 1024)
@@ -132,17 +133,18 @@
 
 def coords_kernel(x_ref, own_modes_ref, other_ref, keep_ref, send_ref, modes_ref, acc_ref):
     half = x_ref.shape[1] // CORES
-    rows = x_ref.shape[0] // CHUNKS
-    weights = pieces_of(get_tiles(other_ref), PIECES)
+    rows = x_ref.shape[0] // BLOCKS
+    weights = pieces_of(get_tiles(other_ref), PIECES).T
 
     def inner(i):
         here = pl.ds(i * rows, rows)
-        value = fold_rows(dot_nt(weights, x_ref[here, half:]), PIECES)
+        value = jnp.dot(x_ref[here, half:], weights, preferred_element_type=jnp.float32)
+        value = fold_rows(value.T, PIECES)
         value = own_modes_ref[:, here] + value
         modes_ref[:, here] = value
         return value
 
-    coords = passes(inner, lambda i: x_ref[pl.ds(i * rows, rows), :], CHUNKS, acc_ref)
+    coords = passes(inner, lambda i: x_ref[pl.ds(i * rows, rows), :], BLOCKS, acc_ref)
     first = lax.axis_index("core") == 0
     own, other = coords[:, :half], coords[:, half:]
     coords = jnp.concatenate([jnp.where(first, own, other), jnp.where(first, other, own)], axis=1)
@@ -166,16 +168,19 @@
     turned = pltpu.roll(total, RANK, axis=2)
     left = lax.broadcasted_iota(jnp.int32, (1, 1, 2 * RANK), 2) < RANK
     groups = total.shape[0]
-    chips, share, _ = out_ref.shape
+    chips, pairs = out_ref.shape[:2]
     slabs = chips // groups
+    share = 4 * pairs - 4
     for x in range(slabs):
         side, place = divmod(x * share, total.shape[1] - 8)
         near, far = (total, turned) if side == 0 else (turned, total)
+        middle = place + share // 2
         chunk = jnp.where(
-            left, near[:, place : place + share], far[:, place + 2 : place + share + 2]
+            left, near[:, place : place + 2 * pairs], far[:, middle : middle + 2 * pairs]
         )
         for g in range(groups):
-            out_ref[slabs * g + x] = chunk[g]
+            for i in range(pairs):
+                out_ref[slabs * g + x, i] = chunk[g, 2 * i : 2 * i + 2]
 
 
 def spread_lane(line, k):
@@ -231,8 +236,13 @@
     reduced_ref, mismatch_ref,
 ):
     packed = jnp.sum(parts_ref[...], axis=0)
-    share = packed.shape[0]
-    coords = jnp.concatenate([packed[:, :RANK], packed[:, RANK:]], axis=0)
+    packed = jnp.concatenate([packed[i] for i in range(packed.shape[0])], axis=0)
+    sides = packed[:, :RANK], packed[:, RANK:]
+    share = reduced_ref.shape[0]
+    half = share // 2
+    coords = jnp.concatenate(
+        [side[:half] for side in sides] + [side[2 : half + 2] for side in sides], axis=0
+    )
     coords = scale * lax.dot_general(
         coords,
         inverse_ref[...],
@@ -334,7 +344,7 @@
     came = lax.ppermute(send, "core", swap)
     correlation = call(correlation_kernel, "correlation", small, [VMEM, VMEM])(mine, theirs)
     came, correlation = lax.optimization_barrier((came, correlation))
-    chunks = shape((chips, share, 2 * RANK), f32)
+    chunks = shape((chips, share // 4 + 1, 2, 2 * RANK), f32)
     parts = call(pair_kernel, "pair", chunks, [VMEM, VMEM])(keep, came)
     parts = lax.all_to_all(parts, CHIPS, 0, 0, tiled=True)
     projection, inverse, pieces = call(

time: 73.6 us -> 71.3 us (0.969)
  waiting for transfers between devices: 10.4 us -> 8.27 us
    all_to_all x1, waiting for transfers between devices: 8.62 us -> 6.48 us  [body(): parts = lax.all_to_all(parts, CHIPS, 0, 0, tiled=True)]
  transfers between devices with their start and end apart: 4 -> 4, of which waited for: 4 -> 4; matrix products, arithmetic and copies ran while one was open for 0% -> 0% of each run, Pallas kernels for 10% -> 11%
where the time goes in v7:
time: 71.3 us; the launch traced here: 71 us
  blocking collectives  37.5 us (53%)
  Pallas kernels  19 us (27%)
  waiting for transfers between devices  8.27 us (12%)
  starting transfers between devices  5.54 us (8%)
  between operations  0.73 us (1%)
    all_to_all x1, blocking collectives, body(): parts = lax.all_to_all(parts, CHIPS, 0, 0, tiled=True)  22.2 us
    all_to_all x1, blocking collectives, body(): mine = lax.all_to_all(spread, CHIPS, 0, 0, tiled=True)  15.3 us
    all_to_all x1, waiting for transfers between devices, body(): parts = lax.all_to_all(parts, CHIPS, 0, 0, tiled=True)  6.48 us
    pallas_call x1, Pallas kernels, body(): call(power_kernel, 'power', (tiles, shape((rows, width), jnp.bfloat16), s...  5.46 us
    pallas_call x1, Pallas kernels, body(): call(factor_kernel, 'factor', (shape((RANK, rows), jnp.bfloat16), small,...  5.2 us
    all_to_all x1, starting transfers between devices, body(): parts = lax.all_to_all(parts, CHIPS, 0, 0, tiled=True)  5.04 us
    pallas_call x1, Pallas kernels, body(): call(coords_kernel, 'coords', (packed, packed, shape((RANK, rows), f32)),...  2.87 us
    pallas_call x1, Pallas kernels, body(): call(lambda *refs: rollout_kernel(factor_scale, width, *refs), 'rollout',...  1.99 us
  transfers between devices with their start and end apart: 4, of which 4 were waited for; matrix products, arithmetic and copies ran while one was open for 0% of the time, Pallas kernels for 11%

profile of v7, /device:TPU:0, one launch (start us, length us, event | category | flops | bytes accessed | tf_op | source)
XLA Modules:
  0.0 71.0 jit_solution(9245939685415350441)
XLA Ops:
  0.6 5.5 %power.1 = (f32[64,8,128]{2,1,0:T(8,128)S(1)}, bf16[2048,2048]{1,0:T(8,128)(2,1)S(1)}, bf16[128,2048]{1,0:T(8,128)(2,1)S(1)}) custom-call(bf16[2048,2048]{1,0:T(8,128)(2,1)} %x_hbm.1, f32[64,2048]{1,0:T(8,128)} %bitcast.6), custom_call_target="tpu_custom_call" | custom-call | tf_op jit(solution)/shard_map/power/pallas_call | solution.py:308
  6.1 0.1 collective-permute-start
  6.2 0.7 %own_power.1.keep_ref = f32[64,8,128]{2,1,0:T(8,128)S(1)} custom-call(bf16[128,2048]{1,0:T(8,128)(2,1)S(1)} %get-tuple-element.17.inner_ref, bf16[2048,2048]{1,0:T(8,128)(2,1)S(1)} %get-tuple-element.16.x_ref), custom_call_target="tpu_custom_call" | custom-call | tf_op jit(solution)/shard_map/own_power/pallas_call | solution.py:325
  6.9 0.8 %collective-permute-done.came_ref = f32[64,8,128]{2,1,0:T(8,128)S(1)} collective-permute-done((f32[64,8,128]{2,1,0:T(8,128)S(1)}, f32[64,8,128]{2,1,0:T(8,128)S(1)}, u32[]{:S(2)}, u32[]{:S(2)}) %collective-permute-start) | collective-permute-done | bytes 262176 | tf_op jit(solution)/shard_map/ppermute | solution.py:324
  7.7 22.2 %all_to_all.15.parts_ref = f32[64,8,128]{2,1,0:T(8,128)S(1)} all-to-all(f32[64,8,128]{2,1,0:T(8,128)S(1)} %add.1), channel_id=1, replica_groups=mesh['yz'=16,'core'=2,'slab'=4] {'yz','slab'}, dimensions={0} | all-to-all | bytes 524288 | tf_op jit(solution)/shard_map/all_to_all | solution.py:327
  29.9 0.1 spread.1
  30.0 15.3 %all_to_all.16.own_ref = f32[64,8,128]{2,1,0:T(8,128)S(1)} all-to-all(f32[64,8,128]{2,1,0:T(8,128)S(1)} %spread.1), channel_id=1, replica_groups=mesh['yz'=16,'core'=2,'slab'=4] {'yz','slab'}, dimensions={0} | all-to-all | bytes 524288 | tf_op jit(solution)/shard_map/all_to_all | solution.py:329
  45.3 0.0 collective-permute-start.1
  45.3 1.3 %own_modes.1.own_modes_ref = f32[64,2048]{1,0:T(8,128)S(1)} custom-call(bf16[2048,2048]{1,0:T(8,128)(2,1)S(1)} %get-tuple-element.16.x_ref, f32[64,8,128]{2,1,0:T(8,128)S(1)} %all_to_all.16.own_ref), custom_call_target="tpu_custom_call" | custom-call | tf_op jit(solution)/shard_map/own_modes/pallas_call | solution.py:331
  46.6 0.0 copy-start.1
  46.6 0.0 copy-start.2
  46.7 0.2 collective-permute-done.1.other_ref
  46.8 2.9 %coords.1 = (f32[16,40,128]{2,1,0:T(8,128)S(1)}, f32[16,40,128]{2,1,0:T(8,128)S(1)}, f32[64,2048]{1,0:T(8,128)S(1)}) custom-call(bf16[2048,2048]{1,0:T(8,128)(2,1)S(1)} %get-tuple-element.16.x_ref, f32[64,2048]{1,0:T(8,128)S(1)} %own_modes.1.own_modes_ref, f32[64,8,128]{2,1,0:T(8,128)S(1)} %collective-permute-done.1.other_ref), custom_call_target="tpu_custom_call" | custom-call | tf_op jit(solution)/shard_map/coords/pallas_call | solution.py:337
  49.7 0.0 copy-start
  49.7 0.4 collective-permute-start.2
  50.1 0.5 correlation.1.corr_ref
  50.6 0.0 copy-done
  50.6 0.8 %collective-permute-done.2.came_ref = f32[16,40,128]{2,1,0:T(8,128)S(1)} collective-permute-done((f32[16,40,128]{2,1,0:T(8,128)S(1)}, f32[16,40,128]{2,1,0:T(8,128)S(1)}, u32[]{:S(2)}, u32[]{:S(2)}) %collective-permute-start.2) | collective-permute-done | bytes 327712 | tf_op jit(solution)/shard_map/ppermute | solution.py:344
  51.4 0.9 %pair.1 = f32[64,5,2,128]{3,2,1,0:T(2,128)} custom-call(f32[16,40,128]{2,1,0:T(8,128)S(1)} %get-tuple-element.23.keep_ref, f32[16,40,128]{2,1,0:T(8,128)S(1)} %collective-permute-done.2.came_ref), custom_call_target="tpu_custom_call" | custom-call | tf_op jit(solution)/shard_map/pair/pallas_call | solution.py:348
  52.3 5.0 %all-to-all-start.2 = ((f32[64,5,2,128]{3,2,1,0:T(2,128)}), f32[64,5,2,128]{3,2,1,0:T(2,128)S(1)}, u32[]{:S(2)}, u32[]{:S(2)}) async-start(f32[64,5,2,128]{3,2,1,0:T(2,128)} %pair.1), calls=%async_computation.2 | async-start | bytes 655360 | tf_op jit(solution)/shard_map/all_to_all | solution.py:349
  57.4 5.2 %factor.1 = (bf16[64,2048]{1,0:T(8,128)(2,1)}, f32[64,64]{1,0:T(8,128)S(1)}, bf16[4096,128]{1,0:T(8,128)(2,1)S(1)}) custom-call(f32[64,64]{1,0:T(8,128)S(1)} %correlation.1.corr_ref, f32[64,2048]{1,0:T(8,128)} %copy-done, f32[64,4096]{1,0:T(8,128)} %bitcast.5), custom_call_target="tpu_custom_call" | custom-call | tf_op jit(solution)/shard_map/factor/pallas_call | solution.py:350
  62.6 6.5 %all-to-all-done.2.refs_0_ = f32[64,5,2,128]{3,2,1,0:T(2,128)S(1)} async-done(((f32[64,5,2,128]{3,2,1,0:T(2,128)}), f32[64,5,2,128]{3,2,1,0:T(2,128)S(1)}, u32[]{:S(2)}, u32[]{:S(2)}) %all-to-all-start.2) | async-done | bytes 327712 | tf_op jit(solution)/shard_map/all_to_all | solution.py:349
  69.1 0.0 copy-done.1
  69.1 0.0 copy-done.2
  69.1 2.0 %rollout.1 = (f32[16,64]{1,0:T(8,128)}, f32[16,64]{1,0:T(8,128)}) custom-call(f32[64,5,2,128]{3,2,1,0:T(2,128)S(1)} %all-to-all-done.2.refs_0_, f32[64,64]{1,0:T(8,128)S(1)} %get-tuple-element.25.refs_1_, f32[64,64]{1,0:T(8,128)S(1)} %copy-done.1, bf16[4096,128]{1,0:T(8,128)(2,1)S(1)} %get-tuple-element.26.refs_3_, f32[1,64]{1,0:T(1,128)S(1)} %bitcast.4), custom_call_target="tpu_custom_call" | custom-call | tf_op jit(solution)/shard_map/rollout/pallas_call | solution.py:366
  (1 shorter events, 0.0 us)
Async XLA Ops:
  6.1 1.6 %collective-permute-start = (f32[64,8,128]{2,1,0:T(8,128)S(1)}, f32[64,8,128]{2,1,0:T(8,128)S(1)}, u32[]{:S(2)}, u32[]{:S(2)}) collective-permute-start(f32[64,8,128]{2,1,0:T(8,128)S(1)} %get-tuple-element.18), channel_id=1, source_target_pairs={{0,4},{4,0},{1,5},{5,1},{2,6},{6,2},{3,7},{7,3},{8,12},{12,8},{9,1... | collective-permute-start | bytes 786440 | tf_op jit(solution)/shard_map/ppermute | solution.py:324
  45.3 1.5 %collective-permute-start.1 = (f32[64,8,128]{2,1,0:T(8,128)S(1)}, f32[64,8,128]{2,1,0:T(8,128)S(1)}, u32[]{:S(2)}, u32[]{:S(2)}) collective-permute-start(f32[64,8,128]{2,1,0:T(8,128)S(1)} %all_to_all.16.own_ref), channel_id=1, source_target_pairs={{0,4},{4,0},{1,5},{5,1},{2,6},{6,2},{3,7},{7,3},{8,12},{12,8},{9,1... | collective-permute-start | bytes 786440 | tf_op jit(solution)/shard_map/ppermute | solution.py:330
  46.6 22.4 %copy-start.1 = (f32[64,64]{1,0:T(8,128)S(1)}, f32[64,64]{1,0:T(8,128)}, u32[]{:S(2)}) copy-start(f32[64,64]{1,0:T(8,128)} %refs_2_.1) | copy-start | bytes 49156
  46.6 22.4 %copy-start.2 = (f32[64]{0:T(128)S(1)}, f32[64]{0:T(128)}, u32[]{:S(2)}) copy-start(f32[64]{0:T(128)} %param.9) | copy-start | bytes 772
  49.7 0.9 %copy-start = (f32[64,2048]{1,0:T(8,128)}, f32[64,2048]{1,0:T(8,128)S(1)}, u32[]{:S(2)}) copy-start(f32[64,2048]{1,0:T(8,128)S(1)} %get-tuple-element.21.modes_hbm) | copy-start | bytes 1572868
  49.7 1.7 %collective-permute-start.2 = (f32[16,40,128]{2,1,0:T(8,128)S(1)}, f32[16,40,128]{2,1,0:T(8,128)S(1)}, u32[]{:S(2)}, u32[]{:S(2)}) collective-permute-start(f32[16,40,128]{2,1,0:T(8,128)S(1)} %get-tuple-element.19), channel_id=1, source_target_pairs={{0,4},{4,0},{1,5},{5,1},{2,6},{6,2},{3,7},{7,3},{8,12},{12,8},{9,1... | collective-permute-start | bytes 983048 | tf_op jit(solution)/shard_map/ppermute | solution.py:344
  52.3 16.7 %all-to-all-start.2 = ((f32[64,5,2,128]{3,2,1,0:T(2,128)}), f32[64,5,2,128]{3,2,1,0:T(2,128)S(1)}, u32[]{:S(2)}, u32[]{:S(2)}) async-start(f32[64,5,2,128]{3,2,1,0:T(2,128)} %pair.1), calls=%async_computation.2 | async-start | bytes 655360 | tf_op jit(solution)/shard_map/all_to_all | solution.py:349

commit v8 on v7

--- a/solution.py
+++ b/solution.py
@@ -163,24 +163,25 @@
     corr_ref[...] = fold_rows(fold_lanes(dot_nt(pieces, pieces), 3), 3)
 
 
-def pair_kernel(keep_ref, came_ref, out_ref):
+def pair_kernel(keep_ref, came_ref, out_hbm, out_ref, sem):
     total = keep_ref[...] + came_ref[...]
     turned = pltpu.roll(total, RANK, axis=2)
     left = lax.broadcasted_iota(jnp.int32, (1, 1, 2 * RANK), 2) < RANK
     groups = total.shape[0]
-    chips, pairs = out_ref.shape[:2]
+    chips, deep = out_ref.shape[:2]
     slabs = chips // groups
-    share = 4 * pairs - 4
+    share = 2 * deep - 2
     for x in range(slabs):
         side, place = divmod(x * share, total.shape[1] - 8)
         near, far = (total, turned) if side == 0 else (turned, total)
-        middle = place + share // 2
-        chunk = jnp.where(
-            left, near[:, place : place + 2 * pairs], far[:, middle : middle + 2 * pairs]
-        )
+        middle = place + deep
+        chunk = jnp.where(left, near[:, place:middle], far[:, middle : middle + deep])
         for g in range(groups):
-            for i in range(pairs):
-                out_ref[slabs * g + x, i] = chunk[g, 2 * i : 2 * i + 2]
+            for i in range(deep):
+                out_ref[slabs * g + x, i] = chunk[g, i : i + 1]
+    copy = pltpu.make_async_copy(out_ref, out_hbm, sem)
+    copy.start()
+    copy.wait()
 
 
 def spread_lane(line, k):
@@ -188,7 +189,8 @@
 
 
 def factor_kernel(
-    corr_ref, modes_hbm, quad_hbm, projection_ref, inverse_ref, pieces_ref, modes_ref, quad_ref, sems
+    corr_ref, modes_hbm, quad_hbm, projection_hbm, inverse_ref, pieces_ref,
+    modes_ref, quad_ref, projection_ref, sems,
 ):
     quad_fetch = pltpu.make_async_copy(quad_hbm, quad_ref, sems.at[0])
     modes_fetch = pltpu.make_async_copy(modes_hbm, modes_ref, sems.at[1])
@@ -222,27 +224,26 @@
     quad_fetch.wait()
     pieces_ref[...] = pieces_of(quad_ref[...], PIECES).T
     modes_fetch.wait()
+    left = pieces_of(inverse_ref[...], 3)
     modes = jnp.dot(
-        inverse_ref[...],
-        modes_ref[...],
-        precision=lax.Precision.HIGHEST,
+        jnp.concatenate([left] * 3, axis=1),
+        pieces_of(modes_ref[...], 3),
         preferred_element_type=jnp.float32,
     )
-    projection_ref[...] = modes.astype(jnp.bfloat16)
+    projection_ref[...] = fold_rows(modes, 3).astype(jnp.bfloat16)
+    copy = pltpu.make_async_copy(projection_ref, projection_hbm, sems.at[2])
+    copy.start()
+    copy.wait()
 
 
 def rollout_kernel(
     scale, width, parts_ref, inverse_ref, linear_ref, pieces_ref, offset_ref,
-    reduced_ref, mismatch_ref,
+    reduced_hbm, mismatch_hbm, reduced_ref, mismatch_ref, sems,
 ):
     packed = jnp.sum(parts_ref[...], axis=0)
     packed = jnp.concatenate([packed[i] for i in range(packed.shape[0])], axis=0)
-    sides = packed[:, :RANK], packed[:, RANK:]
     share = reduced_ref.shape[0]
-    half = share // 2
-    coords = jnp.concatenate(
-        [side[:half] for side in sides] + [side[2 : half + 2] for side in sides], axis=0
-    )
+    coords = jnp.concatenate([packed[:, :RANK], packed[:, RANK:]], axis=0)
     coords = scale * lax.dot_general(
         coords,
         inverse_ref[...],
@@ -250,8 +251,10 @@
         precision=lax.Precision.HIGHEST,
         preferred_element_type=jnp.float32,
     )
-    state, target = coords[:share], coords[share:]
+    state, target = coords[:share], coords[2:]
     reduced_ref[...] = state
+    reduced_copy = pltpu.make_async_copy(reduced_ref, reduced_hbm, sems.at[0])
+    reduced_copy.start()
     pieces = pieces_ref[...]
     upper = lax.broadcasted_iota(jnp.int32, (share, 2 * RANK), 1) >= RANK
     for _ in range(2):
@@ -277,18 +280,22 @@
         state = state + 0.25 * (linear + quadratic + offset_ref[...])
     position = lax.axis_index(EVERY) * share + lax.broadcasted_iota(jnp.int32, (share, 1), 0)
     mismatch_ref[...] = jnp.where(position < width - 2, state - target, jnp.float32(0.0))
+    mismatch_copy = pltpu.make_async_copy(mismatch_ref, mismatch_hbm, sems.at[1])
+    mismatch_copy.start()
+    reduced_copy.wait()
+    mismatch_copy.wait()
 
 
 def in_hbm(value):
     return pltpu.with_memory_space_constraint(value, pltpu.HBM)
 
 
-def call(kernel, name, outs, ins, scratch=()):
+def call(kernel, name, outs, ins, scratch=(), places=None):
     return pl.pallas_call(
         kernel,
         out_shape=outs,
         in_specs=ins,
-        out_specs=jax.tree.map(lambda _: VMEM, outs),
+        out_specs=places or jax.tree.map(lambda _: VMEM, outs),
         scratch_shapes=list(scratch),
         compiler_params=LIMIT,
         name=name,
@@ -344,8 +351,15 @@
     came = lax.ppermute(send, "core", swap)
     correlation = call(correlation_kernel, "correlation", small, [VMEM, VMEM])(mine, theirs)
     came, correlation = lax.optimization_barrier((came, correlation))
-    chunks = shape((chips, share // 4 + 1, 2, 2 * RANK), f32)
-    parts = call(pair_kernel, "pair", chunks, [VMEM, VMEM])(keep, came)
+    chunk = (chips, share // 2 + 1, 1, 2 * RANK)
+    parts = call(
+        pair_kernel,
+        "pair",
+        shape(chunk, f32),
+        [VMEM, VMEM],
+        [pltpu.VMEM(chunk, f32), pltpu.SemaphoreType.DMA(())],
+        HBM,
+    )(keep, came)
     parts = lax.all_to_all(parts, CHIPS, 0, 0, tiled=True)
     projection, inverse, pieces = call(
         factor_kernel,
@@ -359,8 +373,10 @@
         [
             pltpu.VMEM((RANK, rows), f32),
             pltpu.VMEM((RANK, RANK * RANK), f32),
-            pltpu.SemaphoreType.DMA((2,)),
+            pltpu.VMEM((RANK, rows), jnp.bfloat16),
+            pltpu.SemaphoreType.DMA((3,)),
         ],
+        (HBM, VMEM, VMEM),
     )(correlation, in_hbm(modes), in_hbm(quad_op.T))
     factor_scale = math.sqrt(width) / (rows * devices)
     reduced, mismatch = call(
@@ -368,6 +384,12 @@
         "rollout",
         (own, own),
         [VMEM] * 5,
+        [
+            pltpu.VMEM((share, RANK), f32),
+            pltpu.VMEM((share, RANK), f32),
+            pltpu.SemaphoreType.DMA((2,)),
+        ],
+        (HBM, HBM),
     )(parts, inverse, linear_op, pieces, offset[None, :])
     return (projection.T, reduced, mismatch)
 

time: 71.3 us -> 71.2 us (level)
  no operation moved by 1% of the time
where the time goes in v8:
time: 71.2 us; the launch traced here: 70.9 us
  blocking collectives  37.5 us (53%)
  Pallas kernels  18.9 us (27%)
  waiting for transfers between devices  8.06 us (11%)
  starting transfers between devices  5.56 us (8%)
  between operations  0.9 us (1%)
    all_to_all x1, blocking collectives, body(): parts = lax.all_to_all(parts, CHIPS, 0, 0, tiled=True)  22.2 us
    all_to_all x1, blocking collectives, body(): mine = lax.all_to_all(spread, CHIPS, 0, 0, tiled=True)  15.3 us
    all_to_all x1, waiting for transfers between devices, body(): parts = lax.all_to_all(parts, CHIPS, 0, 0, tiled=True)  6.26 us
    pallas_call x1, Pallas kernels, body(): call(power_kernel, 'power', (tiles, shape((rows, width), jnp.bfloat16), s...  5.46 us
    all_to_all x1, starting transfers between devices, body(): parts = lax.all_to_all(parts, CHIPS, 0, 0, tiled=True)  5.05 us
    pallas_call x1, Pallas kernels, body(): call(factor_kernel, 'factor', (shape((RANK, rows), jnp.bfloat16), small,...  5.04 us
    pallas_call x1, Pallas kernels, body(): call(coords_kernel, 'coords', (packed, packed, shape((RANK, rows), f32)),...  2.87 us
    pallas_call x1, Pallas kernels, body(): call(lambda *refs: rollout_kernel(factor_scale, width, *refs), 'rollout',...  2.05 us
  transfers between devices with their start and end apart: 4, of which 4 were waited for; matrix products, arithmetic and copies ran while one was open for 0% of the time, Pallas kernels for 11%

profile of v8, /device:TPU:0, one launch (start us, length us, event | category | flops | bytes accessed | tf_op | source)
XLA Modules:
  0.0 70.9 jit_solution(17671993740348390679)
XLA Ops:
  0.6 5.5 %power.1 = (f32[64,8,128]{2,1,0:T(8,128)S(1)}, bf16[2048,2048]{1,0:T(8,128)(2,1)S(1)}, bf16[128,2048]{1,0:T(8,128)(2,1)S(1)}) custom-call(bf16[2048,2048]{1,0:T(8,128)(2,1)} %x_hbm.1, f32[64,2048]{1,0:T(8,128)} %bitcast.6), custom_call_target="tpu_custom_call" | custom-call | tf_op jit(solution)/shard_map/power/pallas_call | solution.py:315
  6.1 0.1 collective-permute-start
  6.2 0.7 %own_power.1.keep_ref = f32[64,8,128]{2,1,0:T(8,128)S(1)} custom-call(bf16[128,2048]{1,0:T(8,128)(2,1)S(1)} %get-tuple-element.17.inner_ref, bf16[2048,2048]{1,0:T(8,128)(2,1)S(1)} %get-tuple-element.16.x_ref), custom_call_target="tpu_custom_call" | custom-call | tf_op jit(solution)/shard_map/own_power/pallas_call | solution.py:332
  6.9 0.8 %collective-permute-done.came_ref = f32[64,8,128]{2,1,0:T(8,128)S(1)} collective-permute-done((f32[64,8,128]{2,1,0:T(8,128)S(1)}, f32[64,8,128]{2,1,0:T(8,128)S(1)}, u32[]{:S(2)}, u32[]{:S(2)}) %collective-permute-start) | collective-permute-done | bytes 262176 | tf_op jit(solution)/shard_map/ppermute | solution.py:331
  7.7 22.2 %all_to_all.15.parts_ref = f32[64,8,128]{2,1,0:T(8,128)S(1)} all-to-all(f32[64,8,128]{2,1,0:T(8,128)S(1)} %add.1), channel_id=1, replica_groups=mesh['yz'=16,'core'=2,'slab'=4] {'yz','slab'}, dimensions={0} | all-to-all | bytes 524288 | tf_op jit(solution)/shard_map/all_to_all | solution.py:334
  29.9 0.1 spread.1
  30.0 15.3 %all_to_all.16.own_ref = f32[64,8,128]{2,1,0:T(8,128)S(1)} all-to-all(f32[64,8,128]{2,1,0:T(8,128)S(1)} %spread.1), channel_id=1, replica_groups=mesh['yz'=16,'core'=2,'slab'=4] {'yz','slab'}, dimensions={0} | all-to-all | bytes 524288 | tf_op jit(solution)/shard_map/all_to_all | solution.py:336
  45.3 0.0 collective-permute-start.1
  45.3 1.3 %own_modes.1.own_modes_ref = f32[64,2048]{1,0:T(8,128)S(1)} custom-call(bf16[2048,2048]{1,0:T(8,128)(2,1)S(1)} %get-tuple-element.16.x_ref, f32[64,8,128]{2,1,0:T(8,128)S(1)} %all_to_all.16.own_ref), custom_call_target="tpu_custom_call" | custom-call | tf_op jit(solution)/shard_map/own_modes/pallas_call | solution.py:338
  46.6 0.0 copy-start.1
  46.6 0.0 copy-start.2
  46.7 0.2 collective-permute-done.1.other_ref
  46.8 2.9 %coords.1 = (f32[16,40,128]{2,1,0:T(8,128)S(1)}, f32[16,40,128]{2,1,0:T(8,128)S(1)}, f32[64,2048]{1,0:T(8,128)S(1)}) custom-call(bf16[2048,2048]{1,0:T(8,128)(2,1)S(1)} %get-tuple-element.16.x_ref, f32[64,2048]{1,0:T(8,128)S(1)} %own_modes.1.own_modes_ref, f32[64,8,128]{2,1,0:T(8,128)S(1)} %collective-permute-done.1.other_ref), custom_call_target="tpu_custom_call" | custom-call | tf_op jit(solution)/shard_map/coords/pallas_call | solution.py:344
  49.7 0.0 copy-start
  49.7 0.4 collective-permute-start.2
  50.1 0.5 correlation.1.corr_ref
  50.6 0.0 copy-done
  50.6 0.8 %collective-permute-done.2.came_ref = f32[16,40,128]{2,1,0:T(8,128)S(1)} collective-permute-done((f32[16,40,128]{2,1,0:T(8,128)S(1)}, f32[16,40,128]{2,1,0:T(8,128)S(1)}, u32[]{:S(2)}, u32[]{:S(2)}) %collective-permute-start.2) | collective-permute-done | bytes 327712 | tf_op jit(solution)/shard_map/ppermute | solution.py:351
  51.4 0.9 %pair.1 = f32[64,9,1,128]{3,2,1,0:T(1,128)} custom-call(f32[16,40,128]{2,1,0:T(8,128)S(1)} %get-tuple-element.23.keep_ref, f32[16,40,128]{2,1,0:T(8,128)S(1)} %collective-permute-done.2.came_ref), custom_call_target="tpu_custom_call" | custom-call | tf_op jit(solution)/shard_map/pair/pallas_call | solution.py:355
  52.3 5.1 %all-to-all-start.2 = ((f32[64,9,1,128]{3,2,1,0:T(1,128)}), f32[64,9,1,128]{3,2,1,0:T(1,128)S(1)}, u32[]{:S(2)}, u32[]{:S(2)}) async-start(f32[64,9,1,128]{3,2,1,0:T(1,128)} %pair.1), calls=%async_computation.2 | async-start | bytes 589824 | tf_op jit(solution)/shard_map/all_to_all | solution.py:363
  57.4 5.0 %factor.1 = (bf16[64,2048]{1,0:T(8,128)(2,1)}, f32[64,64]{1,0:T(8,128)S(1)}, bf16[4096,128]{1,0:T(8,128)(2,1)S(1)}) custom-call(f32[64,64]{1,0:T(8,128)S(1)} %correlation.1.corr_ref, f32[64,2048]{1,0:T(8,128)} %copy-done, f32[64,4096]{1,0:T(8,128)} %bitcast.5), custom_call_target="tpu_custom_call" | custom-call | tf_op jit(solution)/shard_map/factor/pallas_call | solution.py:364
  62.4 6.3 %all-to-all-done.2.refs_0_ = f32[64,9,1,128]{3,2,1,0:T(1,128)S(1)} async-done(((f32[64,9,1,128]{3,2,1,0:T(1,128)}), f32[64,9,1,128]{3,2,1,0:T(1,128)S(1)}, u32[]{:S(2)}, u32[]{:S(2)}) %all-to-all-start.2) | async-done | bytes 294944 | tf_op jit(solution)/shard_map/all_to_all | solution.py:363
  68.7 0.0 copy-done.1
  68.7 0.0 copy-done.2
  68.7 2.1 %rollout.1 = (f32[16,64]{1,0:T(8,128)}, f32[16,64]{1,0:T(8,128)}) custom-call(f32[64,9,1,128]{3,2,1,0:T(1,128)S(1)} %all-to-all-done.2.refs_0_, f32[64,64]{1,0:T(8,128)S(1)} %get-tuple-element.25.refs_1_, f32[64,64]{1,0:T(8,128)S(1)} %copy-done.1, bf16[4096,128]{1,0:T(8,128)(2,1)S(1)} %get-tuple-element.26.refs_3_, f32[1,64]{1,0:T(1,128)S(1)} %bitcast.4), custom_call_target="tpu_custom_call" | custom-call | tf_op jit(solution)/shard_map/rollout/pallas_call | solution.py:382
  (1 shorter events, 0.0 us)
Async XLA Ops:
  6.1 1.6 %collective-permute-start = (f32[64,8,128]{2,1,0:T(8,128)S(1)}, f32[64,8,128]{2,1,0:T(8,128)S(1)}, u32[]{:S(2)}, u32[]{:S(2)}) collective-permute-start(f32[64,8,128]{2,1,0:T(8,128)S(1)} %get-tuple-element.18), channel_id=1, source_target_pairs={{0,4},{4,0},{1,5},{5,1},{2,6},{6,2},{3,7},{7,3},{8,12},{12,8},{9,1... | collective-permute-start | bytes 786440 | tf_op jit(solution)/shard_map/ppermute | solution.py:331
  45.3 1.5 %collective-permute-start.1 = (f32[64,8,128]{2,1,0:T(8,128)S(1)}, f32[64,8,128]{2,1,0:T(8,128)S(1)}, u32[]{:S(2)}, u32[]{:S(2)}) collective-permute-start(f32[64,8,128]{2,1,0:T(8,128)S(1)} %all_to_all.16.own_ref), channel_id=1, source_target_pairs={{0,4},{4,0},{1,5},{5,1},{2,6},{6,2},{3,7},{7,3},{8,12},{12,8},{9,1... | collective-permute-start | bytes 786440 | tf_op jit(solution)/shard_map/ppermute | solution.py:337
  46.6 22.1 %copy-start.1 = (f32[64,64]{1,0:T(8,128)S(1)}, f32[64,64]{1,0:T(8,128)}, u32[]{:S(2)}) copy-start(f32[64,64]{1,0:T(8,128)} %refs_2_.1) | copy-start | bytes 49156
  46.6 22.1 %copy-start.2 = (f32[64]{0:T(128)S(1)}, f32[64]{0:T(128)}, u32[]{:S(2)}) copy-start(f32[64]{0:T(128)} %param.9) | copy-start | bytes 772
  49.7 0.9 %copy-start = (f32[64,2048]{1,0:T(8,128)}, f32[64,2048]{1,0:T(8,128)S(1)}, u32[]{:S(2)}) copy-start(f32[64,2048]{1,0:T(8,128)S(1)} %get-tuple-element.21.modes_hbm) | copy-start | bytes 1572868
  49.7 1.7 %collective-permute-start.2 = (f32[16,40,128]{2,1,0:T(8,128)S(1)}, f32[16,40,128]{2,1,0:T(8,128)S(1)}, u32[]{:S(2)}, u32[]{:S(2)}) collective-permute-start(f32[16,40,128]{2,1,0:T(8,128)S(1)} %get-tuple-element.19), channel_id=1, source_target_pairs={{0,4},{4,0},{1,5},{5,1},{2,6},{6,2},{3,7},{7,3},{8,12},{12,8},{9,1... | collective-permute-start | bytes 983048 | tf_op jit(solution)/shard_map/ppermute | solution.py:351
  52.3 16.4 %all-to-all-start.2 = ((f32[64,9,1,128]{3,2,1,0:T(1,128)}), f32[64,9,1,128]{3,2,1,0:T(1,128)S(1)}, u32[]{:S(2)}, u32[]{:S(2)}) async-start(f32[64,9,1,128]{3,2,1,0:T(1,128)} %pair.1), calls=%async_computation.2 | async-start | bytes 589824 | tf_op jit(solution)/shard_map/all_to_all | solution.py:363

commit v9 on v8

--- a/solution.py
+++ b/solution.py
@@ -240,9 +240,11 @@
     scale, width, parts_ref, inverse_ref, linear_ref, pieces_ref, offset_ref,
     reduced_hbm, mismatch_hbm, reduced_ref, mismatch_ref, sems,
 ):
-    packed = jnp.sum(parts_ref[...], axis=0)
-    packed = jnp.concatenate([packed[i] for i in range(packed.shape[0])], axis=0)
     share = reduced_ref.shape[0]
+    deep = share // 2 + 1
+    run = 8 * deep
+    total = sum(parts_ref[i : i + run, :] for i in range(0, parts_ref.shape[0], run))
+    packed = sum(total[i : i + deep] for i in range(0, run, deep))
     coords = jnp.concatenate([packed[:, :RANK], packed[:, RANK:]], axis=0)
     coords = scale * lax.dot_general(
         coords,
@@ -360,7 +362,7 @@
         [pltpu.VMEM(chunk, f32), pltpu.SemaphoreType.DMA(())],
         HBM,
     )(keep, came)
-    parts = lax.all_to_all(parts, CHIPS, 0, 0, tiled=True)
+    parts = lax.all_to_all(parts, CHIPS, 0, 0, tiled=True).reshape(-1, 2 * RANK)
     projection, inverse, pieces = call(
         factor_kernel,
         "factor",

time: 71.2 us -> 71 us (level)
  no operation moved by 1% of the time
where the time goes in v9:
time: 71 us; the launch traced here: 70.7 us
  blocking collectives  37.5 us (53%)
  Pallas kernels  18.8 us (26%)
  waiting for transfers between devices  8.06 us (11%)
  starting transfers between devices  5.56 us (8%)
  between operations  0.9 us (1%)
    all_to_all x1, blocking collectives, body(): parts = lax.all_to_all(parts, CHIPS, 0, 0, tiled=True)  22.2 us
    all_to_all x1, blocking collectives, body(): mine = lax.all_to_all(spread, CHIPS, 0, 0, tiled=True)  15.3 us
    all_to_all x1, waiting for transfers between devices, body(): parts = lax.all_to_all(parts, CHIPS, 0, 0, tiled=True).reshape(-1, 2 * RANK)  6.26 us
    pallas_call x1, Pallas kernels, body(): call(power_kernel, 'power', (tiles, shape((rows, width), jnp.bfloat16), s...  5.46 us
    all_to_all x1, starting transfers between devices, body(): parts = lax.all_to_all(parts, CHIPS, 0, 0, tiled=True).reshape(-1, 2 * RANK)  5.05 us
    pallas_call x1, Pallas kernels, body(): call(factor_kernel, 'factor', (shape((RANK, rows), jnp.bfloat16), small,...  5.04 us
    pallas_call x1, Pallas kernels, body(): call(coords_kernel, 'coords', (packed, packed, shape((RANK, rows), f32)),...  2.87 us
    pallas_call x1, Pallas kernels, body(): call(lambda *refs: rollout_kernel(factor_scale, width, *refs), 'rollout',...  1.88 us
  transfers between devices with their start and end apart: 4, of which 4 were waited for; matrix products, arithmetic and copies ran while one was open for 0% of the time, Pallas kernels for 11%

profile of v9, /device:TPU:0, one launch (start us, length us, event | category | flops | bytes accessed | tf_op | source)
XLA Modules:
  0.0 70.7 jit_solution(14788982096387243199)
XLA Ops:
  0.6 5.5 %power.1 = (f32[64,8,128]{2,1,0:T(8,128)S(1)}, bf16[2048,2048]{1,0:T(8,128)(2,1)S(1)}, bf16[128,2048]{1,0:T(8,128)(2,1)S(1)}) custom-call(bf16[2048,2048]{1,0:T(8,128)(2,1)} %x_hbm.1, f32[64,2048]{1,0:T(8,128)} %bitcast.8), custom_call_target="tpu_custom_call" | custom-call | tf_op jit(solution)/shard_map/power/pallas_call | solution.py:317
  6.1 0.1 collective-permute-start
  6.2 0.7 %own_power.1.keep_ref = f32[64,8,128]{2,1,0:T(8,128)S(1)} custom-call(bf16[128,2048]{1,0:T(8,128)(2,1)S(1)} %get-tuple-element.17.inner_ref, bf16[2048,2048]{1,0:T(8,128)(2,1)S(1)} %get-tuple-element.16.x_ref), custom_call_target="tpu_custom_call" | custom-call | tf_op jit(solution)/shard_map/own_power/pallas_call | solution.py:334
  6.9 0.8 %collective-permute-done.came_ref = f32[64,8,128]{2,1,0:T(8,128)S(1)} collective-permute-done((f32[64,8,128]{2,1,0:T(8,128)S(1)}, f32[64,8,128]{2,1,0:T(8,128)S(1)}, u32[]{:S(2)}, u32[]{:S(2)}) %collective-permute-start) | collective-permute-done | bytes 262176 | tf_op jit(solution)/shard_map/ppermute | solution.py:333
  7.7 22.2 %all_to_all.15.parts_ref = f32[64,8,128]{2,1,0:T(8,128)S(1)} all-to-all(f32[64,8,128]{2,1,0:T(8,128)S(1)} %add.1), channel_id=1, replica_groups=mesh['yz'=16,'core'=2,'slab'=4] {'yz','slab'}, dimensions={0} | all-to-all | bytes 524288 | tf_op jit(solution)/shard_map/all_to_all | solution.py:336
  29.9 0.1 spread.1
  30.0 15.3 %all_to_all.16.own_ref = f32[64,8,128]{2,1,0:T(8,128)S(1)} all-to-all(f32[64,8,128]{2,1,0:T(8,128)S(1)} %spread.1), channel_id=1, replica_groups=mesh['yz'=16,'core'=2,'slab'=4] {'yz','slab'}, dimensions={0} | all-to-all | bytes 524288 | tf_op jit(solution)/shard_map/all_to_all | solution.py:338
  45.3 0.0 collective-permute-start.1
  45.3 1.3 %own_modes.1.own_modes_ref = f32[64,2048]{1,0:T(8,128)S(1)} custom-call(bf16[2048,2048]{1,0:T(8,128)(2,1)S(1)} %get-tuple-element.16.x_ref, f32[64,8,128]{2,1,0:T(8,128)S(1)} %all_to_all.16.own_ref), custom_call_target="tpu_custom_call" | custom-call | tf_op jit(solution)/shard_map/own_modes/pallas_call | solution.py:340
  46.6 0.0 copy-start.1
  46.6 0.0 copy-start.2
  46.7 0.2 collective-permute-done.1.other_ref
  46.8 2.9 %coords.1 = (f32[16,40,128]{2,1,0:T(8,128)S(1)}, f32[16,40,128]{2,1,0:T(8,128)S(1)}, f32[64,2048]{1,0:T(8,128)S(1)}) custom-call(bf16[2048,2048]{1,0:T(8,128)(2,1)S(1)} %get-tuple-element.16.x_ref, f32[64,2048]{1,0:T(8,128)S(1)} %own_modes.1.own_modes_ref, f32[64,8,128]{2,1,0:T(8,128)S(1)} %collective-permute-done.1.other_ref), custom_call_target="tpu_custom_call" | custom-call | tf_op jit(solution)/shard_map/coords/pallas_call | solution.py:346
  49.7 0.0 copy-start
  49.7 0.4 collective-permute-start.2
  50.1 0.5 correlation.1.corr_ref
  50.6 0.0 copy-done
  50.6 0.8 %collective-permute-done.2.came_ref = f32[16,40,128]{2,1,0:T(8,128)S(1)} collective-permute-done((f32[16,40,128]{2,1,0:T(8,128)S(1)}, f32[16,40,128]{2,1,0:T(8,128)S(1)}, u32[]{:S(2)}, u32[]{:S(2)}) %collective-permute-start.2) | collective-permute-done | bytes 327712 | tf_op jit(solution)/shard_map/ppermute | solution.py:353
  51.4 0.9 %pair.1 = f32[64,9,1,128]{3,2,1,0:T(1,128)} custom-call(f32[16,40,128]{2,1,0:T(8,128)S(1)} %get-tuple-element.23.keep_ref, f32[16,40,128]{2,1,0:T(8,128)S(1)} %collective-permute-done.2.came_ref), custom_call_target="tpu_custom_call" | custom-call | tf_op jit(solution)/shard_map/pair/pallas_call | solution.py:357
  52.3 5.1 %all-to-all-start.2 = ((f32[64,9,1,128]{3,2,1,0:T(1,128)}), f32[64,9,1,128]{3,2,1,0:T(1,128)S(1)}, u32[]{:S(2)}, u32[]{:S(2)}) async-start(f32[64,9,1,128]{3,2,1,0:T(1,128)} %pair.1), calls=%async_computation.2 | async-start | bytes 589824 | tf_op jit(solution)/shard_map/all_to_all | solution.py:365
  57.4 5.0 %factor.1 = (bf16[64,2048]{1,0:T(8,128)(2,1)}, f32[64,64]{1,0:T(8,128)S(1)}, bf16[4096,128]{1,0:T(8,128)(2,1)S(1)}) custom-call(f32[64,64]{1,0:T(8,128)S(1)} %correlation.1.corr_ref, f32[64,2048]{1,0:T(8,128)} %copy-done, f32[64,4096]{1,0:T(8,128)} %bitcast.7), custom_call_target="tpu_custom_call" | custom-call | tf_op jit(solution)/shard_map/factor/pallas_call | solution.py:366
  62.4 6.3 %all-to-all-done.2 = f32[64,9,1,128]{3,2,1,0:T(1,128)S(1)} async-done(((f32[64,9,1,128]{3,2,1,0:T(1,128)}), f32[64,9,1,128]{3,2,1,0:T(1,128)S(1)}, u32[]{:S(2)}, u32[]{:S(2)}) %all-to-all-start.2) | async-done | bytes 294944 | tf_op jit(solution)/shard_map/all_to_all | solution.py:365
  68.7 0.0 copy-done.1
  68.7 0.0 copy-done.2
  68.7 1.9 %rollout.1 = (f32[16,64]{1,0:T(8,128)}, f32[16,64]{1,0:T(8,128)}) custom-call(f32[576,128]{1,0:T(8,128)S(1)} %bitcast.5, f32[64,64]{1,0:T(8,128)S(1)} %get-tuple-element.25.refs_1_, f32[64,64]{1,0:T(8,128)S(1)} %copy-done.1, bf16[4096,128]{1,0:T(8,128)(2,1)S(1)} %get-tuple-element.26.refs_3_, f32[1,64]{1,0:T(1,128)S(1)} %bitcast.6), custom_call_target="tpu_custom_call" | custom-call | tf_op jit(solution)/shard_map/rollout/pallas_call | solution.py:384
  (1 shorter events, 0.0 us)
Async XLA Ops:
  6.1 1.6 %collective-permute-start = (f32[64,8,128]{2,1,0:T(8,128)S(1)}, f32[64,8,128]{2,1,0:T(8,128)S(1)}, u32[]{:S(2)}, u32[]{:S(2)}) collective-permute-start(f32[64,8,128]{2,1,0:T(8,128)S(1)} %get-tuple-element.18), channel_id=1, source_target_pairs={{0,4},{4,0},{1,5},{5,1},{2,6},{6,2},{3,7},{7,3},{8,12},{12,8},{9,1... | collective-permute-start | bytes 786440 | tf_op jit(solution)/shard_map/ppermute | solution.py:333
  45.3 1.5 %collective-permute-start.1 = (f32[64,8,128]{2,1,0:T(8,128)S(1)}, f32[64,8,128]{2,1,0:T(8,128)S(1)}, u32[]{:S(2)}, u32[]{:S(2)}) collective-permute-start(f32[64,8,128]{2,1,0:T(8,128)S(1)} %all_to_all.16.own_ref), channel_id=1, source_target_pairs={{0,4},{4,0},{1,5},{5,1},{2,6},{6,2},{3,7},{7,3},{8,12},{12,8},{9,1... | collective-permute-start | bytes 786440 | tf_op jit(solution)/shard_map/ppermute | solution.py:339
  46.6 22.1 %copy-start.1 = (f32[64,64]{1,0:T(8,128)S(1)}, f32[64,64]{1,0:T(8,128)}, u32[]{:S(2)}) copy-start(f32[64,64]{1,0:T(8,128)} %refs_2_.1) | copy-start | bytes 49156
  46.6 22.1 %copy-start.2 = (f32[64]{0:T(128)S(1)}, f32[64]{0:T(128)}, u32[]{:S(2)}) copy-start(f32[64]{0:T(128)} %param.9) | copy-start | bytes 772
  49.7 0.9 %copy-start = (f32[64,2048]{1,0:T(8,128)}, f32[64,2048]{1,0:T(8,128)S(1)}, u32[]{:S(2)}) copy-start(f32[64,2048]{1,0:T(8,128)S(1)} %get-tuple-element.21.modes_hbm) | copy-start | bytes 1572868
  49.7 1.7 %collective-permute-start.2 = (f32[16,40,128]{2,1,0:T(8,128)S(1)}, f32[16,40,128]{2,1,0:T(8,128)S(1)}, u32[]{:S(2)}, u32[]{:S(2)}) collective-permute-start(f32[16,40,128]{2,1,0:T(8,128)S(1)} %get-tuple-element.19), channel_id=1, source_target_pairs={{0,4},{4,0},{1,5},{5,1},{2,6},{6,2},{3,7},{7,3},{8,12},{12,8},{9,1... | collective-permute-start | bytes 983048 | tf_op jit(solution)/shard_map/ppermute | solution.py:353
  52.3 16.4 %all-to-all-start.2 = ((f32[64,9,1,128]{3,2,1,0:T(1,128)}), f32[64,9,1,128]{3,2,1,0:T(1,128)S(1)}, u32[]{:S(2)}, u32[]{:S(2)}) async-start(f32[64,9,1,128]{3,2,1,0:T(1,128)} %pair.1), calls=%async_computation.2 | async-start | bytes 589824 | tf_op jit(solution)/shard_map/all_to_all | solution.py:365

commit v10 on v9

--- a/solution.py
+++ b/solution.py
@@ -163,7 +163,7 @@
     corr_ref[...] = fold_rows(fold_lanes(dot_nt(pieces, pieces), 3), 3)
 
 
-def pair_kernel(keep_ref, came_ref, out_hbm, out_ref, sem):
+def pair_kernel(keep_ref, came_ref, out_hbm, out_ref, sems):
     total = keep_ref[...] + came_ref[...]
     turned = pltpu.roll(total, RANK, axis=2)
     left = lax.broadcasted_iota(jnp.int32, (1, 1, 2 * RANK), 2) < RANK
@@ -171,17 +171,25 @@
     chips, deep = out_ref.shape[:2]
     slabs = chips // groups
     share = 2 * deep - 2
-    for x in range(slabs):
-        side, place = divmod(x * share, total.shape[1] - 8)
-        near, far = (total, turned) if side == 0 else (turned, total)
-        middle = place + deep
-        chunk = jnp.where(left, near[:, place:middle], far[:, middle : middle + deep])
-        for g in range(groups):
-            for i in range(deep):
-                out_ref[slabs * g + x, i] = chunk[g, i : i + 1]
-    copy = pltpu.make_async_copy(out_ref, out_hbm, sem)
-    copy.start()
-    copy.wait()
+    part = groups // 2
+    copies = []
+    for start in range(0, groups, part):
+        for x in range(slabs):
+            side, place = divmod(x * share, total.shape[1] - 8)
+            near, far = (total, turned) if side == 0 else (turned, total)
+            near, far = near[start : start + part], far[start : start + part]
+            middle = place + deep
+            chunk = jnp.where(left, near[:, place:middle], far[:, middle : middle + deep])
+            for g in range(part):
+                for i in range(deep):
+                    out_ref[slabs * (start + g) + x, i] = chunk[g, i : i + 1]
+        here = pl.ds(slabs * start, slabs * part)
+        copies.append(
+            pltpu.make_async_copy(out_ref.at[here], out_hbm.at[here], sems.at[start // part])
+        )
+        copies[-1].start()
+    for copy in copies:
+        copy.wait()
 
 
 def spread_lane(line, k):
@@ -359,7 +367,7 @@
         "pair",
         shape(chunk, f32),
         [VMEM, VMEM],
-        [pltpu.VMEM(chunk, f32), pltpu.SemaphoreType.DMA(())],
+        [pltpu.VMEM(chunk, f32), pltpu.SemaphoreType.DMA((2,))],
         HBM,
     )(keep, came)
     parts = lax.all_to_all(parts, CHIPS, 0, 0, tiled=True).reshape(-1, 2 * RANK)

time: 71 us -> 71 us (level)
  no operation moved by 1% of the time
where the time goes in v10:
time: 71 us; the launch traced here: 70.7 us
  blocking collectives  37.5 us (53%)
  Pallas kernels  18.7 us (26%)
  waiting for transfers between devices  8.06 us (11%)
  starting transfers between devices  5.56 us (8%)
  between operations  0.9 us (1%)
    all_to_all x1, blocking collectives, body(): parts = lax.all_to_all(parts, CHIPS, 0, 0, tiled=True)  22.2 us
    all_to_all x1, blocking collectives, body(): mine = lax.all_to_all(spread, CHIPS, 0, 0, tiled=True)  15.3 us
    all_to_all x1, waiting for transfers between devices, body(): parts = lax.all_to_all(parts, CHIPS, 0, 0, tiled=True).reshape(-1, 2 * RANK)  6.27 us
    pallas_call x1, Pallas kernels, body(): call(power_kernel, 'power', (tiles, shape((rows, width), jnp.bfloat16), s...  5.46 us
    all_to_all x1, starting transfers between devices, body(): parts = lax.all_to_all(parts, CHIPS, 0, 0, tiled=True).reshape(-1, 2 * RANK)  5.05 us
    pallas_call x1, Pallas kernels, body(): call(factor_kernel, 'factor', (shape((RANK, rows), jnp.bfloat16), small,...  5.04 us
    pallas_call x1, Pallas kernels, body(): call(coords_kernel, 'coords', (packed, packed, shape((RANK, rows), f32)),...  2.87 us
    pallas_call x1, Pallas kernels, body(): call(lambda *refs: rollout_kernel(factor_scale, width, *refs), 'rollout',...  1.88 us
  transfers between devices with their start and end apart: 4, of which 4 were waited for; matrix products, arithmetic and copies ran while one was open for 0% of the time, Pallas kernels for 11%

profile of v10, /device:TPU:0, one launch (start us, length us, event | category | flops | bytes accessed | tf_op | source)
XLA Modules:
  0.0 70.7 jit_solution(7704746357441866939)
XLA Ops:
  0.6 5.5 %power.1 = (f32[64,8,128]{2,1,0:T(8,128)S(1)}, bf16[2048,2048]{1,0:T(8,128)(2,1)S(1)}, bf16[128,2048]{1,0:T(8,128)(2,1)S(1)}) custom-call(bf16[2048,2048]{1,0:T(8,128)(2,1)} %x_hbm.1, f32[64,2048]{1,0:T(8,128)} %bitcast.8), custom_call_target="tpu_custom_call" | custom-call | tf_op jit(solution)/shard_map/power/pallas_call | solution.py:325
  6.1 0.1 collective-permute-start
  6.2 0.7 %own_power.1.keep_ref = f32[64,8,128]{2,1,0:T(8,128)S(1)} custom-call(bf16[128,2048]{1,0:T(8,128)(2,1)S(1)} %get-tuple-element.17.inner_ref, bf16[2048,2048]{1,0:T(8,128)(2,1)S(1)} %get-tuple-element.16.x_ref), custom_call_target="tpu_custom_call" | custom-call | tf_op jit(solution)/shard_map/own_power/pallas_call | solution.py:342
  6.9 0.8 %collective-permute-done.came_ref = f32[64,8,128]{2,1,0:T(8,128)S(1)} collective-permute-done((f32[64,8,128]{2,1,0:T(8,128)S(1)}, f32[64,8,128]{2,1,0:T(8,128)S(1)}, u32[]{:S(2)}, u32[]{:S(2)}) %collective-permute-start) | collective-permute-done | bytes 262176 | tf_op jit(solution)/shard_map/ppermute | solution.py:341
  7.7 22.2 %all_to_all.15.parts_ref = f32[64,8,128]{2,1,0:T(8,128)S(1)} all-to-all(f32[64,8,128]{2,1,0:T(8,128)S(1)} %add.1), channel_id=1, replica_groups=mesh['yz'=16,'core'=2,'slab'=4] {'yz','slab'}, dimensions={0} | all-to-all | bytes 524288 | tf_op jit(solution)/shard_map/all_to_all | solution.py:344
  29.9 0.1 spread.1
  30.0 15.3 %all_to_all.16.own_ref = f32[64,8,128]{2,1,0:T(8,128)S(1)} all-to-all(f32[64,8,128]{2,1,0:T(8,128)S(1)} %spread.1), channel_id=1, replica_groups=mesh['yz'=16,'core'=2,'slab'=4] {'yz','slab'}, dimensions={0} | all-to-all | bytes 524288 | tf_op jit(solution)/shard_map/all_to_all | solution.py:346
  45.3 0.0 collective-permute-start.1
  45.3 1.3 %own_modes.1.own_modes_ref = f32[64,2048]{1,0:T(8,128)S(1)} custom-call(bf16[2048,2048]{1,0:T(8,128)(2,1)S(1)} %get-tuple-element.16.x_ref, f32[64,8,128]{2,1,0:T(8,128)S(1)} %all_to_all.16.own_ref), custom_call_target="tpu_custom_call" | custom-call | tf_op jit(solution)/shard_map/own_modes/pallas_call | solution.py:348
  46.6 0.0 copy-start.1
  46.6 0.0 copy-start.2
  46.7 0.2 collective-permute-done.1.other_ref
  46.8 2.9 %coords.1 = (f32[16,40,128]{2,1,0:T(8,128)S(1)}, f32[16,40,128]{2,1,0:T(8,128)S(1)}, f32[64,2048]{1,0:T(8,128)S(1)}) custom-call(bf16[2048,2048]{1,0:T(8,128)(2,1)S(1)} %get-tuple-element.16.x_ref, f32[64,2048]{1,0:T(8,128)S(1)} %own_modes.1.own_modes_ref, f32[64,8,128]{2,1,0:T(8,128)S(1)} %collective-permute-done.1.other_ref), custom_call_target="tpu_custom_call" | custom-call | tf_op jit(solution)/shard_map/coords/pallas_call | solution.py:354
  49.7 0.0 copy-start
  49.7 0.4 collective-permute-start.2
  50.1 0.5 correlation.1.corr_ref
  50.6 0.0 copy-done
  50.6 0.8 %collective-permute-done.2.came_ref = f32[16,40,128]{2,1,0:T(8,128)S(1)} collective-permute-done((f32[16,40,128]{2,1,0:T(8,128)S(1)}, f32[16,40,128]{2,1,0:T(8,128)S(1)}, u32[]{:S(2)}, u32[]{:S(2)}) %collective-permute-start.2) | collective-permute-done | bytes 327712 | tf_op jit(solution)/shard_map/ppermute | solution.py:361
  51.4 0.8 %pair.1 = f32[64,9,1,128]{3,2,1,0:T(1,128)} custom-call(f32[16,40,128]{2,1,0:T(8,128)S(1)} %get-tuple-element.23.keep_ref, f32[16,40,128]{2,1,0:T(8,128)S(1)} %collective-permute-done.2.came_ref), custom_call_target="tpu_custom_call" | custom-call | tf_op jit(solution)/shard_map/pair/pallas_call | solution.py:365
  52.3 5.1 %all-to-all-start.2 = ((f32[64,9,1,128]{3,2,1,0:T(1,128)}), f32[64,9,1,128]{3,2,1,0:T(1,128)S(1)}, u32[]{:S(2)}, u32[]{:S(2)}) async-start(f32[64,9,1,128]{3,2,1,0:T(1,128)} %pair.1), calls=%async_computation.2 | async-start | bytes 589824 | tf_op jit(solution)/shard_map/all_to_all | solution.py:373
  57.3 5.0 %factor.1 = (bf16[64,2048]{1,0:T(8,128)(2,1)}, f32[64,64]{1,0:T(8,128)S(1)}, bf16[4096,128]{1,0:T(8,128)(2,1)S(1)}) custom-call(f32[64,64]{1,0:T(8,128)S(1)} %correlation.1.corr_ref, f32[64,2048]{1,0:T(8,128)} %copy-done, f32[64,4096]{1,0:T(8,128)} %bitcast.7), custom_call_target="tpu_custom_call" | custom-call | tf_op jit(solution)/shard_map/factor/pallas_call | solution.py:374
  62.4 6.3 %all-to-all-done.2 = f32[64,9,1,128]{3,2,1,0:T(1,128)S(1)} async-done(((f32[64,9,1,128]{3,2,1,0:T(1,128)}), f32[64,9,1,128]{3,2,1,0:T(1,128)S(1)}, u32[]{:S(2)}, u32[]{:S(2)}) %all-to-all-start.2) | async-done | bytes 294944 | tf_op jit(solution)/shard_map/all_to_all | solution.py:373
  68.7 0.0 copy-done.1
  68.7 0.0 copy-done.2
  68.7 1.9 %rollout.1 = (f32[16,64]{1,0:T(8,128)}, f32[16,64]{1,0:T(8,128)}) custom-call(f32[576,128]{1,0:T(8,128)S(1)} %bitcast.5, f32[64,64]{1,0:T(8,128)S(1)} %get-tuple-element.25.refs_1_, f32[64,64]{1,0:T(8,128)S(1)} %copy-done.1, bf16[4096,128]{1,0:T(8,128)(2,1)S(1)} %get-tuple-element.26.refs_3_, f32[1,64]{1,0:T(1,128)S(1)} %bitcast.6), custom_call_target="tpu_custom_call" | custom-call | tf_op jit(solution)/shard_map/rollout/pallas_call | solution.py:392
  (1 shorter events, 0.0 us)
Async XLA Ops:
  6.1 1.6 %collective-permute-start = (f32[64,8,128]{2,1,0:T(8,128)S(1)}, f32[64,8,128]{2,1,0:T(8,128)S(1)}, u32[]{:S(2)}, u32[]{:S(2)}) collective-permute-start(f32[64,8,128]{2,1,0:T(8,128)S(1)} %get-tuple-element.18), channel_id=1, source_target_pairs={{0,4},{4,0},{1,5},{5,1},{2,6},{6,2},{3,7},{7,3},{8,12},{12,8},{9,1... | collective-permute-start | bytes 786440 | tf_op jit(solution)/shard_map/ppermute | solution.py:341
  45.3 1.5 %collective-permute-start.1 = (f32[64,8,128]{2,1,0:T(8,128)S(1)}, f32[64,8,128]{2,1,0:T(8,128)S(1)}, u32[]{:S(2)}, u32[]{:S(2)}) collective-permute-start(f32[64,8,128]{2,1,0:T(8,128)S(1)} %all_to_all.16.own_ref), channel_id=1, source_target_pairs={{0,4},{4,0},{1,5},{5,1},{2,6},{6,2},{3,7},{7,3},{8,12},{12,8},{9,1... | collective-permute-start | bytes 786440 | tf_op jit(solution)/shard_map/ppermute | solution.py:347
  46.6 22.0 %copy-start.1 = (f32[64,64]{1,0:T(8,128)S(1)}, f32[64,64]{1,0:T(8,128)}, u32[]{:S(2)}) copy-start(f32[64,64]{1,0:T(8,128)} %refs_2_.1) | copy-start | bytes 49156
  46.6 22.0 %copy-start.2 = (f32[64]{0:T(128)S(1)}, f32[64]{0:T(128)}, u32[]{:S(2)}) copy-start(f32[64]{0:T(128)} %param.9) | copy-start | bytes 772
  49.7 0.9 %copy-start = (f32[64,2048]{1,0:T(8,128)}, f32[64,2048]{1,0:T(8,128)S(1)}, u32[]{:S(2)}) copy-start(f32[64,2048]{1,0:T(8,128)S(1)} %get-tuple-element.21.modes_hbm) | copy-start | bytes 1572868
  49.7 1.7 %collective-permute-start.2 = (f32[16,40,128]{2,1,0:T(8,128)S(1)}, f32[16,40,128]{2,1,0:T(8,128)S(1)}, u32[]{:S(2)}, u32[]{:S(2)}) collective-permute-start(f32[16,40,128]{2,1,0:T(8,128)S(1)} %get-tuple-element.19), channel_id=1, source_target_pairs={{0,4},{4,0},{1,5},{5,1},{2,6},{6,2},{3,7},{7,3},{8,12},{12,8},{9,1... | collective-permute-start | bytes 983048 | tf_op jit(solution)/shard_map/ppermute | solution.py:361
  52.3 16.4 %all-to-all-start.2 = ((f32[64,9,1,128]{3,2,1,0:T(1,128)}), f32[64,9,1,128]{3,2,1,0:T(1,128)S(1)}, u32[]{:S(2)}, u32[]{:S(2)}) async-start(f32[64,9,1,128]{3,2,1,0:T(1,128)} %pair.1), calls=%async_computation.2 | async-start | bytes 589824 | tf_op jit(solution)/shard_map/all_to_all | solution.py:373

commit v11 on v10

--- a/solution.py
+++ b/solution.py
@@ -50,10 +50,10 @@
         value = inner(i)
         if held is not None:
             part = jnp.dot(held, block(i - 1), preferred_element_type=jnp.float32)
-            acc_ref[...] = part if i == 1 else acc_ref[...] + part
+            total = part if i == 1 else total + part
         held = pieces_of(value, PIECES)
     part = jnp.dot(held, block(count - 1), preferred_element_type=jnp.float32)
-    return fold_rows(acc_ref[...] + part, PIECES)
+    return fold_rows(total + part, PIECES)
 
 
 def put_tiles(out_ref, value):

time: 71 us -> 71.1 us (level)
  no operation moved by 1% of the time
where the time goes in v11:
time: 71.1 us; the launch traced here: 70.9 us
  blocking collectives  37.5 us (53%)
  Pallas kernels  18.9 us (27%)
  waiting for transfers between devices  8.07 us (11%)
  starting transfers between devices  5.56 us (8%)
  between operations  0.9 us (1%)
    all_to_all x1, blocking collectives, body(): parts = lax.all_to_all(parts, CHIPS, 0, 0, tiled=True)  22.2 us
    all_to_all x1, blocking collectives, body(): mine = lax.all_to_all(spread, CHIPS, 0, 0, tiled=True)  15.3 us
    all_to_all x1, waiting for transfers between devices, body(): parts = lax.all_to_all(parts, CHIPS, 0, 0, tiled=True).reshape(-1, 2 * RANK)  6.26 us
    pallas_call x1, Pallas kernels, body(): call(power_kernel, 'power', (tiles, shape((rows, width), jnp.bfloat16), s...  5.64 us
    all_to_all x1, starting transfers between devices, body(): parts = lax.all_to_all(parts, CHIPS, 0, 0, tiled=True).reshape(-1, 2 * RANK)  5.06 us
    pallas_call x1, Pallas kernels, body(): call(factor_kernel, 'factor', (shape((RANK, rows), jnp.bfloat16), small,...  5.03 us
    pallas_call x1, Pallas kernels, body(): call(coords_kernel, 'coords', (packed, packed, shape((RANK, rows), f32)),...  2.85 us
    pallas_call x1, Pallas kernels, body(): call(lambda *refs: rollout_kernel(factor_scale, width, *refs), 'rollout',...  1.88 us
  transfers between devices with their start and end apart: 4, of which 4 were waited for; matrix products, arithmetic and copies ran while one was open for 0% of the time, Pallas kernels for 11%

profile of v11, /device:TPU:0, one launch (start us, length us, event | category | flops | bytes accessed | tf_op | source)
XLA Modules:
  0.0 70.9 jit_solution(10897082511730099511)
XLA Ops:
  0.6 5.6 %power.1 = (f32[64,8,128]{2,1,0:T(8,128)S(1)}, bf16[2048,2048]{1,0:T(8,128)(2,1)S(1)}, bf16[128,2048]{1,0:T(8,128)(2,1)S(1)}) custom-call(bf16[2048,2048]{1,0:T(8,128)(2,1)} %x_hbm.1, f32[64,2048]{1,0:T(8,128)} %bitcast.8), custom_call_target="tpu_custom_call" | custom-call | tf_op jit(solution)/shard_map/power/pallas_call | solution.py:325
  6.3 0.1 collective-permute-start
  6.4 0.7 %own_power.1.keep_ref = f32[64,8,128]{2,1,0:T(8,128)S(1)} custom-call(bf16[128,2048]{1,0:T(8,128)(2,1)S(1)} %get-tuple-element.17.inner_ref, bf16[2048,2048]{1,0:T(8,128)(2,1)S(1)} %get-tuple-element.16.x_ref), custom_call_target="tpu_custom_call" | custom-call | tf_op jit(solution)/shard_map/own_power/pallas_call | solution.py:342
  7.1 0.8 %collective-permute-done.came_ref = f32[64,8,128]{2,1,0:T(8,128)S(1)} collective-permute-done((f32[64,8,128]{2,1,0:T(8,128)S(1)}, f32[64,8,128]{2,1,0:T(8,128)S(1)}, u32[]{:S(2)}, u32[]{:S(2)}) %collective-permute-start) | collective-permute-done | bytes 262176 | tf_op jit(solution)/shard_map/ppermute | solution.py:341
  7.9 22.2 %all_to_all.15.parts_ref = f32[64,8,128]{2,1,0:T(8,128)S(1)} all-to-all(f32[64,8,128]{2,1,0:T(8,128)S(1)} %add.1), channel_id=1, replica_groups=mesh['yz'=16,'core'=2,'slab'=4] {'yz','slab'}, dimensions={0} | all-to-all | bytes 524288 | tf_op jit(solution)/shard_map/all_to_all | solution.py:344
  30.1 0.1 spread.1
  30.2 15.3 %all_to_all.16.own_ref = f32[64,8,128]{2,1,0:T(8,128)S(1)} all-to-all(f32[64,8,128]{2,1,0:T(8,128)S(1)} %spread.1), channel_id=1, replica_groups=mesh['yz'=16,'core'=2,'slab'=4] {'yz','slab'}, dimensions={0} | all-to-all | bytes 524288 | tf_op jit(solution)/shard_map/all_to_all | solution.py:346
  45.5 0.0 collective-permute-start.1
  45.5 1.3 %own_modes.1.own_modes_ref = f32[64,2048]{1,0:T(8,128)S(1)} custom-call(bf16[2048,2048]{1,0:T(8,128)(2,1)S(1)} %get-tuple-element.16.x_ref, f32[64,8,128]{2,1,0:T(8,128)S(1)} %all_to_all.16.own_ref), custom_call_target="tpu_custom_call" | custom-call | tf_op jit(solution)/shard_map/own_modes/pallas_call | solution.py:348
  46.8 0.0 copy-start.1
  46.8 0.0 copy-start.2
  46.8 0.2 collective-permute-done.1.other_ref
  47.0 2.9 %coords.1 = (f32[16,40,128]{2,1,0:T(8,128)S(1)}, f32[16,40,128]{2,1,0:T(8,128)S(1)}, f32[64,2048]{1,0:T(8,128)S(1)}) custom-call(bf16[2048,2048]{1,0:T(8,128)(2,1)S(1)} %get-tuple-element.16.x_ref, f32[64,2048]{1,0:T(8,128)S(1)} %own_modes.1.own_modes_ref, f32[64,8,128]{2,1,0:T(8,128)S(1)} %collective-permute-done.1.other_ref), custom_call_target="tpu_custom_call" | custom-call | tf_op jit(solution)/shard_map/coords/pallas_call | solution.py:354
  49.9 0.0 copy-start
  49.9 0.4 collective-permute-start.2
  50.3 0.5 correlation.1.corr_ref
  50.8 0.0 copy-done
  50.8 0.8 %collective-permute-done.2.came_ref = f32[16,40,128]{2,1,0:T(8,128)S(1)} collective-permute-done((f32[16,40,128]{2,1,0:T(8,128)S(1)}, f32[16,40,128]{2,1,0:T(8,128)S(1)}, u32[]{:S(2)}, u32[]{:S(2)}) %collective-permute-start.2) | collective-permute-done | bytes 327712 | tf_op jit(solution)/shard_map/ppermute | solution.py:361
  51.6 0.8 %pair.1 = f32[64,9,1,128]{3,2,1,0:T(1,128)} custom-call(f32[16,40,128]{2,1,0:T(8,128)S(1)} %get-tuple-element.23.keep_ref, f32[16,40,128]{2,1,0:T(8,128)S(1)} %collective-permute-done.2.came_ref), custom_call_target="tpu_custom_call" | custom-call | tf_op jit(solution)/shard_map/pair/pallas_call | solution.py:365
  52.5 5.1 %all-to-all-start.2 = ((f32[64,9,1,128]{3,2,1,0:T(1,128)}), f32[64,9,1,128]{3,2,1,0:T(1,128)S(1)}, u32[]{:S(2)}, u32[]{:S(2)}) async-start(f32[64,9,1,128]{3,2,1,0:T(1,128)} %pair.1), calls=%async_computation.2 | async-start | bytes 589824 | tf_op jit(solution)/shard_map/all_to_all | solution.py:373
  57.5 5.0 %factor.1 = (bf16[64,2048]{1,0:T(8,128)(2,1)}, f32[64,64]{1,0:T(8,128)S(1)}, bf16[4096,128]{1,0:T(8,128)(2,1)S(1)}) custom-call(f32[64,64]{1,0:T(8,128)S(1)} %correlation.1.corr_ref, f32[64,2048]{1,0:T(8,128)} %copy-done, f32[64,4096]{1,0:T(8,128)} %bitcast.7), custom_call_target="tpu_custom_call" | custom-call | tf_op jit(solution)/shard_map/factor/pallas_call | solution.py:374
  62.6 6.3 %all-to-all-done.2 = f32[64,9,1,128]{3,2,1,0:T(1,128)S(1)} async-done(((f32[64,9,1,128]{3,2,1,0:T(1,128)}), f32[64,9,1,128]{3,2,1,0:T(1,128)S(1)}, u32[]{:S(2)}, u32[]{:S(2)}) %all-to-all-start.2) | async-done | bytes 294944 | tf_op jit(solution)/shard_map/all_to_all | solution.py:373
  68.8 0.0 copy-done.1
  68.8 0.0 copy-done.2
  68.8 1.9 %rollout.1 = (f32[16,64]{1,0:T(8,128)}, f32[16,64]{1,0:T(8,128)}) custom-call(f32[576,128]{1,0:T(8,128)S(1)} %bitcast.5, f32[64,64]{1,0:T(8,128)S(1)} %get-tuple-element.25.refs_1_, f32[64,64]{1,0:T(8,128)S(1)} %copy-done.1, bf16[4096,128]{1,0:T(8,128)(2,1)S(1)} %get-tuple-element.26.refs_3_, f32[1,64]{1,0:T(1,128)S(1)} %bitcast.6), custom_call_target="tpu_custom_call" | custom-call | tf_op jit(solution)/shard_map/rollout/pallas_call | solution.py:392
  (1 shorter events, 0.0 us)
Async XLA Ops:
  6.3 1.6 %collective-permute-start = (f32[64,8,128]{2,1,0:T(8,128)S(1)}, f32[64,8,128]{2,1,0:T(8,128)S(1)}, u32[]{:S(2)}, u32[]{:S(2)}) collective-permute-start(f32[64,8,128]{2,1,0:T(8,128)S(1)} %get-tuple-element.18), channel_id=1, source_target_pairs={{0,4},{4,0},{1,5},{5,1},{2,6},{6,2},{3,7},{7,3},{8,12},{12,8},{9,1... | collective-permute-start | bytes 786440 | tf_op jit(solution)/shard_map/ppermute | solution.py:341
  45.5 1.5 %collective-permute-start.1 = (f32[64,8,128]{2,1,0:T(8,128)S(1)}, f32[64,8,128]{2,1,0:T(8,128)S(1)}, u32[]{:S(2)}, u32[]{:S(2)}) collective-permute-start(f32[64,8,128]{2,1,0:T(8,128)S(1)} %all_to_all.16.own_ref), channel_id=1, source_target_pairs={{0,4},{4,0},{1,5},{5,1},{2,6},{6,2},{3,7},{7,3},{8,12},{12,8},{9,1... | collective-permute-start | bytes 786440 | tf_op jit(solution)/shard_map/ppermute | solution.py:347
  46.8 22.0 %copy-start.1 = (f32[64,64]{1,0:T(8,128)S(1)}, f32[64,64]{1,0:T(8,128)}, u32[]{:S(2)}) copy-start(f32[64,64]{1,0:T(8,128)} %refs_2_.1) | copy-start | bytes 49156
  46.8 22.0 %copy-start.2 = (f32[64]{0:T(128)S(1)}, f32[64]{0:T(128)}, u32[]{:S(2)}) copy-start(f32[64]{0:T(128)} %param.9) | copy-start | bytes 772
  49.9 0.9 %copy-start = (f32[64,2048]{1,0:T(8,128)}, f32[64,2048]{1,0:T(8,128)S(1)}, u32[]{:S(2)}) copy-start(f32[64,2048]{1,0:T(8,128)S(1)} %get-tuple-element.21.modes_hbm) | copy-start | bytes 1572868
  49.9 1.7 %collective-permute-start.2 = (f32[16,40,128]{2,1,0:T(8,128)S(1)}, f32[16,40,128]{2,1,0:T(8,128)S(1)}, u32[]{:S(2)}, u32[]{:S(2)}) collective-permute-start(f32[16,40,128]{2,1,0:T(8,128)S(1)} %get-tuple-element.19), channel_id=1, source_target_pairs={{0,4},{4,0},{1,5},{5,1},{2,6},{6,2},{3,7},{7,3},{8,12},{12,8},{9,1... | collective-permute-start | bytes 983048 | tf_op jit(solution)/shard_map/ppermute | solution.py:361
  52.5 16.4 %all-to-all-start.2 = ((f32[64,9,1,128]{3,2,1,0:T(1,128)}), f32[64,9,1,128]{3,2,1,0:T(1,128)S(1)}, u32[]{:S(2)}, u32[]{:S(2)}) async-start(f32[64,9,1,128]{3,2,1,0:T(1,128)} %pair.1), calls=%async_computation.2 | async-start | bytes 589824 | tf_op jit(solution)/shard_map/all_to_all | solution.py:373
